TPU v7x, 32 devices: a whole 2x2x4 slice. The times are simulated.
32 devices in a mesh: frame: 8 (over y, x, core), tensor: 4 (over z).
Axes of the slice: x: 2, y: 2, z: 4, core: 2. Of those that a mesh axis runs over, the one named last changes fastest.
Arguments:
- tokens: bfloat16 [4, 16, 256, 1024], P(None, 'frame', 'tensor'), may hold values from -6 to 6
- noise_steps: int32 [4, 16], P(None, 'frame'), may hold values from 0 to 999
- ada_weight: bfloat16 [1024, 6, 1024], P(None, None, 'tensor'), may hold values from -0.1875 to 0.1875
- ada_bias: bfloat16 [6, 1024], P(None, 'tensor'), may hold values from -3 to 3
- qkv_weight: bfloat16 [1024, 3, 1024], P(None, None, 'tensor'), may hold values from -0.1875 to 0.1875
- qv_bias: bfloat16 [2, 1024], P(None, 'tensor'), may hold values from -3 to 3
- out_weight: bfloat16 [1024, 1024], P('tensor'), may hold values from -2 to 2
- out_bias: bfloat16 [1024], replicated, may hold values from -3 to 3
- up_weight: bfloat16 [1024, 4096], P(None, 'tensor'), may hold values from -0.1875 to 0.1875
- up_bias: bfloat16 [4096], P('tensor'), may hold values from -3 to 3
- down_weight: bfloat16 [4096, 1024], P('tensor'), may hold values from -0.09375 to 0.09375
- down_bias: bfloat16 [1024], replicated, may hold values from -3 to 3
- cotangent: bfloat16 [4, 16, 256, 1024], P(None, 'frame', 'tensor'), may hold values from -6 to 6
Outputs:
- out: bfloat16 [4, 16, 256, 1024], P(None, 'frame', 'tensor')
- grad_tokens: float32 [4, 16, 256, 1024], P(None, 'frame', 'tensor')
- grad_ada_weight: float32 [1024, 6, 1024], P(None, None, 'tensor')
- grad_ada_bias: float32 [6, 1024], P(None, 'tensor')
- grad_qkv_weight: float32 [1024, 3, 1024], P(None, None, 'tensor')
- grad_qv_bias: float32 [2, 1024], P(None, 'tensor')
- grad_out_weight: float32 [1024, 1024], P('tensor')
- grad_out_bias: float32 [1024], replicated
- grad_up_weight: float32 [1024, 4096], P(None, 'tensor')
- grad_up_bias: float32 [4096], P('tensor')
- grad_down_weight: float32 [4096, 1024], P('tensor')
- grad_down_bias: float32 [1024], replicated
Inputs may be any that keep to these rules, and one draw needn't show every extreme that they name: `noise_steps`: timestep of each frame of each clip; a few timesteps are very common.
All inputs are finite; a program needn't handle non-finite values.
Results may differ from a plain program's by a relative error of at most 0.014.
The roundings to bfloat16 on the way count: a program that leaves them out, or rounds other values in their place, can miss the bound.
Values may be sent and summed in bfloat16 or wider, within the bound.
No kernel may reach another device: no remote copies, remote signals or barrier semaphores. Data moves between devices by JAX's collectives and lax.ppermute only.
A program may use at most 192 MiB of HBM per device.

v0:
```python
from functools import partial
import math

import jax
import jax.numpy as jnp
from jax import lax
from jax.sharding import PartitionSpec as P

HD = 64


highest = lax.Precision.HIGHEST
masked_value = -1e30


def noise_embedding(noise_steps, model_width):
    half_width = model_width // 2
    frequency = jnp.exp(-math.log(10000.0) * jnp.arange(half_width, dtype=jnp.float32) / half_width)
    angles = noise_steps.astype(jnp.float32)[..., None] * frequency
    return jnp.concatenate([jnp.cos(angles), jnp.sin(angles)], axis=-1)


def layer_norm(values):
    centred = values - jnp.mean(values, axis=-1, keepdims=True)
    inverse = lax.rsqrt(jnp.mean(centred * centred, axis=-1, keepdims=True) + 1e-06)
    return (centred * inverse, inverse)


def norm_back(grad_normed, normed, inverse):
    return inverse * (
        grad_normed
        - jnp.mean(grad_normed, axis=-1, keepdims=True)
        - normed * jnp.mean(grad_normed * normed, axis=-1, keepdims=True)
    )


def frame_slice(values_in, index, head_count, head_size):
    piece = lax.dynamic_index_in_dim(values_in, index, 1, keepdims=False)
    return piece.reshape(piece.shape[0], piece.shape[1], head_count, head_size)


def masked_scores(query_block, key_block, query_frames, key_frames, score_scale):
    scores = (
        jnp.einsum("cqhe,ckhe->chqk", query_block, key_block, preferred_element_type=jnp.float32)
        * score_scale
    )
    allowed = key_frames[None, :] <= query_frames[:, None]
    return jnp.where(allowed, scores, masked_value)


def on_device(
    tokens,
    noise_steps,
    ada_weight,
    ada_bias,
    qkv_weight,
    qv_bias,
    out_weight,
    out_bias,
    up_weight,
    up_bias,
    down_weight,
    down_bias,
    cotangent,
):
    clip_count, local_frames, local_patches, model_width = tokens.shape
    tensor_count = lax.axis_size("tensor")
    patch_count = local_patches * tensor_count
    local_width = qkv_weight.shape[2]
    head_size = HD
    head_count = local_width // head_size
    frame_count = local_frames * lax.axis_size("frame")
    first_frame = lax.axis_index("frame") * local_frames
    key_stop = first_frame + local_frames
    score_scale = head_size ** (-0.5)
    row_count = local_frames * patch_count
    local_ids = first_frame + jnp.arange(row_count, dtype=jnp.int32) // patch_count

    def frame_ids_of(index):
        return jnp.zeros((patch_count,), jnp.int32) + index

    act_noise = jax.nn.silu(noise_embedding(noise_steps, model_width)).astype(jnp.bfloat16)
    mod_local = jnp.einsum(
        "cfd,dkj->cfkj", act_noise, ada_weight, preferred_element_type=jnp.float32
    ) + ada_bias.astype(jnp.float32)
    modulation = lax.all_gather(mod_local, "tensor", axis=3, tiled=True)
    shift_one = modulation[:, :, None, 0]
    scale_one = modulation[:, :, None, 1]
    gate_one = modulation[:, :, None, 2]
    shift_two = modulation[:, :, None, 3]
    scale_two = modulation[:, :, None, 4]
    gate_two = modulation[:, :, None, 5]
    token_values = tokens.astype(jnp.float32)
    normed_one, inverse_one = layer_norm(token_values)
    hidden_one = (normed_one * (1.0 + scale_one) + shift_one).astype(jnp.bfloat16)
    hidden_all = lax.all_gather(hidden_one, "tensor", axis=2, tiled=True)
    projected = jnp.einsum(
        "cfpd,dkj->cfpkj", hidden_all, qkv_weight, preferred_element_type=jnp.float32
    )
    bias_pair = qv_bias.astype(jnp.float32)
    queries = (projected[:, :, :, 0] + bias_pair[0]).astype(jnp.bfloat16)
    keys = projected[:, :, :, 1].astype(jnp.bfloat16)
    values = (projected[:, :, :, 2] + bias_pair[1]).astype(jnp.bfloat16)
    keys_all, values_all = (
        lax.all_gather(keys, "frame", axis=1, tiled=True),
        lax.all_gather(values, "frame", axis=1, tiled=True),
    )
    query_rows = queries.reshape(clip_count, row_count, head_count, head_size)
    stat_shape = (clip_count, head_count, row_count)

    def frame_scores(index):
        key_block = frame_slice(keys_all, index, head_count, head_size)
        return (
            key_block,
            masked_scores(query_rows, key_block, local_ids, frame_ids_of(index), score_scale),
        )

    def stats_step(index, carry):
        row_max, row_total = carry
        scores = frame_scores(index)[1]
        new_max = jnp.maximum(row_max, jnp.max(scores, axis=-1))
        row_total = row_total * jnp.exp(row_max - new_max) + jnp.sum(
            jnp.exp(scores - new_max[..., None]), axis=-1
        )
        return (new_max, row_total)

    row_max, row_total = lax.fori_loop(
        0,
        key_stop,
        stats_step,
        (jnp.full(stat_shape, masked_value, jnp.float32), jnp.zeros(stat_shape, jnp.float32)),
    )
    row_lse = row_max + jnp.log(row_total)

    def out_step(index, total):
        scores = frame_scores(index)[1]
        attn_probs = jnp.exp(scores - row_lse[..., None]).astype(jnp.bfloat16)
        value_block = frame_slice(values_all, index, head_count, head_size)
        return total + jnp.einsum(
            "chqk,ckhe->cqhe", attn_probs, value_block, preferred_element_type=jnp.float32
        )

    out_rows = lax.fori_loop(
        0,
        key_stop,
        out_step,
        jnp.zeros((clip_count, row_count, head_count, head_size), jnp.float32),
    )
    local_shape = (clip_count, local_frames, patch_count, local_width)
    attended = out_rows.astype(jnp.bfloat16).reshape(local_shape)
    attn_term = jnp.einsum(
        "cfpj,jd->cfpd", attended, out_weight, preferred_element_type=jnp.float32
    )
    branch_one = lax.psum_scatter(
        attn_term, "tensor", scatter_dimension=2, tiled=True
    ) + out_bias.astype(jnp.float32)
    middle = token_values + gate_one * branch_one
    normed_two, inverse_two = layer_norm(middle)
    hidden_two = (normed_two * (1.0 + scale_two) + shift_two).astype(jnp.bfloat16)
    hidden_two_all = lax.all_gather(hidden_two, "tensor", axis=2, tiled=True)
    pre_gelu = jnp.einsum(
        "cfpd,dh->cfph", hidden_two_all, up_weight, preferred_element_type=jnp.float32
    ) + up_bias.astype(jnp.float32)
    activated = jax.nn.gelu(pre_gelu, approximate=True).astype(jnp.bfloat16)
    mlp_term = jnp.einsum(
        "cfph,hd->cfpd", activated, down_weight, preferred_element_type=jnp.float32
    )
    branch_two = lax.psum_scatter(
        mlp_term.astype(jnp.bfloat16), "tensor", scatter_dimension=2, tiled=True
    ).astype(jnp.float32) + down_bias.astype(jnp.float32)
    result = (middle + gate_two * branch_two).astype(jnp.bfloat16)
    upstream = cotangent.astype(jnp.float32)
    grad_branch_two = (gate_two * upstream).astype(jnp.bfloat16)
    grad_gate_two = jnp.sum(upstream * branch_two, axis=2)
    grad_two_all = lax.all_gather(grad_branch_two, "tensor", axis=2, tiled=True)
    grad_down_bias = jnp.sum(grad_two_all, axis=(0, 1, 2), dtype=jnp.float32)
    grad_down_weight = jnp.einsum(
        "cfph,cfpd->hd", activated, grad_two_all, preferred_element_type=jnp.float32
    )
    grad_activated = jnp.einsum(
        "cfpd,hd->cfph", grad_two_all, down_weight, preferred_element_type=jnp.float32
    )
    gelu_value, gelu_back = jax.vjp(partial(jax.nn.gelu, approximate=True), pre_gelu)
    grad_pre = gelu_back(grad_activated)[0].astype(jnp.bfloat16)
    grad_up_bias = jnp.sum(grad_pre, axis=(0, 1, 2), dtype=jnp.float32)
    grad_up_weight = jnp.einsum(
        "cfpd,cfph->dh", hidden_two_all, grad_pre, preferred_element_type=jnp.float32
    )
    grad_hidden_two = lax.psum_scatter(
        jnp.einsum("cfph,dh->cfpd", grad_pre, up_weight, preferred_element_type=jnp.float32),
        "tensor",
        scatter_dimension=2,
        tiled=True,
    )
    grad_scale_two = jnp.sum(grad_hidden_two * normed_two, axis=2)
    grad_shift_two = jnp.sum(grad_hidden_two, axis=2)
    grad_middle = upstream + norm_back(grad_hidden_two * (1.0 + scale_two), normed_two, inverse_two)
    grad_branch_one = (gate_one * grad_middle).astype(jnp.bfloat16)
    grad_gate_one = jnp.sum(grad_middle * branch_one, axis=2)
    grad_one_all = lax.all_gather(grad_branch_one, "tensor", axis=2, tiled=True)
    grad_out_bias = jnp.sum(grad_one_all, axis=(0, 1, 2), dtype=jnp.float32)
    grad_out_weight = jnp.einsum(
        "cfpj,cfpd->jd", attended, grad_one_all, preferred_element_type=jnp.float32
    )
    grad_attended = jnp.einsum(
        "cfpd,jd->cfpj", grad_one_all, out_weight, preferred_element_type=jnp.float32
    ).astype(jnp.bfloat16)
    grad_rows = grad_attended.reshape(clip_count, row_count, head_count, head_size)

    def probs_and_grads(index):
        key_block, scores = frame_scores(index)
        attn_probs = jnp.exp(scores - row_lse[..., None])
        value_block = frame_slice(values_all, index, head_count, head_size)
        grad_probs = jnp.einsum(
            "cqhe,ckhe->chqk", grad_rows, value_block, preferred_element_type=jnp.float32
        )
        return (key_block, attn_probs, grad_probs)

    def delta_step(index, total):
        attn_probs, grad_probs = probs_and_grads(index)[1:]
        return total + jnp.sum(grad_probs * attn_probs, axis=-1)

    row_delta = lax.fori_loop(0, key_stop, delta_step, jnp.zeros(stat_shape, jnp.float32))
    row_shape = (clip_count, row_count, head_count, head_size)
    full_shape = (clip_count, frame_count, patch_count, local_width)

    def grad_step(index, carry):
        grad_q_total, grad_k_total, grad_v_total = carry
        key_block, attn_probs, grad_probs = probs_and_grads(index)
        grad_scores = (attn_probs * (grad_probs - row_delta[..., None])).astype(jnp.bfloat16)
        grad_q_total = grad_q_total + jnp.einsum(
            "chqk,ckhe->cqhe", grad_scores, key_block, preferred_element_type=jnp.float32
        )
        grad_k_frame = (
            jnp.einsum(
                "chqk,cqhe->ckhe", grad_scores, query_rows, preferred_element_type=jnp.float32
            )
            * score_scale
        )
        grad_v_frame = jnp.einsum(
            "chqk,cqhe->ckhe",
            attn_probs.astype(jnp.bfloat16),
            grad_rows,
            preferred_element_type=jnp.float32,
        )
        grad_k_total = lax.dynamic_update_index_in_dim(
            grad_k_total, grad_k_frame.reshape(clip_count, patch_count, local_width), index, 1
        )
        grad_v_total = lax.dynamic_update_index_in_dim(
            grad_v_total, grad_v_frame.reshape(clip_count, patch_count, local_width), index, 1
        )
        return (grad_q_total, grad_k_total, grad_v_total)

    grad_q_rows, grad_k_full, grad_v_full = lax.fori_loop(
        0,
        key_stop,
        grad_step,
        (
            jnp.zeros(row_shape, jnp.float32),
            jnp.zeros(full_shape, jnp.float32),
            jnp.zeros(full_shape, jnp.float32),
        ),
    )
    grad_keys_sum, grad_values_sum = (
        lax.psum_scatter(grad_k_full, "frame", scatter_dimension=1, tiled=True),
        lax.psum_scatter(grad_v_full, "frame", scatter_dimension=1, tiled=True),
    )
    grad_queries = (grad_q_rows * score_scale).reshape(local_shape).astype(jnp.bfloat16)
    grad_keys = grad_keys_sum.astype(jnp.bfloat16)
    grad_values = grad_values_sum.astype(jnp.bfloat16)
    grad_qv_bias = jnp.stack(
        [
            jnp.sum(grad_queries, axis=(0, 1, 2), dtype=jnp.float32),
            jnp.sum(grad_values, axis=(0, 1, 2), dtype=jnp.float32),
        ]
    )
    grad_projected = jnp.stack([grad_queries, grad_keys, grad_values], axis=3)
    grad_qkv_weight = jnp.einsum(
        "cfpd,cfpkj->dkj", hidden_all, grad_projected, preferred_element_type=jnp.float32
    )
    grad_hidden_one = lax.psum_scatter(
        jnp.einsum(
            "cfpkj,dkj->cfpd", grad_projected, qkv_weight, preferred_element_type=jnp.float32
        ),
        "tensor",
        scatter_dimension=2,
        tiled=True,
    )
    grad_scale_one = jnp.sum(grad_hidden_one * normed_one, axis=2)
    grad_shift_one = jnp.sum(grad_hidden_one, axis=2)
    grad_tokens = grad_middle + norm_back(
        grad_hidden_one * (1.0 + scale_one), normed_one, inverse_one
    )
    grad_modulation = jnp.stack(
        [
            grad_shift_one,
            grad_scale_one,
            grad_gate_one,
            grad_shift_two,
            grad_scale_two,
            grad_gate_two,
        ],
        axis=2,
    )
    grad_mod_local = lax.psum_scatter(grad_modulation, "tensor", scatter_dimension=3, tiled=True)
    grad_ada_weight = jnp.einsum(
        "cfd,cfkj->dkj", act_noise.astype(jnp.float32), grad_mod_local, precision=highest
    )
    grad_ada_bias = jnp.sum(grad_mod_local, axis=(0, 1))
    summed = lax.psum(
        (
            grad_ada_weight,
            grad_ada_bias,
            grad_qkv_weight,
            grad_qv_bias,
            grad_out_weight,
            grad_out_bias,
            grad_up_weight,
            grad_up_bias,
            grad_down_weight,
            grad_down_bias,
        ),
        "frame",
    )
    return (
        result,
        grad_tokens,
        summed[0],
        summed[1],
        summed[2],
        summed[3],
        summed[4],
        summed[5],
        summed[6],
        summed[7],
        summed[8],
        summed[9],
    )


def solution(mesh):
    in_specs = (
        P(None, "frame", "tensor", None),
        P(None, "frame"),
        P(None, None, "tensor"),
        P(None, "tensor"),
        P(None, None, "tensor"),
        P(None, "tensor"),
        P("tensor", None),
        P(),
        P(None, "tensor"),
        P("tensor"),
        P("tensor", None),
        P(),
        P(None, "frame", "tensor", None),
    )
    out_specs = (
        P(None, "frame", "tensor", None),
        P(None, "frame", "tensor", None),
        P(None, None, "tensor"),
        P(None, "tensor"),
        P(None, None, "tensor"),
        P(None, "tensor"),
        P("tensor", None),
        P(),
        P(None, "tensor"),
        P("tensor"),
        P("tensor", None),
        P(),
    )
    return jax.shard_map(
        on_device, mesh=mesh, in_specs=in_specs, out_specs=out_specs, check_vma=False
    )
```

profile of v0, /device:TPU:0, one launch (start us, length us, event | category | flops | bytes accessed | tf_op | source)
XLA Modules:
  0.0 2704.1 jit_solution(12222632920348842979)
XLA Ops:
  13.1 15.5 all_gather.21
  30.3 82.1 %all-gather.8.cloned.1.call-done = bf16[4,2,256,1024]{3,2,1,0:T(8,128)(2,1)} async-done(((bf16[4,2,64,1024]{3,2,1,0:T(8,128)(2,1)}), bf16[4,2,256,1024]{3,2,1,0:T(8,128)(2,1)}) %all-gather.8.cloned.1.call-update) | async-done | bytes 4194320 | tf_op jit(solution)/shard_map/all_gather | solution.py:96
  130.8 44.1 %all-gather.18.cloned.1.call-done = bf16[4,16,256,1,256]{4,2,3,1,0:T(8,128)(2,1)} async-done(((bf16[4,2,256,1,256]{4,2,3,1,0:T(8,128)(2,1)}), bf16[4,16,256,1,256]{4,2,3,1,0:T(8,128)(2,1)}) %all-gather.18.cloned.1.call-update) | async-done | bytes 8388624 | tf_op jit(solution)/shard_map/all_gather | solution.py:105
  175.0 12.3 copy.77
  187.2 8.5 while.50
  195.8 36.1 %all-gather.10.cloned.1.call-done = bf16[4,16,256,256]{3,2,1,0:T(8,128)(2,1)} async-done(((bf16[4,2,256,256]{3,2,1,0:T(8,128)(2,1)}), bf16[4,16,256,256]{3,2,1,0:T(8,128)(2,1)}) %all-gather.10.cloned.1.call-update) | async-done | bytes 8388624 | tf_op jit(solution)/shard_map/all_gather | solution.py:106
  231.9 12.3 copy.76
  245.7 13.9 while.51
  268.3 264.5 %reduce-scatter.14.cloned.1.call-done = f32[4,2,64,1024]{3,2,1,0:T(8,128)} async-done(((f32[4,2,256,1024]{3,2,1,0:T(8,128)}), f32[4,2,64,1024]{3,2,1,0:T(8,128)}) %reduce-scatter.14.cloned.1.call-update) | async-done | bytes 2097168 | tf_op jit(solution)/shard_map/reduce_scatter | solution.py:154
  539.8 78.8 %all-gather.12.cloned.1.call-done = bf16[4,2,256,1024]{3,2,1,0:T(8,128)(2,1)} async-done(((bf16[4,2,64,1024]{3,2,1,0:T(8,128)(2,1)}), bf16[4,2,256,1024]{3,2,1,0:T(8,128)(2,1)}) %all-gather.12.cloned.1.call-update) | async-done | bytes 4194320 | tf_op jit(solution)/shard_map/all_gather | solution.py:160
  618.6 10.9 fusion.78
  629.5 70.4 %all-gather.14.cloned.1.call-done = bf16[4,2,256,1024]{3,2,1,0:T(8,128)(2,1)} async-done(((bf16[4,2,64,1024]{3,2,1,0:T(8,128)(2,1)}), bf16[4,2,256,1024]{3,2,1,0:T(8,128)(2,1)}) %all-gather.14.cloned.1.call-update) | async-done | bytes 4194320 | tf_op jit(solution)/shard_map/all_gather | solution.py:175
  699.9 13.8 convert_reduce_fusion.1
  715.7 6.9 fusion.76
  723.1 11.8 convolution_convert_fusion
  735.6 130.2 %reduce-scatter.18.cloned.1.call-done = f32[4,2,64,1024]{3,2,1,0:T(8,128)} async-done(((f32[4,2,256,1024]{3,2,1,0:T(8,128)}), f32[4,2,64,1024]{3,2,1,0:T(8,128)}) %reduce-scatter.18.cloned.1.call-update) | async-done | bytes 2097168 | tf_op jit(solution)/shard_map/reduce_scatter | solution.py:189
  869.0 77.1 %reduce-scatter.16.cloned.1.call-done = bf16[4,2,64,1024]{3,2,1,0:T(8,128)(2,1)} async-done(((bf16[4,2,256,1024]{3,2,1,0:T(8,128)(2,1)}), bf16[4,2,64,1024]{3,2,1,0:T(8,128)(2,1)}) %reduce-scatter.16.cloned.1.call-update) | async-done | bytes 1048592 | tf_op jit(solution)/shard_map/reduce_scatter | solution.py:168
  955.1 80.1 %all-gather.16.cloned.1.call-done = bf16[4,2,256,1024]{3,2,1,0:T(8,128)(2,1)} async-done(((bf16[4,2,64,1024]{3,2,1,0:T(8,128)(2,1)}), bf16[4,2,256,1024]{3,2,1,0:T(8,128)(2,1)}) %all-gather.16.cloned.1.call-update) | async-done | bytes 4194320 | tf_op jit(solution)/shard_map/all_gather | solution.py:200
  1041.3 13.5 while.52
  1056.3 7.8 broadcast.202.clone2
  1064.1 7.8 broadcast.202.clone
  1071.9 53.0 %while.53 = (s32[]{:T(128)}, f32[4,512,4,64]{1,3,2,0:T(8,128)}, f32[4,16,256,256]{3,2,1,0:T(8,128)}, f32[4,16,256,256]{3,2,1,0:T(8,128)}, s32[]{:T(128)}, /*inde...) while((s32[]{:T(128)}, f32[4,512,4,64]{1,3,2,0:T(8,128)}, ...), condition=%wide.region_19.20_spmd.clone, body=%wide.region_18.19_spmd.clone.sunk | while | flops 1363940352 | bytes 93947680 | solution.py:254
  1129.0 1115.0 %all-reduce.9 = (bf16[4,16,256,256]{3,2,1,0:T(8,128)(2,1)}, bf16[4,16,256,256]{3,2,1,0:T(8,128)(2,1)}) all-reduce(f32[4,16,256,256]{3,2,1,0:T(8,128)} %get-tuple-element.213, f32[4,16,256,256]{3,2,1,0:T(8,128)} %get-tuple-element.212), channel_id=7, replica_groups=mesh['frame'=8,'tensor'=4] {'frame'}, use_global_device_ids=true, to_apply=%region_21.22.clone | all-reduce | flops 8388608 | bytes 50331648
  2253.0 11.0 convolution_bitcast_fusion.3
  2263.9 11.7 convolution_bitcast_fusion.2
  2281.2 112.8 %reduce-scatter.20.cloned.1.call-done = f32[4,2,64,1024]{3,2,1,0:T(8,128)} async-done(((f32[4,2,256,1024]{3,2,1,0:T(8,128)}), f32[4,2,64,1024]{3,2,1,0:T(8,128)}) %reduce-scatter.20.cloned.1.call-update) | async-done | bytes 2097168 | tf_op jit(solution)/shard_map/reduce_scatter | solution.py:281
  2396.8 6.4 copy.112
  2403.2 7.4 reshape.169
  2415.1 18.0 reduce-scatter.22.cloned.1.call-done
  2453.1 24.7 all-reduce.2
  2477.8 203.0 %all-reduce.8.cloned.1.call-done = (f32[1024,6,256]{2,0,1:T(8,128)}, f32[1024,3,256]{2,0,1:T(8,128)}, f32[256,1024]{1,0:T(8,128)}, f32[1024,1024]{1,0:T(8,128)}, f32[1024,1024]{1,0:T(8,128)}) async-done(((f32[1024,6,256]{2,0,1:T(8,128)}, f32[1024,3,256]{2,0,1:T(8,128)}, f32[256,1024]{1,0:T(8,128)}, f32[1024,1024]{1,0:T(8,128)}, f32[1024,1024]{1,0:T(8,128)}), (f32[1024,6,256]{2,0,1:T(8,128)}, ...) | async-done | bytes 18874384 | tf_op jit(solution)/shard_map/psum | solution.py:310
  2680.9 6.4 copy.199
  (266 shorter events, 209.1 us)
Async XLA Ops:
  7.2 105.2 %all-gather.8.cloned.1.call-start = ((), (), s32[]{:S(2)}) async-start(), calls=%async_computation.5 | async-start | bytes 5242880 | tf_op jit(solution)/shard_map/all_gather | solution.py:96
  7.2 21.4 copy-start.5
  9.9 18.7 copy-start.33
  11.6 17.1 copy-start.35
  12.5 16.1 copy-start.25
  12.5 16.1 copy-start.27
  28.6 89.5 %copy-start.22 = (f32[4,2,1024]{2,1,0:T(2,128)}, f32[4,2,1024]{2,1,0:T(2,128)S(1)}, u32[]{:S(2)}) copy-start(f32[4,2,1024]{2,1,0:T(2,128)S(1)} %copy.72) | copy-start | bytes 98308
  30.2 91.7 %copy-start.37 = (bf16[2,256]{1,0:T(2,128)(2,1)S(1)}, bf16[2,256]{1,0:T(2,128)(2,1)}, u32[]{:S(2)}) copy-start(bf16[2,256]{1,0:T(2,128)(2,1)} %param.26) | copy-start | bytes 3076
  30.2 144.7 %all-gather.18.cloned.1.call-start = ((), (), s32[]{:S(2)}) async-start(), calls=%async_computation.14 | async-start | bytes 9437184 | tf_op jit(solution)/shard_map/all_gather | solution.py:105
  121.9 110.0 %all-gather.10.cloned.1.call-start = ((), (), s32[]{:S(2)}) async-start(), calls=%async_computation.6 | async-start | bytes 9437184 | tf_op jit(solution)/shard_map/all_gather | solution.py:106
  124.9 408.0 %reduce-scatter.14.cloned.1.call-start = ((), (), s32[]{:S(2)}) async-start(), calls=%async_computation.7 | async-start | bytes 10485760 | tf_op jit(solution)/shard_map/reduce_scatter | solution.py:154
  267.6 351.0 %all-gather.12.cloned.1.call-start = ((), (), s32[]{:S(2)}) async-start(), calls=%async_computation.8 | async-start | bytes 5242880 | tf_op jit(solution)/shard_map/all_gather | solution.py:160
  537.0 163.0 %all-gather.14.cloned.1.call-start = ((), (), s32[]{:S(2)}) async-start(), calls=%async_computation.10 | async-start | bytes 5242880 | tf_op jit(solution)/shard_map/all_gather | solution.py:175
  539.5 326.3 %reduce-scatter.18.cloned.1.call-start = ((), (), s32[]{:S(2)}) async-start(), calls=%async_computation.11 | async-start | bytes 10485760 | tf_op jit(solution)/shard_map/reduce_scatter | solution.py:189
  539.8 183.3 %copy-start.38 = (f32[1024]{0:T(1024)}, f32[1024]{0:T(1024)S(1)}, u32[]{:S(2)}) copy-start(f32[1024]{0:T(1024)S(1)} %convert_element_type.127) | copy-start | bytes 12292
  699.9 15.8 copy-start.45
  722.6 223.5 %reduce-scatter.16.cloned.1.call-start = ((), (), s32[]{:S(2)}) async-start(), calls=%async_computation.9 | async-start | bytes 5242880 | tf_op jit(solution)/shard_map/reduce_scatter | solution.py:168
  734.9 300.3 %all-gather.16.cloned.1.call-start = ((), (), s32[]{:S(2)}) async-start(), calls=%async_computation.12 | async-start | bytes 5242880 | tf_op jit(solution)/shard_map/all_gather | solution.py:200
  951.2 84.0 %copy-start.24 = (bf16[256,1024]{1,0:T(8,128)(2,1)S(1)}, bf16[256,1024]{1,0:T(8,128)(2,1)}, u32[]{:S(2)}) copy-start(bf16[256,1024]{1,0:T(8,128)(2,1)} %param.27) | copy-start | bytes 1572868
  953.8 1440.1 %reduce-scatter.20.cloned.1.call-start = ((), (), s32[]{:S(2)}) async-start(), calls=%async_computation.13 | async-start | bytes 10485760 | tf_op jit(solution)/shard_map/reduce_scatter | solution.py:281
  2252.5 180.6 %reduce-scatter.22.cloned.1.call-start = ((), (), s32[]{:S(2)}) async-start(), calls=%async_computation.15 | async-start | bytes 655360
  2275.6 118.3 %copy-start.6 = (bf16[4,2,64,1024]{3,2,1,0:T(8,128)(2,1)S(1)}, bf16[4,2,64,1024]{3,2,1,0:T(8,128)(2,1)}, u32[]{:S(2)}) copy-start(bf16[4,2,64,1024]{3,2,1,0:T(8,128)(2,1)} %param.21) | copy-start | bytes 3145732
  2275.6 118.3 %copy-start.23 = (f32[4,2,1024]{2,1,0:T(2,128)S(1)}, f32[4,2,1024]{2,1,0:T(2,128)}, u32[]{:S(2)}) copy-start(f32[4,2,1024]{2,1,0:T(2,128)} %copy-done.22) | copy-start | bytes 98308
  2275.6 118.3 %copy-start.34 = (f32[4,2,64]{2,1,0:T(2,128)S(1)}, f32[4,2,64]{2,1,0:T(2,128)}, u32[]{:S(2)}) copy-start(f32[4,2,64]{2,1,0:T(2,128)} %copy-done.33) | copy-start | bytes 6148
  2275.7 118.3 %copy-start.36 = (f32[4,2,64]{2,1,0:T(2,128)S(1)}, f32[4,2,64]{2,1,0:T(2,128)}, u32[]{:S(2)}) copy-start(f32[4,2,64]{2,1,0:T(2,128)} %copy-done.35) | copy-start | bytes 6148
  2275.7 121.0 %copy-start.32 = (f32[4,2,1024]{2,1,0:T(2,128)S(1)}, f32[4,2,1024]{2,1,0:T(2,128)}, u32[]{:S(2)}) copy-start(f32[4,2,1024]{2,1,0:T(2,128)} %get-tuple-element.504) | copy-start | bytes 98308
  2275.7 121.0 %copy-start.30 = (f32[4,2,1024]{2,1,0:T(2,128)S(1)}, f32[4,2,1024]{2,1,0:T(2,128)}, u32[]{:S(2)}) copy-start(f32[4,2,1024]{2,1,0:T(2,128)} %get-tuple-element.416) | copy-start | bytes 98308
  2275.7 121.0 %copy-start.29 = (f32[4,2,1024]{2,1,0:T(2,128)S(1)}, f32[4,2,1024]{2,1,0:T(2,128)}, u32[]{:S(2)}) copy-start(f32[4,2,1024]{2,1,0:T(2,128)} %get-tuple-element.410) | copy-start | bytes 98308
  2275.7 121.0 %copy-start.31 = (f32[4,2,1024]{2,1,0:T(2,128)S(1)}, f32[4,2,1024]{2,1,0:T(2,128)}, u32[]{:S(2)}) copy-start(f32[4,2,1024]{2,1,0:T(2,128)} %get-tuple-element.517) | copy-start | bytes 98308
  2410.6 24.7 copy-start.26
  2410.6 24.7 copy-start.28
  2410.6 270.3 %all-reduce.8.cloned.1.call-start = ((), (), s32[]{:S(2)}) async-start(), calls=%async_computation.16 | async-start | bytes 37748736 | tf_op jit(solution)/shard_map/psum | solution.py:310
  (33 other events, 155.9 us)
Sparse Core Ops, SparseCore 0:
  30.3 82.0 all-gather.7
  122.0 52.9 all-gather.17
  177.4 54.3 all-gather.9
  267.7 265.1 reduce-scatter.13
  537.1 81.4 all-gather.11
  620.6 79.2 all-gather.13
  722.8 142.9 reduce-scatter.17
  868.7 77.4 reduce-scatter.15
  953.9 81.2 all-gather.15
  2252.6 141.2 reduce-scatter.19
  2410.7 22.3 reduce-scatter.21
  2440.4 240.3 all-reduce.7
where the time goes:
time: 2720 us; the launch traced here: 2700 us
  waiting for transfers between devices  1200 us (44%)
  blocking collectives  1160 us (43%)
  matrix products  159 us (6%)
  local copies, waits for them, and re-layouts  126 us (5%)
  other arithmetic  48.3 us (2%)
    unnamed x1, blocking collectives  1110 us
    reduce_scatter x1, waiting for transfers between devices, on_device(): lax.psum_scatter(attn_term, 'tensor', scatter_dimension=2, tiled=True)  265 us
    psum x1, waiting for transfers between devices, on_device(): lax.psum((grad_ada_weight, grad_ada_bias, grad_qkv_weight, grad_qv_bias,...  203 us
    reduce_scatter x1, waiting for transfers between devices, on_device(): lax.psum_scatter(jnp.einsum('cfph,dh->cfpd', grad_pre, up_weight, preferr...  130 us
    reduce_scatter x1, waiting for transfers between devices, on_device(): lax.psum_scatter(jnp.einsum('cfpkj,dkj->cfpd', grad_projected, qkv_weight...  113 us
    all_gather x1, waiting for transfers between devices, on_device(): hidden_all = lax.all_gather(hidden_one, 'tensor', axis=2, tiled=True)  82.1 us
    all_gather x1, waiting for transfers between devices, on_device(): grad_one_all = lax.all_gather(grad_branch_one, 'tensor', axis=2, tiled=True)  80.1 us
    all_gather x1, waiting for transfers between devices, on_device(): hidden_two_all = lax.all_gather(hidden_two, 'tensor', axis=2, tiled=True)  78.8 us
  transfers between devices with their start and end apart: 12, of which 12 were waited for; matrix products, arithmetic and copies ran while one was open for 4% of the time, Pallas kernels for 0%

commit v1 on v0

v1 whole, which is shorter than its diff:
```python
from functools import partial
import math

import jax
import jax.numpy as jnp
from jax import lax
from jax.experimental import pallas as pl
from jax.experimental.pallas import tpu as pltpu
from jax.sharding import PartitionSpec as P

HD = 64
f32 = jnp.float32
bf16 = jnp.bfloat16
score_scale = HD ** (-0.5)


def noise_embedding(noise_steps, model_width):
    half_width = model_width // 2
    frequency = jnp.exp(-math.log(10000.0) * jnp.arange(half_width, dtype=f32) / half_width)
    angles = noise_steps.astype(f32)[..., None] * frequency
    return jnp.concatenate([jnp.cos(angles), jnp.sin(angles)], axis=-1)


def noise_activation(noise_steps, model_width):
    return jax.nn.silu(noise_embedding(noise_steps, model_width)).astype(bf16)


def layer_norm(values):
    centred = values - jnp.mean(values, axis=-1, keepdims=True)
    inverse = lax.rsqrt(jnp.mean(centred * centred, axis=-1, keepdims=True) + 1e-06)
    return (centred * inverse, inverse)


def norm_back(grad_normed, normed, inverse):
    return inverse * (
        grad_normed
        - jnp.mean(grad_normed, axis=-1, keepdims=True)
        - normed * jnp.mean(grad_normed * normed, axis=-1, keepdims=True)
    )


def dot(left, right):
    return lax.dot_general(left, right, (((1,), (0,)), ((), ())), preferred_element_type=f32)


def dot_nt(left, right):
    return lax.dot_general(left, right, (((1,), (1,)), ((), ())), preferred_element_type=f32)


def dot_tn(left, right):
    return lax.dot_general(left, right, (((0,), (0,)), ((), ())), preferred_element_type=f32)


def head_blocks(transposed, head_count, patch_count):
    rows = lax.broadcasted_iota(jnp.int32, transposed.shape, 0) // HD
    return jnp.concatenate(
        [jnp.where(rows == head, transposed, 0.0) for head in range(head_count)], axis=1
    ).astype(bf16)


def head_rows(natural, head_count):
    lanes = lax.broadcasted_iota(jnp.int32, natural.shape, 1) // HD
    return jnp.concatenate(
        [jnp.where(lanes == head, natural, 0.0) for head in range(head_count)], axis=0
    ).astype(bf16)


def attend_kernel(frame_ids, q_ref, k_ref, vt_ref, out_ref, lse_ref, *, head_count, patch_count):
    key_stop = frame_ids[pl.program_id(0)] + 1
    q_cols = head_blocks(
        jnp.swapaxes(q_ref[...].astype(f32), 0, 1) * score_scale, head_count, patch_count
    )
    width = head_count * patch_count

    def step(index, carry):
        row_max, row_total, sums = carry
        start = pl.multiple_of(index * patch_count, patch_count)
        scores = dot(k_ref[pl.ds(start, patch_count), :], q_cols)
        new_max = jnp.maximum(row_max, jnp.max(scores, axis=0, keepdims=True))
        rescale = jnp.exp(row_max - new_max)
        weights = jnp.exp(scores - new_max)
        row_total = row_total * rescale + jnp.sum(weights, axis=0, keepdims=True)
        weights = weights.astype(bf16)
        values_t = vt_ref[:, pl.ds(start, patch_count)]
        parts = []
        for head in range(head_count):
            cols = slice(head * patch_count, (head + 1) * patch_count)
            rows = slice(head * HD, (head + 1) * HD)
            parts.append(sums[head] * rescale[:, cols] + dot(values_t[rows], weights[:, cols]))
        return (new_max, row_total, tuple(parts))

    row_max, row_total, sums = lax.fori_loop(
        0,
        key_stop,
        step,
        (
            jnp.full((1, width), -1e30, f32),
            jnp.zeros((1, width), f32),
            tuple(jnp.zeros((HD, patch_count), f32) for _ in range(head_count)),
        ),
    )
    inverse = 1.0 / row_total
    out_t = jnp.concatenate(
        [
            sums[head] * inverse[:, head * patch_count : (head + 1) * patch_count]
            for head in range(head_count)
        ],
        axis=0,
    )
    out_ref[...] = jnp.swapaxes(out_t, 0, 1).astype(bf16)
    lse_ref[0] = row_max + jnp.log(row_total)


def attend(queries, keys, values, frame_ids, head_count, patch_count):
    row_count, lanes = queries.shape
    key_rows = keys.shape[0]
    steps = row_count // patch_count
    width = head_count * patch_count
    pairs = steps * (key_rows // patch_count + 1) // 2
    work = pairs * patch_count * width
    return pl.pallas_call(
        partial(attend_kernel, head_count=head_count, patch_count=patch_count),
        grid_spec=pltpu.PrefetchScalarGridSpec(
            num_scalar_prefetch=1,
            grid=(steps,),
            in_specs=[
                pl.BlockSpec((patch_count, lanes), lambda j, ids: (j, 0)),
                pl.BlockSpec((key_rows, lanes), lambda j, ids: (0, 0)),
                pl.BlockSpec((lanes, key_rows), lambda j, ids: (0, 0)),
            ],
            out_specs=[
                pl.BlockSpec((patch_count, lanes), lambda j, ids: (j, 0)),
                pl.BlockSpec((1, 1, width), lambda j, ids: (j, 0, 0)),
            ],
        ),
        out_shape=[
            jax.ShapeDtypeStruct((row_count, lanes), bf16),
            jax.ShapeDtypeStruct((steps, 1, width), f32),
        ],
        compiler_params=pltpu.CompilerParams(vmem_limit_bytes=32 << 20),
        cost_estimate=pl.CostEstimate(
            flops=work * 1024, bytes_accessed=8 * row_count * lanes, transcendentals=work
        ),
        name="attend",
    )(frame_ids, queries, keys, values.T)


def attend_back_kernel(
    frame_ids,
    q_ref,
    grad_ref,
    out_ref,
    lse_ref,
    k_ref,
    v_ref,
    kt_ref,
    dq_ref,
    dk_ref,
    dv_ref,
    dk_sum,
    dv_sum,
    *,
    head_count,
    patch_count,
):
    position = pl.program_id(0)
    key_stop = frame_ids[position] + 1

    @pl.when(position == 0)
    def _():
        dk_sum[...] = jnp.zeros_like(dk_sum)
        dv_sum[...] = jnp.zeros_like(dv_sum)

    q_rows = q_ref[...].astype(f32) * score_scale
    grad_rows = grad_ref[...].astype(f32)
    grad_t = jnp.swapaxes(grad_rows, 0, 1)
    grad_out_t = grad_t * jnp.swapaxes(out_ref[...].astype(f32), 0, 1)
    delta = jnp.concatenate(
        [
            jnp.sum(grad_out_t[head * HD : (head + 1) * HD], axis=0, keepdims=True)
            for head in range(head_count)
        ],
        axis=1,
    )
    q_cols = head_blocks(jnp.swapaxes(q_rows, 0, 1), head_count, patch_count)
    grad_cols = head_blocks(grad_t, head_count, patch_count)
    q_stack = head_rows(q_rows, head_count)
    grad_stack = head_rows(grad_rows, head_count)
    lse = lse_ref[0]

    def step(index, sums):
        start = pl.multiple_of(index * patch_count, patch_count)
        here = pl.ds(start, patch_count)
        scores = dot(k_ref[here, :], q_cols)
        grad_probs = dot(v_ref[here, :], grad_cols)
        probs = jnp.exp(scores - lse)
        grad_scores = (probs * (grad_probs - delta)).astype(bf16)
        dv_sum[here, :] += dot(probs.astype(bf16), grad_stack)
        dk_sum[here, :] += dot(grad_scores, q_stack)
        keys_t = kt_ref[:, here]
        return tuple(
            sums[head]
            + dot(
                keys_t[head * HD : (head + 1) * HD],
                grad_scores[:, head * patch_count : (head + 1) * patch_count],
            )
            for head in range(head_count)
        )

    sums = lax.fori_loop(
        0, key_stop, step, tuple(jnp.zeros((HD, patch_count), f32) for _ in range(head_count))
    )
    dq_t = jnp.concatenate(sums, axis=0) * score_scale
    dq_ref[...] = jnp.swapaxes(dq_t, 0, 1).astype(bf16)

    @pl.when(position == pl.num_programs(0) - 1)
    def _():
        dk_ref[...] = dk_sum[...].astype(bf16)
        dv_ref[...] = dv_sum[...].astype(bf16)


def attend_back(queries, keys, values, out, lse, grad, frame_ids, head_count, patch_count):
    row_count, lanes = queries.shape
    key_rows = keys.shape[0]
    steps = row_count // patch_count
    width = head_count * patch_count
    pairs = steps * (key_rows // patch_count + 1) // 2
    work = pairs * patch_count * width
    block = pl.BlockSpec((patch_count, lanes), lambda j, ids: (j, 0))
    whole = pl.BlockSpec((key_rows, lanes), lambda j, ids: (0, 0))
    return pl.pallas_call(
        partial(attend_back_kernel, head_count=head_count, patch_count=patch_count),
        grid_spec=pltpu.PrefetchScalarGridSpec(
            num_scalar_prefetch=1,
            grid=(steps,),
            in_specs=[
                block,
                block,
                block,
                pl.BlockSpec((1, 1, width), lambda j, ids: (j, 0, 0)),
                whole,
                whole,
                pl.BlockSpec((lanes, key_rows), lambda j, ids: (0, 0)),
            ],
            out_specs=[block, whole, whole],
            scratch_shapes=[
                pltpu.VMEM((key_rows, lanes), f32),
                pltpu.VMEM((key_rows, lanes), f32),
            ],
        ),
        out_shape=[
            jax.ShapeDtypeStruct((row_count, lanes), bf16),
            jax.ShapeDtypeStruct((key_rows, lanes), bf16),
            jax.ShapeDtypeStruct((key_rows, lanes), bf16),
        ],
        compiler_params=pltpu.CompilerParams(vmem_limit_bytes=40 << 20),
        cost_estimate=pl.CostEstimate(
            flops=work * 2560, bytes_accessed=16 * row_count * lanes, transcendentals=work
        ),
        name="attend_back",
    )(frame_ids, queries, grad, out, lse, keys, values, keys.T)


def on_device(
    tokens,
    noise_steps,
    ada_weight,
    ada_bias,
    qkv_weight,
    qv_bias,
    out_weight,
    out_bias,
    up_weight,
    up_bias,
    down_weight,
    down_bias,
    cotangent,
):
    clip_count, local_frames, local_patches, model_width = tokens.shape
    tensor_count = lax.axis_size("tensor")
    frame_devices = lax.axis_size("frame")
    frame_at = lax.axis_index("frame")
    tensor_at = lax.axis_index("tensor")
    patch_count = local_patches * tensor_count
    hidden_width = up_weight.shape[1] * tensor_count
    head_total = model_width // HD
    shard_heads = head_total // tensor_count
    head_count = head_total // frame_devices
    lanes = head_count * HD
    unit_total = clip_count * local_frames
    units = unit_total // tensor_count
    sharers = tensor_count // clip_count
    share_at = tensor_at % sharers
    frame_count = frame_devices * local_frames
    own_rows = units * patch_count
    all_rows = frame_devices * own_rows
    slot = frame_at % shard_heads
    first_shard = (frame_at // shard_heads) * head_count
    shard_groups = tensor_count // head_count


    def to_units(values):
        return lax.all_to_all(
            values.reshape(unit_total, local_patches, model_width),
            "tensor",
            split_axis=0,
            concat_axis=1,
            tiled=True,
        )

    def from_units(values):
        return lax.all_to_all(
            values, "tensor", split_axis=1, concat_axis=0, tiled=True
        ).reshape(clip_count, local_frames, local_patches, model_width)

    unit_tokens = to_units(tokens)
    act_noise = noise_activation(noise_steps, model_width).reshape(unit_total, model_width)
    mod_local = jnp.einsum(
        "ud,dkj->ukj", act_noise, ada_weight, preferred_element_type=f32
    ) + ada_bias.astype(f32)
    modulation = lax.all_to_all(mod_local, "tensor", split_axis=0, concat_axis=2, tiled=True)
    shift_one = modulation[:, None, 0]
    scale_one = modulation[:, None, 1]
    gate_one = modulation[:, None, 2]
    shift_two = modulation[:, None, 3]
    scale_two = modulation[:, None, 4]
    gate_two = modulation[:, None, 5]

    slot_weight = lax.dynamic_slice_in_dim(qkv_weight, slot * HD, HD, axis=2)
    slot_weight = slot_weight.transpose(1, 2, 0).reshape(3 * HD, model_width)
    slots_all = lax.all_gather(slot_weight, "tensor", axis=0)
    head_weight = lax.dynamic_slice_in_dim(slots_all, first_shard, head_count, axis=0)
    head_weight = (
        head_weight.reshape(head_count, 3, HD, model_width)
        .transpose(1, 0, 2, 3)
        .reshape(3 * lanes, model_width)
    )
    slot_bias = lax.dynamic_slice_in_dim(qv_bias, slot * HD, HD, axis=1).reshape(2 * HD)
    small_all = lax.all_gather(jnp.concatenate([slot_bias, up_bias]), "tensor", axis=0)
    head_bias = lax.dynamic_slice_in_dim(small_all[:, : 2 * HD], first_shard, head_count, axis=0)
    head_bias = head_bias.reshape(head_count, 2, HD).transpose(1, 0, 2).reshape(2, lanes)
    head_bias = head_bias.astype(f32)
    qkv_bias = jnp.concatenate([head_bias[0], jnp.zeros((lanes,), f32), head_bias[1]])
    hidden_part = hidden_width // (tensor_count * frame_devices)
    up_bias_all = (
        small_all[:, 2 * HD :]
        .reshape(tensor_count, frame_devices, hidden_part)
        .transpose(1, 0, 2)
        .reshape(hidden_width)
        .astype(f32)
    )

    token_values = unit_tokens.astype(f32)
    normed_one, inverse_one = layer_norm(token_values)
    hidden_one = (normed_one * (1.0 + scale_one) + shift_one).astype(bf16)
    hidden_all = lax.all_gather(
        hidden_one.reshape(own_rows, model_width), "frame", axis=0, tiled=True
    )

    def own_part(values):
        size = values.shape[0] // frame_devices
        return lax.dynamic_slice_in_dim(values, frame_at * size, size, axis=0)

    out_part = lax.all_gather(own_part(out_weight), "tensor", axis=0)
    up_part = lax.all_gather(own_part(up_weight), "tensor", axis=0)
    down_part = lax.all_gather(own_part(down_weight), "tensor", axis=0)
    out_rows = out_part.shape[1]
    up_rows = up_part.shape[1]
    up_part = (
        up_part.reshape(tensor_count, up_rows, frame_devices, hidden_part)
        .transpose(1, 2, 0, 3)
        .reshape(up_rows, hidden_width)
    )
    out_full = lax.all_gather(out_part, "frame", axis=0)
    head_parts = HD // out_rows
    out_full = (
        out_full.reshape(
            shard_heads, head_parts, shard_groups, head_count, out_rows, model_width
        )
        .transpose(2, 0, 3, 1, 4, 5)
        .reshape(model_width, model_width)
    )
    up_full = lax.all_gather(up_part, "frame", axis=0, tiled=True)
    down_full = lax.all_gather(down_part, "frame", axis=0).reshape(hidden_width, model_width)

    projected = (dot_nt(hidden_all, head_weight) + qkv_bias).astype(bf16)
    queries = projected[:, :lanes]
    keys = projected[:, lanes : 2 * lanes]
    values = projected[:, 2 * lanes :]

    def share(mine):
        if sharers == 1:
            return mine
        pieces = [mine]
        for shift in range(1, sharers):
            perm = [
                (t, (t // sharers) * sharers + (t + shift) % sharers) for t in range(tensor_count)
            ]
            pieces.append(lax.ppermute(mine, "tensor", perm))
        stacked = jnp.stack(pieces)
        stacked = jnp.stack(
            [
                lax.dynamic_index_in_dim(
                    stacked, (share_at - member) % sharers, 0, keepdims=False
                )
                for member in range(sharers)
            ]
        )
        return (
            stacked.reshape(sharers, frame_devices, own_rows, lanes)
            .transpose(1, 0, 2, 3)
            .reshape(sharers * all_rows, lanes)
        )

    def unshare(partial_sums):
        if sharers == 1:
            return partial_sums
        pieces = (
            partial_sums.reshape(frame_devices, sharers, own_rows, lanes)
            .transpose(1, 0, 2, 3)
            .reshape(sharers, all_rows, lanes)
        )
        total = lax.dynamic_index_in_dim(pieces, share_at, 0, keepdims=False).astype(f32)
        for shift in range(1, sharers):
            perm = [
                (t, (t // sharers) * sharers + (t + shift) % sharers) for t in range(tensor_count)
            ]
            piece = lax.dynamic_index_in_dim(
                pieces, (share_at + shift) % sharers, 0, keepdims=False
            )
            total = total + lax.ppermute(piece, "tensor", perm).astype(f32)
        return total.astype(bf16)

    keys_all = share(keys)
    values_all = share(values)
    unit_ids = jnp.arange(frame_devices * units, dtype=jnp.int32)
    frame_ids = (
        (unit_ids // units) * local_frames + share_at.astype(jnp.int32) * units + unit_ids % units
    )
    attended_heads, row_lse = attend(
        queries, keys_all, values_all, frame_ids, head_count, patch_count
    )
    attended = lax.all_to_all(
        attended_heads.reshape(frame_devices, own_rows, lanes),
        "frame",
        split_axis=0,
        concat_axis=2,
        tiled=True,
    ).reshape(own_rows, model_width)

    unit_shape = (units, patch_count, model_width)
    branch_one = dot(attended, out_full).reshape(unit_shape) + out_bias.astype(f32)
    middle = token_values + gate_one * branch_one
    normed_two, inverse_two = layer_norm(middle)
    hidden_two = (normed_two * (1.0 + scale_two) + shift_two).astype(bf16)
    hidden_two = hidden_two.reshape(own_rows, model_width)
    pre_gelu = dot(hidden_two, up_full) + up_bias_all
    activated = jax.nn.gelu(pre_gelu, approximate=True).astype(bf16)
    branch_two = dot(activated, down_full).reshape(unit_shape) + down_bias.astype(f32)
    result = from_units((middle + gate_two * branch_two).astype(bf16))

    upstream = to_units(cotangent).astype(f32)
    grad_branch_two = (gate_two * upstream).astype(bf16)
    grad_gate_two = jnp.sum(upstream * branch_two, axis=1)
    grad_two = grad_branch_two.reshape(own_rows, model_width)
    grad_down_bias = jnp.sum(grad_two.astype(f32), axis=0)
    grad_down = dot_tn(activated, grad_two).astype(bf16)
    grad_down_sum = lax.psum_scatter(grad_down, "frame", scatter_dimension=0, tiled=True)
    grad_activated = dot_nt(grad_two, down_full)
    gelu_back = jax.vjp(partial(jax.nn.gelu, approximate=True), pre_gelu)[1]
    grad_pre = gelu_back(grad_activated)[0].astype(bf16)
    grad_up_bias = jnp.sum(grad_pre.astype(f32), axis=0)
    grad_up = dot_tn(hidden_two, grad_pre).astype(bf16)
    grad_up_sum = lax.psum_scatter(grad_up, "frame", scatter_dimension=0, tiled=True)
    grad_hidden_two = dot_nt(grad_pre, up_full).reshape(unit_shape)
    grad_scale_two = jnp.sum(grad_hidden_two * normed_two, axis=1)
    grad_shift_two = jnp.sum(grad_hidden_two, axis=1)
    grad_middle = upstream + norm_back(grad_hidden_two * (1.0 + scale_two), normed_two, inverse_two)
    grad_branch_one = (gate_one * grad_middle).astype(bf16)
    grad_gate_one = jnp.sum(grad_middle * branch_one, axis=1)
    grad_one = grad_branch_one.reshape(own_rows, model_width)
    grad_out_bias = jnp.sum(grad_one.astype(f32), axis=0)
    grad_attended = dot_nt(grad_one, out_full).astype(bf16)
    grad_heads = lax.all_to_all(
        grad_attended.reshape(own_rows, frame_devices, lanes),
        "frame",
        split_axis=1,
        concat_axis=0,
        tiled=True,
    ).reshape(all_rows, lanes)
    grad_out = (
        dot_tn(attended, grad_one)
        .astype(bf16)
        .reshape(shard_groups, shard_heads, head_count, head_parts, out_rows, model_width)
        .transpose(1, 3, 0, 2, 4, 5)
        .reshape(frame_devices, tensor_count * out_rows, model_width)
    )
    width_part = model_width // frame_devices
    bias_row = jnp.concatenate(
        [
            grad_down_bias.reshape(frame_devices, width_part),
            grad_out_bias.reshape(frame_devices, width_part),
            grad_up_bias.reshape(frame_devices, tensor_count * hidden_part),
        ],
        axis=1,
    ).astype(bf16)
    bias_row = jnp.pad(
        bias_row[:, None, :], ((0, 0), (0, 15), (0, model_width - bias_row.shape[1]))
    )
    grad_out_sum = lax.psum_scatter(
        jnp.concatenate([grad_out, bias_row], axis=1).reshape(-1, model_width),
        "frame",
        scatter_dimension=0,
        tiled=True,
    )
    bias_sum = grad_out_sum[tensor_count * out_rows]
    down_out_bias = jnp.broadcast_to(bias_sum[: 2 * width_part], (tensor_count, 2 * width_part))
    up_bias_sum = bias_sum[2 * width_part : 2 * width_part + tensor_count * hidden_part].reshape(
        tensor_count, hidden_part
    )
    bias_tail = jnp.concatenate([down_out_bias, up_bias_sum], axis=1)
    bias_tail = jnp.pad(
        bias_tail[:, None, :], ((0, 0), (0, 15), (0, model_width - bias_tail.shape[1]))
    )
    up_tail = (
        grad_up_sum.reshape(up_rows, frame_devices, tensor_count, hidden_part)
        .transpose(2, 0, 1, 3)
        .reshape(tensor_count, -1, model_width)
    )
    tails = [
        grad_down_sum.reshape(tensor_count, hidden_part, model_width),
        up_tail,
        grad_out_sum[: tensor_count * out_rows].reshape(tensor_count, out_rows, model_width),
        bias_tail,
    ]
    sizes = [tail.shape[1] for tail in tails]
    tail_sum = lax.psum_scatter(
        jnp.concatenate(tails, axis=1), "tensor", scatter_dimension=0, tiled=False
    )
    tail_all = lax.all_gather(tail_sum, "frame", axis=0)
    cuts = [0]
    for size in sizes:
        cuts.append(cuts[-1] + size)
    tail_down, tail_up, tail_out, tail_bias = (
        tail_all[:, cuts[n] : cuts[n + 1]].astype(f32) for n in range(4)
    )
    final_down = tail_down.reshape(down_weight.shape)
    final_up = tail_up.reshape(up_weight.shape)
    final_out = tail_out.reshape(out_weight.shape)
    tail_bias = tail_bias[:, 0]
    final_down_bias = tail_bias[:, :width_part].reshape(model_width)
    final_out_bias = tail_bias[:, width_part : 2 * width_part].reshape(model_width)
    final_up_bias = tail_bias[:, 2 * width_part : 2 * width_part + hidden_part].reshape(
        up_bias.shape
    )

    grad_q, grad_k_all, grad_v_all = attend_back(
        queries,
        keys_all,
        values_all,
        attended_heads,
        row_lse,
        grad_heads,
        frame_ids,
        head_count,
        patch_count,
    )
    grad_k = unshare(grad_k_all)
    grad_v = unshare(grad_v_all)
    grad_projected = jnp.concatenate([grad_q, grad_k, grad_v], axis=1)
    grad_hidden_one = lax.psum_scatter(
        dot(grad_projected, head_weight).astype(bf16), "frame", scatter_dimension=0, tiled=True
    )
    grad_hidden_one = grad_hidden_one.astype(f32).reshape(unit_shape)

    grad_head_weight = dot_tn(grad_projected, hidden_all).astype(bf16)
    grad_slots = (
        grad_head_weight.reshape(3, head_count, HD, model_width)
        .transpose(1, 0, 2, 3)
        .reshape(head_count, 3 * HD, model_width)
    )
    grad_head_bias = jnp.stack(
        [jnp.sum(grad_q.astype(f32), axis=0), jnp.sum(grad_v.astype(f32), axis=0)]
    ).astype(bf16)
    grad_head_bias = grad_head_bias.reshape(2, head_count, HD).transpose(1, 0, 2)
    grad_head_bias = jnp.pad(
        grad_head_bias.reshape(head_count, 1, 2 * HD),
        ((0, 0), (0, 15), (0, model_width - 2 * HD)),
    )
    grad_slots = jnp.concatenate([grad_slots, grad_head_bias], axis=1)
    slot_rows = grad_slots.shape[1]
    grad_slots = lax.dynamic_update_slice_in_dim(
        jnp.zeros((tensor_count, slot_rows, model_width), bf16), grad_slots, first_shard, axis=0
    )
    slots_sum = lax.psum_scatter(grad_slots, "tensor", scatter_dimension=0, tiled=False)
    slots_sum = lax.all_gather(slots_sum, "frame", axis=0)
    slots_sum = lax.dynamic_slice_in_dim(
        slots_sum, (tensor_at // head_count) * shard_heads, shard_heads, axis=0
    ).astype(f32)
    final_qkv = (
        slots_sum[:, : 3 * HD]
        .reshape(shard_heads, 3, HD, model_width)
        .transpose(3, 1, 0, 2)
        .reshape(qkv_weight.shape)
    )
    final_qv_bias = (
        slots_sum[:, 3 * HD, : 2 * HD]
        .reshape(shard_heads, 2, HD)
        .transpose(1, 0, 2)
        .reshape(qv_bias.shape)
    )

    grad_scale_one = jnp.sum(grad_hidden_one * normed_one, axis=1)
    grad_shift_one = jnp.sum(grad_hidden_one, axis=1)
    grad_tokens = grad_middle + norm_back(
        grad_hidden_one * (1.0 + scale_one), normed_one, inverse_one
    )
    grad_tokens = from_units(grad_tokens.astype(bf16)).astype(f32)
    grad_modulation = jnp.stack(
        [
            grad_shift_one,
            grad_scale_one,
            grad_gate_one,
            grad_shift_two,
            grad_scale_two,
            grad_gate_two,
        ],
        axis=1,
    )
    grad_mod_local = lax.all_to_all(
        grad_modulation, "tensor", split_axis=2, concat_axis=0, tiled=True
    )
    grad_mod_all = lax.all_gather(grad_mod_local, "frame", axis=0, tiled=True)
    noise_all = lax.all_gather(noise_steps, "frame", axis=0)
    act_all = noise_activation(noise_all, model_width).reshape(-1, model_width)
    grad_ada_weight = jnp.einsum(
        "ud,ukj->dkj", act_all.astype(f32), grad_mod_all, precision=lax.Precision.HIGH
    )
    grad_ada_bias = jnp.sum(grad_mod_all, axis=0)
    return (
        result,
        grad_tokens,
        grad_ada_weight,
        grad_ada_bias,
        final_qkv,
        final_qv_bias,
        final_out,
        final_out_bias,
        final_up,
        final_up_bias,
        final_down,
        final_down_bias,
    )


def solution(mesh):
    in_specs = (
        P(None, "frame", "tensor", None),
        P(None, "frame"),
        P(None, None, "tensor"),
        P(None, "tensor"),
        P(None, None, "tensor"),
        P(None, "tensor"),
        P("tensor", None),
        P(),
        P(None, "tensor"),
        P("tensor"),
        P("tensor", None),
        P(),
        P(None, "frame", "tensor", None),
    )
    out_specs = (
        P(None, "frame", "tensor", None),
        P(None, "frame", "tensor", None),
        P(None, None, "tensor"),
        P(None, "tensor"),
        P(None, None, "tensor"),
        P(None, "tensor"),
        P("tensor", None),
        P(),
        P(None, "tensor"),
        P("tensor"),
        P("tensor", None),
        P(),
    )
    return jax.shard_map(
        on_device, mesh=mesh, in_specs=in_specs, out_specs=out_specs, check_vma=False
    )
```

time: 2720 us -> 859 us (0.32)
  blocking collectives: 1160 us -> 100 us
  waiting for transfers between devices: 1200 us -> 356 us
  Pallas kernels: 0 us -> 135 us
  local copies, waits for them, and re-layouts: 126 us -> 66 us
  matrix products: 159 us -> 105 us
  starting transfers between devices: 1.69 us -> 31.2 us
    unnamed x1 -> x0, blocking collectives: 1110 us -> none
    reduce_scatter x4 -> x6, waiting for transfers between devices: 585 us -> 214 us  [the longest x1 68.2 us: on_device(): lax.psum_scatter(dot(grad_projected, head_weight).astype(bf16), 'frame',...]
    all_gather x6 -> x9, waiting for transfers between devices: 392 us -> 79.1 us  [the longest x1 49.6 us: on_device(): lax.all_gather(hidden_one.reshape(own_rows, model_width), 'frame', axis=0...]
    psum x1 -> x0, waiting for transfers between devices: 203 us -> none  [on_device(): lax.psum((grad_ada_weight, grad_ada_bias, grad_qkv_weight, grad_qv_bias,...]
    pallas_call x0 -> x2, Pallas kernels: none -> 135 us  [the longest x1 68.3 us: attend(): pl.pallas_call(partial(attend_kernel, head_count=head_count, patch_count=...]
    all_gather x1 -> x4, blocking collectives: 15.5 us -> 87.5 us  [the longest x1 52.9 us: on_device(): lax.all_gather(jnp.concatenate([slot_bias, up_bias]), 'tensor', axis=0)]
    all_to_all x0 -> x7, waiting for transfers between devices: none -> 62.2 us  [the longest x2 33 us: to_units(): lax.all_to_all(values.reshape(unit_total, local_patches, model_width), 't...]
    dot_general x32 -> x14, matrix products: 159 us -> 105 us  [the longest x4 37.7 us: dot(): lax.dot_general(left, right, (((1,), (0,)), ((), ())), preferred_element_...]
  transfers between devices with their start and end apart: 12 -> 22, of which waited for: 12 -> 11; matrix products, arithmetic and copies ran while one was open for 4% -> 17% of each run, Pallas kernels for 0% -> 16%
where the time goes in v1:
time: 859 us; the launch traced here: 851 us
  waiting for transfers between devices  356 us (41%)
  Pallas kernels  135 us (16%)
  matrix products  105 us (12%)
  blocking collectives  100 us (12%)
  local copies, waits for them, and re-layouts  66 us (8%)
  other arithmetic  42.5 us (5%)
  starting transfers between devices  31.2 us (4%)
  between operations  15.1 us (2%)
    pallas_call x1, Pallas kernels, attend(): pl.pallas_call(partial(attend_kernel, head_count=head_count, patch_count=...  68.3 us
    reduce_scatter x1, waiting for transfers between devices, on_device(): lax.psum_scatter(dot(grad_projected, head_weight).astype(bf16), 'frame',...  68.2 us
    pallas_call x1, Pallas kernels, attend_back(): pl.pallas_call(partial(attend_back_kernel, head_count=head_count, patch_c...  66.7 us
    reduce_scatter x1, waiting for transfers between devices, on_device(): lax.psum_scatter(grad_down, 'frame', scatter_dimension=0, tiled=True)  65.8 us
    all_gather x1, blocking collectives, on_device(): lax.all_gather(jnp.concatenate([slot_bias, up_bias]), 'tensor', axis=0)  52.9 us
    reduce_scatter x1, waiting for transfers between devices, on_device(): lax.psum_scatter(jnp.concatenate(tails, axis=1), 'tensor', scatter_dimens...  52 us
    all_gather x1, waiting for transfers between devices, on_device(): lax.all_gather(hidden_one.reshape(own_rows, model_width), 'frame', axis=0...  49.6 us
    dot_general x4, matrix products, dot(): lax.dot_general(left, right, (((1,), (0,)), ((), ())), preferred_element_...  37.7 us
  transfers between devices with their start and end apart: 22, of which 11 were waited for; matrix products, arithmetic and copies ran while one was open for 17% of the time, Pallas kernels for 16%

profile of v1, /device:TPU:0, one launch (start us, length us, event | category | flops | bytes accessed | tf_op | source)
XLA Modules:
  0.0 850.8 jit_solution(2579070424221385475)
XLA Ops:
  13.5 12.8 %all_to_all.108 = f32[8,6,256]{2,1,0:T(8,128)S(1)} all-to-all(f32[8,6,256]{2,1,0:T(8,128)S(1)} %copy.235), channel_id=1, replica_groups=mesh['frame'=8,'tensor'=4] {'tensor'}, dimensions={0} | all-to-all | bytes 98304 | tf_op jit(solution)/shard_map/all_to_all | solution.py:321
  31.4 33.0 %all-to-all-done = bf16[8,64,1024]{2,1,0:T(8,128)(2,1)S(1)} async-done(((bf16[8,64,1024]{2,1,0:T(8,128)(2,1)}), bf16[8,64,1024]{2,1,0:T(8,128)(2,1)S(1)}, u32[]{:S(2)}, u32[]{:S(2)}) %all-to-all-start) | async-done | bytes 1048608 | tf_op jit(solution)/shard_map/all_to_all | solution.py:303
  71.1 16.5 %all-gather.1 = bf16[128,1024]{1,0:T(8,128)(2,1)} all-gather(bf16[32,1024]{1,0:T(8,128)(2,1)S(1)} %constant_dynamic-slice_fusion.2), channel_id=3, replica_groups=mesh['frame'=8,'tensor'=4] {'tensor'}, dimensions={0}, use_global_device_ids=true | all-gather | bytes 327680 | tf_op jit(solution)/shard_map/all_gather | solution.py:364
  96.0 52.9 %all-gather.7 = bf16[4,1,1152]{2,1,0:T(2,128)(2,1)S(1)} all-gather(bf16[1,1,1152]{2,1,0:T(2,128)(2,1)S(1)} %reshape.479), channel_id=2, replica_groups=mesh['frame'=8,'tensor'=4] {'tensor'}, dimensions={0}, use_global_device_ids=true | all-gather | bytes 11520 | tf_op jit(solution)/shard_map/all_gather | solution.py:339
  150.6 49.6 %all-gather.19.cloned.1.call-done = bf16[4096,1024]{1,0:T(8,128)(2,1)} async-done(((bf16[512,1024]{1,0:T(8,128)(2,1)}), bf16[4096,1024]{1,0:T(8,128)(2,1)}) %all-gather.19.cloned.1.call-update) | async-done | bytes 8388624 | tf_op jit(solution)/shard_map/all_gather | solution.py:356
  200.2 9.2 %add_convert_fusion = bf16[4096,384]{0,1:T(8,128)(2,1)S(1)} fusion(bf16[4096,1024]{1,0:T(8,128)(2,1)} %all-gather.19.cloned.1.call-done, bf16[384,1024]{1,0:T(8,128)(2,1)S(1)} %bitcast.299, f32[384]{0:T(512)S(1)} %pad_maximum_fusion.4), kind=kOutput, calls=%fused_computation.13 | convolution fusion | flops 3224371200 | bytes 12322304 | tf_op jit(solution)/shard_map/dot_general | solution.py:47
  213.9 68.3 %attend.1 = (bf16[4096,128]{1,0:T(8,128)(2,1)S(1)}, f32[16,1,512]{2,1,0:T(1,128)S(1)}) custom-call(s32[16]{0:T(128)S(1)} %fusion.46.frame_ids, bf16[4096,128]{1,0:T(8,128)(2,1)S(1)} %copy.244.q_ref, bf16[4096,128]{1,0:T(8,128)(2,1)S(1)} %copy.245.k_ref, bf16[128,4096]{1,0:T(8,128)(2,1)S(1)} %copy-done.4), custom_call_target="tpu_custom_call" | custom-call | flops 18253611008 | bytes 4194304 | tf_op jit(solution)/shard_map/attend/pallas_call | solution.py:121
  295.8 9.4 %all-to-all-done.2 = bf16[8,512,128]{1,2,0:T(8,128)(2,1)} async-done(((bf16[8,512,128]{1,2,0:T(8,128)(2,1)}), bf16[8,512,128]{1,2,0:T(8,128)(2,1)}, u32[]{:S(2)}, u32[]{:S(2)}) %all-to-all-start.2) | async-done | bytes 1048608 | tf_op jit(solution)/shard_map/all_to_all | solution.py:443
  307.4 5.2 fusion.56
  315.4 11.7 %multiply_convert_fusion = (bf16[512,4096]{1,0:T(8,128)(2,1)}, f32[512,4096]{1,0:T(8,128)}) fusion(f32[4096]{0:T(1024)S(1)} %bitcast.307, bf16[512,1024]{1,0:T(8,128)(2,1)} %bitcast.297, bf16[1024,4096]{0,1:T(8,128)(2,1)} %all-gather.23.cloned.1.call-done), kind=kOutput, calls=%fused_computation.9 | convolution fusion | flops 4315938816 | bytes 22036480 | tf_op jit(solution)/shard_map/dot_general | solution.py:43
  327.1 18.6 %all-gather.35.cloned.1.call-done = bf16[32,128,1024]{2,1,0:T(8,128)(2,1)} async-done(((bf16[4,128,1024]{2,1,0:T(8,128)(2,1)}), bf16[32,128,1024]{2,1,0:T(8,128)(2,1)}) %all-gather.35.cloned.1.call-update) | async-done | bytes 8388624 | tf_op jit(solution)/shard_map/all_gather | solution.py:384
  345.7 12.0 %fusion.16 = (f32[2,1024]{1,0:T(2,128)S(1)}, bf16[2,256,1024]{2,1,0:T(8,128)(2,1)}, bf16[2,256,1024]{2,1,0:T(8,128)(2,1)}) fusion(f32[2,4,64,1024]{3,2,1,0:T(8,128)} %copy.253, f32[1024]{0:T(1024)S(1)} %convert_element_type.250, f32[2,256,1024]{2,1,0:T(8,128)} %copy-done.5, f32[2,1024]{1,0:T(2,128)S(1)} %get-tuple-element.126, ...), kind=kOutput, calls=%fused_computation.40 | convolution fusion | flops 4299159552 | bytes 18894848 | tf_op jit(solution)/shard_map/dot_general | solution.py:43
  357.7 13.8 %fusion.54 = (bf16[4096]{0:T(1024)(128)(2,1)S(1)}, bf16[512,4096]{1,0:T(8,128)(2,1)}) fusion(f32[512,4096]{1,0:T(8,128)} %get-tuple-element.141, f32[4096]{0:T(1024)S(1)} %bitcast.308, bf16[512,1024]{1,0:T(8,128)(2,1)} %bitcast.320, bf16[4096,1024]{1,0:T(8,128)(2,1)S(1)} %bitcast.318), kind=kOutput, calls=%fused_computation.167 | convolution fusion | flops 4341100544 | bytes 22044672 | tf_op jit(solution)/shard_map/dot_general | solution.py:47
  371.5 6.7 fusion.13
  379.6 5.5 fusion.53
  390.2 10.4 %convolution_convert_fusion = bf16[1024,4096]{1,0:T(8,128)(2,1)} fusion(bf16[512,1024]{1,0:T(8,128)(2,1)} %bitcast.298, bf16[512,4096]{1,0:T(8,128)(2,1)} %get-tuple-element.107), kind=kOutput, calls=%fused_computation.10 | convolution fusion | flops 4299161600 | bytes 13631488 | tf_op jit(solution)/shard_map/dot_general | solution.py:51
  402.7 9.2 %convolution_convert_fusion.1 = bf16[4096,1024]{1,0:T(8,128)(2,1)} fusion(bf16[512,4096]{1,0:T(8,128)(2,1)} %get-tuple-element.140, bf16[512,1024]{1,0:T(8,128)(2,1)S(1)} %fusion.12), kind=kOutput, calls=%fused_computation.11 | convolution fusion | flops 4299161600 | bytes 13631488 | tf_op jit(solution)/shard_map/dot_general | solution.py:51
  423.0 16.1 %all-to-all-done.5 = bf16[512,8,128]{2,0,1:T(8,128)(2,1)} async-done(((bf16[512,8,128]{2,0,1:T(8,128)(2,1)}), bf16[512,8,128]{2,0,1:T(8,128)(2,1)}, u32[]{:S(2)}, u32[]{:S(2)}) %all-to-all-start.5) | async-done | bytes 1048608 | tf_op jit(solution)/shard_map/all_to_all | solution.py:484
  441.5 66.7 %attend_back.1 = (bf16[4096,128]{1,0:T(8,128)(2,1)S(1)}, bf16[4096,128]{1,0:T(8,128)(2,1)S(1)}, bf16[4096,128]{1,0:T(8,128)(2,1)S(1)}) custom-call(s32[16]{0:T(128)S(1)} %fusion.46.frame_ids, bf16[4096,128]{1,0:T(8,128)(2,1)S(1)} %copy.244.q_ref, bf16[4096,128]{1,0:T(8,128)(2,1)} %bitcast.54.grad_ref, bf16[4096,128]{1,0:T(8,128)(2,1)S(1)} %get-tuple-element.17.out_ref, ...), custom_call_target="tpu_custom_call" | custom-call | flops 45634027520 | bytes 8388608 | tf_op jit(solution)/shard_map/attend_back/pallas_call | solution.py:231
  510.0 6.8 convolution_convert_fusion.5
  522.4 65.8 %reduce-scatter.11.cloned.1.call-done = bf16[512,1024]{1,0:T(8,128)(2,1)} async-done(((bf16[4096,1024]{1,0:T(8,128)(2,1)}), bf16[512,1024]{1,0:T(8,128)(2,1)}) %reduce-scatter.11.cloned.1.call-update) | async-done | bytes 1048592 | tf_op jit(solution)/shard_map/reduce_scatter | solution.py:468
  592.0 8.7 %convolution_convert_fusion.2 = bf16[4096,1024]{1,0:T(8,128)(2,1)} fusion(bf16[4096,384]{1,0:T(8,128)(2,1)} %copy-done.17, bf16[384,1024]{1,0:T(8,128)(2,1)S(1)} %bitcast.300), kind=kOutput, calls=%fused_computation.12 | convolution fusion | flops 3225419776 | bytes 12320768 | tf_op jit(solution)/shard_map/dot_general | solution.py:43
  600.8 27.8 %reduce-scatter.9.cloned.1.call-done = bf16[1,208,1024]{2,1,0:T(8,128)(2,1)} async-done(((bf16[4,208,1024]{2,1,0:T(8,128)(2,1)}), bf16[1,208,1024]{2,1,0:T(8,128)(2,1)}) %reduce-scatter.9.cloned.1.call-update) | async-done | bytes 426000 | tf_op jit(solution)/shard_map/reduce_scatter | solution.py:595
  628.7 52.0 %reduce-scatter.17.cloned.1.call-done = bf16[1,304,1024]{2,1,0:T(8,128)(2,1)} async-done(((bf16[4,304,1024]{2,1,0:T(8,128)(2,1)}), bf16[1,304,1024]{2,1,0:T(8,128)(2,1)}) %reduce-scatter.17.cloned.1.call-update) | async-done | bytes 622608 | tf_op jit(solution)/shard_map/reduce_scatter | solution.py:537
  687.2 68.2 %reduce-scatter.7.cloned.1.call-done = bf16[512,1024]{1,0:T(8,128)(2,1)} async-done(((bf16[4096,1024]{1,0:T(8,128)(2,1)}), bf16[512,1024]{1,0:T(8,128)(2,1)}) %reduce-scatter.7.cloned.1.call-update) | async-done | bytes 1048592 | tf_op jit(solution)/shard_map/reduce_scatter | solution.py:571
  764.6 4.8 all-to-all-start.7
  775.1 4.3 all-to-all-start.6
  779.5 8.7 %all-gather.8 = s32[8,4,2]{1,2,0:T(2,128)S(1)} all-gather(s32[1,4,2]{1,2,0:T(2,128)S(1)} %bitcast.314), channel_id=8, replica_groups=mesh['frame'=8,'tensor'=4] {'frame'}, dimensions={0}, use_global_device_ids=true | all-gather | bytes 288 | tf_op jit(solution)/shard_map/all_gather | solution.py:634
  804.7 9.3 %all_gather.77 = f32[64,6,256]{2,0,1:T(8,128)S(1)} all-gather(f32[8,6,256]{2,0,1:T(8,128)S(1)} %all_to_all.99), channel_id=1, replica_groups=mesh['frame'=8,'tensor'=4] {'frame'}, dimensions={0}, use_global_device_ids=true | all-gather | bytes 442368 | tf_op jit(solution)/shard_map/all_gather | solution.py:633
  814.6 4.6 fusion.38
  822.1 10.8 %all-gather.27.cloned.1.call-done = bf16[8,304,1024]{2,1,0:T(8,128)(2,1)} async-done(((bf16[1,304,1024]{2,1,0:T(8,128)(2,1)}), bf16[8,304,1024]{2,1,0:T(8,128)(2,1)}) %all-gather.27.cloned.1.call-update) | async-done | bytes 4980752 | tf_op jit(solution)/shard_map/all_gather | solution.py:540
  839.3 4.7 bitcast_convert_fusion
  (272 shorter events, 131.4 us)
Async XLA Ops:
  7.2 80.5 %all-gather.31.cloned.1.call-start = ((), (), s32[]{:S(2)}) async-start(), calls=%async_computation.26 | async-start | bytes 1310720 | tf_op jit(solution)/shard_map/all_gather | solution.py:365
  9.1 81.7 %all-gather.33.cloned.1.call-start = ((), (), s32[]{:S(2)}) async-start(), calls=%async_computation.27 | async-start | bytes 1310720 | tf_op jit(solution)/shard_map/all_gather | solution.py:366
  26.3 38.1 %all-to-all-start = ((bf16[8,64,1024]{2,1,0:T(8,128)(2,1)}), bf16[8,64,1024]{2,1,0:T(8,128)(2,1)S(1)}, u32[]{:S(2)}, u32[]{:S(2)}) async-start(bf16[8,64,1024]{2,1,0:T(8,128)(2,1)} %bitcast.293), calls=%async_computation | async-start | bytes 2097152 | tf_op jit(solution)/shard_map/all_to_all | solution.py:303
  29.9 119.5 %all-gather.21.cloned.1.call-start = ((), (), s32[]{:S(2)}) async-start(), calls=%async_computation.15 | async-start | bytes 1966080 | tf_op jit(solution)/shard_map/all_gather | solution.py:331
  31.3 168.9 %all-gather.19.cloned.1.call-start = ((), (), s32[]{:S(2)}) async-start(), calls=%async_computation.14 | async-start | bytes 9437184 | tf_op jit(solution)/shard_map/all_gather | solution.py:356
  70.2 222.4 %all-gather.29.cloned.1.call-start = ((), (), s32[]{:S(2)}) async-start(), calls=%async_computation.25 | async-start | bytes 2359296 | tf_op jit(solution)/shard_map/all_gather | solution.py:374
  87.6 227.7 %all-gather.23.cloned.1.call-start = ((), (), s32[]{:S(2)}) async-start(), calls=%async_computation.16 | async-start | bytes 9437184 | tf_op jit(solution)/shard_map/all_gather | solution.py:383
  90.8 254.9 %all-gather.35.cloned.1.call-start = ((), (), s32[]{:S(2)}) async-start(), calls=%async_computation.28 | async-start | bytes 9437184 | tf_op jit(solution)/shard_map/all_gather | solution.py:384
  91.5 192.0 %all-to-all-start.4 = ((bf16[8,64,1024]{2,1,0:T(8,128)(2,1)}), bf16[8,64,1024]{2,1,0:T(8,128)(2,1)}, u32[]{:S(2)}, u32[]{:S(2)}) async-start(bf16[8,64,1024]{2,1,0:T(8,128)(2,1)} %bitcast.44), calls=%async_computation.4 | async-start | bytes 2097152 | tf_op jit(solution)/shard_map/all_to_all | solution.py:303
  150.6 58.8 %copy-start.13 = (bf16[3,2,64,1024]{3,2,1,0:T(8,128)(2,1)}, bf16[3,2,64,1024]{3,2,1,0:T(8,128)(2,1)S(1)}, u32[]{:S(2)}) copy-start(bf16[3,2,64,1024]{3,2,1,0:T(8,128)(2,1)S(1)} %copy.242) | copy-start | bytes 2359300
  283.6 21.7 %all-to-all-start.2 = ((bf16[8,512,128]{1,2,0:T(8,128)(2,1)}), bf16[8,512,128]{1,2,0:T(8,128)(2,1)}, u32[]{:S(2)}, u32[]{:S(2)}) async-start(bf16[8,512,128]{1,2,0:T(8,128)(2,1)} %copy.246), calls=%async_computation.2 | async-start | bytes 2097152 | tf_op jit(solution)/shard_map/all_to_all | solution.py:443
  287.9 230.6 %reduce-scatter.15.cloned.1.call-start = ((), (), s32[]{:S(2)}) async-start(), calls=%async_computation.22 | async-start | bytes 2654208 | tf_op jit(solution)/shard_map/reduce_scatter | solution.py:510
  389.8 130.2 %reduce-scatter.13.cloned.1.call-start = ((), (), s32[]{:S(2)}) async-start(), calls=%async_computation.21 | async-start | bytes 9437184 | tf_op jit(solution)/shard_map/reduce_scatter | solution.py:474
  400.6 187.6 %reduce-scatter.11.cloned.1.call-start = ((), (), s32[]{:S(2)}) async-start(), calls=%async_computation.20 | async-start | bytes 9437184 | tf_op jit(solution)/shard_map/reduce_scatter | solution.py:468
  416.2 22.8 %all-to-all-start.5 = ((bf16[512,8,128]{2,0,1:T(8,128)(2,1)}), bf16[512,8,128]{2,0,1:T(8,128)(2,1)}, u32[]{:S(2)}, u32[]{:S(2)}) async-start(bf16[512,8,128]{2,0,1:T(8,128)(2,1)} %bitcast.277), calls=%async_computation.5 | async-start | bytes 2097152 | tf_op jit(solution)/shard_map/all_to_all | solution.py:484
  420.5 208.1 %reduce-scatter.9.cloned.1.call-start = ((), (), s32[]{:S(2)}) async-start(), calls=%async_computation.18 | async-start | bytes 2129920 | tf_op jit(solution)/shard_map/reduce_scatter | solution.py:595
  518.4 162.2 %reduce-scatter.17.cloned.1.call-start = ((), (), s32[]{:S(2)}) async-start(), calls=%async_computation.23 | async-start | bytes 3112960 | tf_op jit(solution)/shard_map/reduce_scatter | solution.py:537
  521.8 66.5 %slice-start = ((bf16[144,1024]{1,0:T(8,128)(2,1)}), bf16[128,1024]{1,0:T(8,128)(2,1)S(1)}, s32[]{:S(2)}) async-start(bf16[144,1024]{1,0:T(8,128)(2,1)} %reduce-scatter.15.cloned.1.call-done), calls=%async_computation.29 | async-start | bytes 524288 | tf_op jit(solution)/shard_map/slice | solution.py:533
  590.8 164.5 %reduce-scatter.7.cloned.1.call-start = ((), (), s32[]{:S(2)}) async-start(), calls=%async_computation.17 | async-start | bytes 9437184 | tf_op jit(solution)/shard_map/reduce_scatter | solution.py:571
  600.7 80.0 %copy-start.26 = (f32[2,4,64]{2,1,0:T(4,128)S(1)}, f32[2,4,64]{2,1,0:T(4,128)}, u32[]{:S(2)}) copy-start(f32[2,4,64]{2,1,0:T(4,128)} %copy-done.25) | copy-start | bytes 6148
  600.7 80.1 %copy-start.22 = (f32[2,4,64]{2,1,0:T(4,128)S(1)}, f32[2,4,64]{2,1,0:T(4,128)}, u32[]{:S(2)}) copy-start(f32[2,4,64]{2,1,0:T(4,128)} %copy-done.21) | copy-start | bytes 6148
  600.7 80.1 %copy-start.12 = (bf16[2,256,1024]{2,1,0:T(8,128)(2,1)S(1)}, bf16[2,256,1024]{2,1,0:T(8,128)(2,1)}, u32[]{:S(2)}) copy-start(bf16[2,256,1024]{2,1,0:T(8,128)(2,1)} %get-tuple-element.118) | copy-start | bytes 3145732
  600.7 191.5 %all-gather.25.cloned.1.call-start = ((), (), s32[]{:S(2)}) async-start(), calls=%async_computation.19 | async-start | bytes 3833856 | tf_op jit(solution)/shard_map/all_gather | solution.py:596
  628.6 204.3 %all-gather.27.cloned.1.call-start = ((), (), s32[]{:S(2)}) async-start(), calls=%async_computation.24 | async-start | bytes 5603328 | tf_op jit(solution)/shard_map/all_gather | solution.py:540
  680.8 74.6 %copy-start.20 = (f32[2,1024]{1,0:T(2,128)S(1)}, f32[2,1024]{1,0:T(2,128)}, u32[]{:S(2)}) copy-start(f32[2,1024]{1,0:T(2,128)} %copy-done.19) | copy-start | bytes 24580
  680.8 74.6 %copy-start.28 = (f32[512]{0:T(512)S(1)}, f32[512]{0:T(512)}, u32[]{:S(2)}) copy-start(f32[512]{0:T(512)} %copy-done.27) | copy-start | bytes 6148
  680.8 74.6 %copy-start.30 = (f32[512]{0:T(512)S(1)}, f32[512]{0:T(512)}, u32[]{:S(2)}) copy-start(f32[512]{0:T(512)} %copy-done.29) | copy-start | bytes 6148
  682.9 81.7 %all-to-all-start.3 = ((bf16[2,256,1024]{2,0,1:T(2,128)(2,1)}), bf16[2,256,1024]{2,0,1:T(2,128)(2,1)}, u32[]{:S(2)}, u32[]{:S(2)}) async-start(bf16[2,256,1024]{2,0,1:T(2,128)(2,1)} %copy.251), calls=%async_computation.3 | async-start | bytes 2097152 | tf_op jit(solution)/shard_map/all_to_all | solution.py:312
  687.2 70.9 %copy-start.8 = (f32[2,256,1024]{2,1,0:T(8,128)S(1)}, f32[2,256,1024]{2,1,0:T(8,128)}, u32[]{:S(2)}) copy-start(f32[2,256,1024]{2,1,0:T(8,128)} %get-tuple-element.139) | copy-start | bytes 6291460
  687.2 70.9 %copy-start.24 = (f32[1024]{0:T(1024)S(1)}, f32[1024]{0:T(1024)}, u32[]{:S(2)}) copy-start(f32[1024]{0:T(1024)} %copy-done.23) | copy-start | bytes 12292
  764.6 10.5 %all-to-all-start.7 = ((f32[4,1,3072]{2,1,0:T(1,128)}), f32[4,1,3072]{2,1,0:T(1,128)S(1)}, u32[]{:S(2)}, u32[]{:S(2)}) async-start(f32[4,1,3072]{2,1,0:T(1,128)} %reshape.512), calls=%async_computation.8 | async-start | bytes 98304 | tf_op jit(solution)/shard_map/all_to_all | solution.py:630
  775.1 44.1 %all-to-all-start.6 = ((bf16[2,256,1024]{2,0,1:T(2,128)(2,1)}), bf16[2,256,1024]{2,0,1:T(2,128)(2,1)}, u32[]{:S(2)}, u32[]{:S(2)}) async-start(bf16[2,256,1024]{2,0,1:T(2,128)(2,1)} %copy.258), calls=%async_computation.7 | async-start | bytes 2097152 | tf_op jit(solution)/shard_map/all_to_all | solution.py:312
  (32 other events, 256.7 us)
Sparse Core Ops, SparseCore 0:
  10.2 42.5 all-gather.30
  54.9 30.4 all-gather.32
  87.6 56.7 all-gather.20
  146.7 53.4 all-gather.18
  201.9 27.9 all-gather.28
  232.2 56.0 all-gather.22
  290.1 55.5 all-gather.34
  389.9 46.3 reduce-scatter.14
  440.2 73.4 reduce-scatter.12
  516.9 71.2 reduce-scatter.10
  591.2 37.3 reduce-scatter.8
  631.4 49.1 reduce-scatter.16
  684.5 70.8 reduce-scatter.6
  757.1 33.4 all-gather.24
  792.3 40.5 all-gather.26

commit v2 on v1

v2 whole, which is shorter than its diff:
```python
from functools import partial
import math

import jax
import jax.numpy as jnp
from jax import lax
from jax.experimental import pallas as pl
from jax.experimental.pallas import tpu as pltpu
from jax.sharding import PartitionSpec as P

HD = 64
f32 = jnp.float32
bf16 = jnp.bfloat16
score_scale = HD ** (-0.5)


def noise_embedding(noise_steps, model_width):
    half_width = model_width // 2
    frequency = jnp.exp(-math.log(10000.0) * jnp.arange(half_width, dtype=f32) / half_width)
    angles = noise_steps.astype(f32)[..., None] * frequency
    return jnp.concatenate([jnp.cos(angles), jnp.sin(angles)], axis=-1)


def noise_activation(noise_steps, model_width):
    return jax.nn.silu(noise_embedding(noise_steps, model_width)).astype(bf16)


def layer_norm(values):
    centred = values - jnp.mean(values, axis=-1, keepdims=True)
    inverse = lax.rsqrt(jnp.mean(centred * centred, axis=-1, keepdims=True) + 1e-06)
    return (centred * inverse, inverse)


def norm_back(grad_normed, normed, inverse):
    return inverse * (
        grad_normed
        - jnp.mean(grad_normed, axis=-1, keepdims=True)
        - normed * jnp.mean(grad_normed * normed, axis=-1, keepdims=True)
    )


def dot(left, right):
    return lax.dot_general(left, right, (((1,), (0,)), ((), ())), preferred_element_type=f32)


def dot_nt(left, right):
    return lax.dot_general(left, right, (((1,), (1,)), ((), ())), preferred_element_type=f32)


def dot_tn(left, right):
    return lax.dot_general(left, right, (((0,), (0,)), ((), ())), preferred_element_type=f32)


GROUP = 4


def head_blocks(transposed, head_count):
    rows = lax.broadcasted_iota(jnp.int32, transposed.shape, 0) // HD
    return jnp.concatenate(
        [jnp.where(rows == head, transposed, 0.0) for head in range(head_count)], axis=1
    ).astype(bf16)


def head_rows(natural, head_count):
    lanes = lax.broadcasted_iota(jnp.int32, natural.shape, 1) // HD
    return jnp.concatenate(
        [jnp.where(lanes == head, natural, 0.0) for head in range(head_count)], axis=0
    ).astype(bf16)


def over_key_frames(key_stop, step, carry):
    done = 0
    size = 1
    while size < GROUP:
        once = (key_stop // size) % 2
        carry = lax.fori_loop(
            0, once, lambda _, c, first=done, size=size: step(first, size, c), carry
        )
        done = done + once * size
        size *= 2
    return lax.fori_loop(
        0, key_stop // GROUP, lambda n, c: step(done + GROUP * n, GROUP, c), carry
    )


def attend_kernel(frame_ids, q_ref, k_ref, vt_ref, *refs, head_count, patch_count, first):
    out_ref, lse_ref = refs[-2:]
    key_stop = frame_ids[pl.program_id(0) + first] + 1
    q_cols = head_blocks(jnp.swapaxes(q_ref[...].astype(f32), 0, 1) * score_scale, head_count)
    width = head_count * patch_count

    def step(first, frames, carry):
        row_max, row_total, sums = carry
        start = pl.multiple_of(first * patch_count, patch_count)
        scores = dot(k_ref[pl.ds(start, frames * patch_count), :], q_cols)
        new_max = jnp.maximum(row_max, jnp.max(scores, axis=0, keepdims=True))
        rescale = jnp.exp(row_max - new_max)
        weights = jnp.exp(scores - new_max)
        row_total = row_total * rescale + jnp.sum(weights, axis=0, keepdims=True)
        weights = weights.astype(bf16)
        values_t = vt_ref[:, pl.ds(start, frames * patch_count)]
        parts = []
        for head in range(head_count):
            cols = slice(head * patch_count, (head + 1) * patch_count)
            rows = slice(head * HD, (head + 1) * HD)
            parts.append(sums[head] * rescale[:, cols] + dot(values_t[rows], weights[:, cols]))
        return (new_max, row_total, tuple(parts))

    row_max, row_total, sums = over_key_frames(
        key_stop,
        step,
        (
            jnp.full((1, width), -1e30, f32),
            jnp.zeros((1, width), f32),
            tuple(jnp.zeros((HD, patch_count), f32) for _ in range(head_count)),
        ),
    )
    inverse = 1.0 / row_total
    out_t = jnp.concatenate(
        [
            sums[head] * inverse[:, head * patch_count : (head + 1) * patch_count]
            for head in range(head_count)
        ],
        axis=0,
    )
    out_ref[...] = jnp.swapaxes(out_t, 0, 1).astype(bf16)
    lse_ref[0] = row_max + jnp.log(row_total)


def pair_count(frame_total, first, steps):
    return steps * (frame_total * (2 * first + steps) // (2 * (first + steps)) + 1) // 2


def attend(queries, keys, values_t, frame_ids, head_count, patch_count, first, last, waits):
    lanes = queries.shape[1]
    key_rows = keys.shape[0]
    steps = last - first
    row_count = steps * patch_count
    width = head_count * patch_count
    work = pair_count(key_rows // patch_count, first, steps) * patch_count * width
    return pl.pallas_call(
        partial(
            attend_kernel, head_count=head_count, patch_count=patch_count, first=first
        ),
        grid_spec=pltpu.PrefetchScalarGridSpec(
            num_scalar_prefetch=1,
            grid=(steps,),
            in_specs=[
                pl.BlockSpec((patch_count, lanes), lambda j, ids: (j + first, 0)),
                pl.BlockSpec((key_rows, lanes), lambda j, ids: (0, 0)),
                pl.BlockSpec((lanes, key_rows), lambda j, ids: (0, 0)),
            ]
            + [pl.BlockSpec(memory_space=pl.ANY) for _ in waits],
            out_specs=[
                pl.BlockSpec((patch_count, lanes), lambda j, ids: (j, 0)),
                pl.BlockSpec((1, 1, width), lambda j, ids: (j, 0, 0)),
            ],
        ),
        out_shape=[
            jax.ShapeDtypeStruct((row_count, lanes), bf16),
            jax.ShapeDtypeStruct((steps, 1, width), f32),
        ],
        compiler_params=pltpu.CompilerParams(vmem_limit_bytes=40 << 20),
        cost_estimate=pl.CostEstimate(
            flops=work * 1024, bytes_accessed=8 * row_count * lanes, transcendentals=work
        ),
        name="attend",
    )(frame_ids, queries, keys, values_t, *waits)


def attend_back_kernel(
    frame_ids,
    q_ref,
    grad_ref,
    out_ref,
    lse_ref,
    k_ref,
    v_ref,
    kt_ref,
    *refs,
    head_count,
    patch_count,
    first,
    has_start,
):
    dq_ref, dk_ref, dv_ref, dk_sum, dv_sum = refs[-5:]
    position = pl.program_id(0)
    key_stop = frame_ids[position + first] + 1

    @pl.when(position == 0)
    def _():
        dk_sum[...] = refs[0][...] if has_start else jnp.zeros_like(dk_sum)
        dv_sum[...] = refs[1][...] if has_start else jnp.zeros_like(dv_sum)

    q_rows = q_ref[...].astype(f32) * score_scale
    grad_rows = grad_ref[...].astype(f32)
    grad_t = jnp.swapaxes(grad_rows, 0, 1)
    grad_out_t = grad_t * jnp.swapaxes(out_ref[...].astype(f32), 0, 1)
    delta = jnp.concatenate(
        [
            jnp.sum(grad_out_t[head * HD : (head + 1) * HD], axis=0, keepdims=True)
            for head in range(head_count)
        ],
        axis=1,
    )
    q_cols = head_blocks(jnp.swapaxes(q_rows, 0, 1), head_count)
    grad_cols = head_blocks(grad_t, head_count)
    q_stack = head_rows(q_rows, head_count)
    grad_stack = head_rows(grad_rows, head_count)
    lse = lse_ref[0]

    def step(first, frames, sums):
        start = pl.multiple_of(first * patch_count, patch_count)
        here = pl.ds(start, frames * patch_count)
        scores = dot(k_ref[here, :], q_cols)
        grad_probs = dot(v_ref[here, :], grad_cols)
        probs = jnp.exp(scores - lse)
        grad_scores = (probs * (grad_probs - delta)).astype(bf16)
        dv_sum[here, :] += dot(probs.astype(bf16), grad_stack)
        dk_sum[here, :] += dot(grad_scores, q_stack)
        keys_t = kt_ref[:, here]
        return tuple(
            sums[head]
            + dot(
                keys_t[head * HD : (head + 1) * HD],
                grad_scores[:, head * patch_count : (head + 1) * patch_count],
            )
            for head in range(head_count)
        )

    sums = over_key_frames(
        key_stop, step, tuple(jnp.zeros((HD, patch_count), f32) for _ in range(head_count))
    )
    dq_t = jnp.concatenate(sums, axis=0) * score_scale
    dq_ref[...] = jnp.swapaxes(dq_t, 0, 1).astype(bf16)

    @pl.when(position == pl.num_programs(0) - 1)
    def _():
        dk_ref[...] = dk_sum[...].astype(dk_ref.dtype)
        dv_ref[...] = dv_sum[...].astype(dv_ref.dtype)


def attend_back(
    queries, keys, values, keys_t, out, lse, grad, frame_ids, head_count, patch_count, first, last, start, sum_type, waits
):
    lanes = queries.shape[1]
    key_rows = keys.shape[0]
    steps = last - first
    row_count = steps * patch_count
    width = head_count * patch_count
    work = pair_count(key_rows // patch_count, first, steps) * patch_count * width
    block = pl.BlockSpec((patch_count, lanes), lambda j, ids: (j + first, 0))
    whole = pl.BlockSpec((key_rows, lanes), lambda j, ids: (0, 0))
    return pl.pallas_call(
        partial(
            attend_back_kernel,
            head_count=head_count,
            patch_count=patch_count,
            first=first,
            has_start=len(start) > 0,
        ),
        grid_spec=pltpu.PrefetchScalarGridSpec(
            num_scalar_prefetch=1,
            grid=(steps,),
            in_specs=[
                block,
                block,
                block,
                pl.BlockSpec((1, 1, width), lambda j, ids: (j + first, 0, 0)),
                whole,
                whole,
                pl.BlockSpec((lanes, key_rows), lambda j, ids: (0, 0)),
            ]
            + [whole for _ in start]
            + [pl.BlockSpec(memory_space=pl.ANY) for _ in waits],
            out_specs=[
                pl.BlockSpec((patch_count, lanes), lambda j, ids: (j, 0)),
                whole,
                whole,
            ],
            scratch_shapes=[
                pltpu.VMEM((key_rows, lanes), f32),
                pltpu.VMEM((key_rows, lanes), f32),
            ],
        ),
        out_shape=[
            jax.ShapeDtypeStruct((row_count, lanes), bf16),
            jax.ShapeDtypeStruct((key_rows, lanes), sum_type),
            jax.ShapeDtypeStruct((key_rows, lanes), sum_type),
        ],
        compiler_params=pltpu.CompilerParams(vmem_limit_bytes=48 << 20),
        cost_estimate=pl.CostEstimate(
            flops=work * 2560, bytes_accessed=16 * row_count * lanes, transcendentals=work
        ),
        name="attend_back",
    )(frame_ids, queries, grad, out, lse, keys, values, keys_t, *start, *waits)


def mlp_kernel(
    core_ref,
    hidden_ref,
    grad_ref,
    bias_ref,
    bias_other_ref,
    up_ref,
    up_other_ref,
    down_ref,
    down_other_ref,
    branch_ref,
    back_ref,
    keep_ref,
    send_ref,
    keep_bias_ref,
    send_bias_ref,
    hidden_t,
    grad_t,
):
    step = pl.program_id(0)
    rows, width = hidden_ref.shape

    @pl.when(step == 0)
    def _():
        branch_ref[...] = jnp.zeros_like(branch_ref)
        back_ref[...] = jnp.zeros_like(back_ref)
        for start in range(0, width, 256):
            cols = slice(start, start + 256)
            hidden_t[cols, :] = jnp.swapaxes(hidden_ref[:, cols].astype(f32), 0, 1).astype(bf16)
            grad_t[cols, :] = jnp.swapaxes(grad_ref[:, cols].astype(f32), 0, 1).astype(bf16)

    slope = math.sqrt(2.0 / math.pi)
    for up, down, bias, out_ref, out_bias_ref in (
        (up_other_ref, down_other_ref, bias_other_ref, send_ref, send_bias_ref),
        (up_ref, down_ref, bias_ref, keep_ref, keep_bias_ref),
    ):
        shards, part = up.shape[1], up.shape[2]
        units = shards * part
        up_rows = up[0].reshape(units, width)
        down_rows = down[0].reshape(units, width)
        pre = dot(up_rows, hidden_t[...]) + bias[0]
        square = pre * pre
        bend = jnp.tanh(slope * pre * (1.0 + 0.044715 * square))
        activated = (0.5 * pre * (1.0 + bend)).astype(bf16)
        gain = 0.5 * (1.0 + bend) + (0.5 * slope) * pre * (1.0 - bend * bend) * (
            1.0 + (3 * 0.044715) * square
        )
        grad_pre = (dot(down_rows, grad_t[...]) * gain).astype(bf16)
        out_bias_ref[0] = jnp.sum(grad_pre.astype(f32), axis=1, keepdims=True)
        out_ref[0, :, :part, :] = (
            dot(grad_pre, hidden_ref[...]).astype(bf16).reshape(shards, part, width)
        )
        out_ref[0, :, part:, :] = (
            dot(activated, grad_ref[...]).astype(bf16).reshape(shards, part, width)
        )
        branch_ref[...] += dot_tn(activated, down_rows)
        back_ref[...] += dot_tn(grad_pre, up_rows)


def mlp(core, hidden, grad, bias, weights, part):
    frame_parts, shards, _, width = weights.shape
    rows = hidden.shape[0]
    steps = frame_parts // 2
    units = shards * part

    def own(m, c):
        return 2 * m + c[0]

    def other(m, c):
        return 2 * m + 1 - c[0]

    def weight_spec(which, row):
        return pl.BlockSpec((1, shards, part, width), lambda m, c: (which(m, c), 0, row, 0))

    whole = pl.BlockSpec((rows, width), lambda m, c: (0, 0), pipeline_mode=pl.Buffered(1))
    sums = pl.BlockSpec((rows, width), lambda m, c: (0, 0))
    out = pl.BlockSpec((1, shards, 2 * part, width), lambda m, c: (m, 0, 0, 0))
    column = pl.BlockSpec((1, units, 1), lambda m, c: (m, 0, 0))
    work = rows * width * units * frame_parts
    return pl.pallas_call(
        mlp_kernel,
        grid_spec=pltpu.PrefetchScalarGridSpec(
            num_scalar_prefetch=1,
            grid=(steps,),
            in_specs=[
                whole,
                whole,
                pl.BlockSpec((1, units, 1), lambda m, c: (own(m, c), 0, 0)),
                pl.BlockSpec((1, units, 1), lambda m, c: (other(m, c), 0, 0)),
                weight_spec(own, 0),
                weight_spec(other, 0),
                weight_spec(own, 1),
                weight_spec(other, 1),
            ],
            out_specs=[sums, sums, out, out, column, column],
            scratch_shapes=[pltpu.VMEM((width, rows), bf16), pltpu.VMEM((width, rows), bf16)],
        ),
        out_shape=[
            jax.ShapeDtypeStruct((rows, width), f32),
            jax.ShapeDtypeStruct((rows, width), f32),
            jax.ShapeDtypeStruct((steps, shards, 2 * part, width), bf16),
            jax.ShapeDtypeStruct((steps, shards, 2 * part, width), bf16),
            jax.ShapeDtypeStruct((steps, units, 1), f32),
            jax.ShapeDtypeStruct((steps, units, 1), f32),
        ],
        compiler_params=pltpu.CompilerParams(vmem_limit_bytes=48 << 20),
        cost_estimate=pl.CostEstimate(
            flops=12 * work,
            bytes_accessed=frame_parts * units * width * 8,
            transcendentals=rows * units * frame_parts,
        ),
        name="mlp",
    )(core, hidden, grad, bias, bias, weights, weights, weights, weights)


def after(value, *others):
    return lax.optimization_barrier((value,) + others)[0]


def on_device(
    tokens,
    noise_steps,
    ada_weight,
    ada_bias,
    qkv_weight,
    qv_bias,
    out_weight,
    out_bias,
    up_weight,
    up_bias,
    down_weight,
    down_bias,
    cotangent,
):
    clip_count, local_frames, local_patches, model_width = tokens.shape
    tensor_count = lax.axis_size("tensor")
    frame_devices = lax.axis_size("frame")
    frame_at = lax.axis_index("frame")
    tensor_at = lax.axis_index("tensor")
    patch_count = local_patches * tensor_count
    hidden_width = up_weight.shape[1] * tensor_count
    head_total = model_width // HD
    shard_heads = head_total // tensor_count
    head_count = head_total // frame_devices
    lanes = head_count * HD
    unit_total = clip_count * local_frames
    units = unit_total // tensor_count
    sharers = tensor_count // clip_count
    share_at = tensor_at % sharers
    own_rows = units * patch_count
    all_rows = frame_devices * own_rows
    slot = frame_at % shard_heads
    group_at = frame_at // shard_heads
    shard_groups = tensor_count // head_count
    shard_base = (tensor_at // sharers) * sharers
    core = frame_at % 2
    chips = frame_devices // 2
    unit_shape = (units, patch_count, model_width)
    column_part = model_width // tensor_count


    def swap_frame(values):
        return lax.all_to_all(values, "frame", split_axis=0, concat_axis=0, tiled=True)

    def shifted(values, shift):
        return lax.ppermute(
            values, "tensor", [(t, (t + shift) % tensor_count) for t in range(tensor_count)]
        )

    def tensor_parts(values):
        return [shifted(values, tensor_count - 1 - n) for n in range(tensor_count - 1)] + [values]

    def tensor_sum(parts):
        total = parts[-1].astype(f32)
        for n in range(tensor_count - 1):
            total = total + shifted(parts[n], n + 1).astype(f32)
        return total

    def exchange(parts):
        last = tensor_count - 1
        return [shifted(parts[last - 1 - n], last - n) for n in range(last)] + [parts[last]]

    def to_relative(values):
        return [
            lax.dynamic_index_in_dim(
                values, (tensor_at + 1 + n) % tensor_count, 0, keepdims=False
            )
            for n in range(tensor_count)
        ]

    def rolled(values, start):
        return lax.dynamic_slice_in_dim(
            jnp.concatenate([values, values]), start % tensor_count, tensor_count, axis=0
        )

    def from_relative(parts, first=0):
        return rolled(jnp.stack(parts), first - tensor_at - 1)

    def head_pairs(head, member):
        pairs = []
        for i in range(frame_devices):
            for t in range(member, tensor_count, sharers):
                shard = (t - member + i // shard_heads + head * shard_groups) % tensor_count
                pairs.append((i * tensor_count + shard, i * tensor_count + t))
        return pairs

    def from_owners(values, head):
        total = None
        for member in range(sharers):
            got = lax.ppermute(values, ("frame", "tensor"), head_pairs(head, member))
            total = got if total is None else total + got
        return total

    def to_owners(pieces):
        total = 0.0
        for head, piece in enumerate(pieces):
            for member in range(sharers):
                pairs = [(user, owner) for owner, user in head_pairs(head, member)]
                total = total + lax.ppermute(piece, ("frame", "tensor"), pairs).astype(f32)
        return total.astype(bf16)

    def to_units(values):
        parts = to_relative(
            values.reshape(tensor_count, units, local_patches, model_width)
        )
        return jnp.stack(exchange(parts), axis=1).reshape(units, patch_count, model_width)

    def from_units(values):
        parts = values.reshape(units, tensor_count, local_patches, model_width)
        return from_relative(exchange([parts[:, n] for n in range(tensor_count)])).reshape(
            clip_count, local_frames, local_patches, model_width
        )

    def core_sum(keep, send):
        got = lax.ppermute(send, "frame", [(i, i ^ 1) for i in range(frame_devices)])
        return keep + got

    def scatter(values):
        return lax.psum_scatter(
            values.reshape(-1, model_width),
            "frame",
            scatter_dimension=0,
            axis_index_groups=[list(range(c, frame_devices, 2)) for c in range(2)],
            tiled=True,
        ).reshape(values.shape[1:])

    def frame_parts(values):
        return (
            lax.all_gather(values.astype(bf16), "frame", axis=0, tiled=True)
            .reshape(frame_devices, -1, model_width)
            .astype(f32)
        )

    unit_tokens = to_units(tokens)
    act_noise = noise_activation(noise_steps, model_width).reshape(unit_total, model_width)
    mod_local = jnp.einsum(
        "ud,dkj->ukj", act_noise, ada_weight, preferred_element_type=f32
    ) + ada_bias.astype(f32)
    modulation = (
        from_relative(
            exchange(to_relative(mod_local.reshape(tensor_count, units * 6, column_part)))
        )
        .reshape(tensor_count, units, 6, column_part)
        .transpose(1, 2, 0, 3)
        .reshape(units, 6, model_width)
    )
    shift_one = modulation[:, None, 0]
    scale_one = modulation[:, None, 1]
    gate_one = modulation[:, None, 2]
    shift_two = modulation[:, None, 3]
    scale_two = modulation[:, None, 4]
    gate_two = modulation[:, None, 5]

    slot_weight = lax.dynamic_slice_in_dim(qkv_weight, slot * HD, HD, axis=2)
    slot_weight = slot_weight.transpose(1, 2, 0).reshape(3 * HD, model_width)
    slot_bias = lax.dynamic_slice_in_dim(qv_bias, slot * HD, HD, axis=1).reshape(1, 2 * HD)
    slot_bias = jnp.pad(slot_bias, ((0, 15), (0, model_width - 2 * HD)))
    slot_pack = jnp.concatenate([slot_weight, slot_bias])

    def own_part(values):
        size = values.shape[0] // frame_devices
        return lax.dynamic_slice_in_dim(values, frame_at * size, size, axis=0)

    hidden_part = hidden_width // (tensor_count * frame_devices)
    half = hidden_part // 2
    out_rows = out_weight.shape[0] // frame_devices
    up_part = lax.dynamic_slice_in_dim(
        up_weight, frame_at * hidden_part, hidden_part, axis=1
    ).transpose(1, 0)
    down_part = own_part(down_weight)
    bias_part = lax.dynamic_slice_in_dim(up_bias, frame_at * hidden_part, hidden_part, axis=0)
    bias_part = jnp.pad(bias_part[None, :], ((0, 15), (0, model_width - hidden_part)))
    first_pack = jnp.concatenate([up_part[:half], down_part[:half], bias_part])
    second_pack = jnp.concatenate([up_part[half:], down_part[half:]])
    out_pack = own_part(out_weight)
    slot_pack = after(slot_pack, unit_tokens)
    head_pack = jnp.stack([from_owners(slot_pack, head) for head in range(head_count)])
    first_list = tensor_parts(after(jnp.concatenate([first_pack, out_pack]), head_pack))
    out_at = first_pack.shape[0]
    first_parts = jnp.concatenate(
        [
            from_relative([part[:out_at] for part in first_list]),
            from_relative([part[out_at:] for part in first_list], shard_base),
        ],
        axis=1,
    ).reshape(-1, model_width)
    head_weight = (
        head_pack[:, : 3 * HD]
        .reshape(head_count, 3, HD, model_width)
        .transpose(1, 0, 2, 3)
        .reshape(3 * lanes, model_width)
    )
    head_bias = head_pack[:, 3 * HD, : 2 * HD]
    head_bias = head_bias.reshape(head_count, 2, HD).transpose(1, 0, 2).reshape(2, lanes)
    head_bias = head_bias.astype(f32)
    qkv_bias = jnp.concatenate([head_bias[0], jnp.zeros((lanes,), f32), head_bias[1]])

    token_values = unit_tokens.astype(f32)
    normed_one, inverse_one = layer_norm(token_values)
    hidden_one = (normed_one * (1.0 + scale_one) + shift_one).astype(bf16)
    hidden_all = lax.all_gather(
        hidden_one.reshape(own_rows, model_width), "frame", axis=0, tiled=True
    )

    first_all = lax.all_gather(first_parts, "frame", axis=0, tiled=True)
    first_all = first_all.reshape(frame_devices, tensor_count, -1, model_width)
    up_bias_all = first_all[:, :, 2 * half, :hidden_part].astype(f32)
    first_bias = up_bias_all[:, :, :half].reshape(frame_devices, tensor_count * half, 1)
    second_bias = up_bias_all[:, :, half:].reshape(frame_devices, tensor_count * half, 1)
    head_parts = HD // out_rows
    out_full = (
        first_all[:, :, 2 * half + 16 :]
        .reshape(shard_heads, head_parts, head_count, shard_groups, out_rows, model_width)
        .transpose(3, 0, 2, 1, 4, 5)
        .reshape(model_width, model_width)
    )

    projected = (dot_nt(hidden_all, head_weight) + qkv_bias).astype(bf16)
    queries = projected[:, :lanes]
    keys = projected[:, lanes : 2 * lanes]
    values = projected[:, 2 * lanes :]

    def share(mine):
        if sharers == 1:
            return mine
        pieces = [mine]
        for shift in range(1, sharers):
            perm = [
                (t, (t // sharers) * sharers + (t + shift) % sharers) for t in range(tensor_count)
            ]
            pieces.append(lax.ppermute(mine, "tensor", perm))
        stacked = jnp.stack(pieces)
        stacked = jnp.stack(
            [
                lax.dynamic_index_in_dim(
                    stacked, (share_at - member) % sharers, 0, keepdims=False
                )
                for member in range(sharers)
            ]
        )
        return (
            stacked.reshape(sharers, frame_devices, own_rows, lanes)
            .transpose(1, 0, 2, 3)
            .reshape(sharers * all_rows, lanes)
        )

    def unshare(partial_sums):
        if sharers == 1:
            return partial_sums
        pieces = (
            partial_sums.reshape(frame_devices, sharers, own_rows, lanes)
            .transpose(1, 0, 2, 3)
            .reshape(sharers, all_rows, lanes)
        )
        total = lax.dynamic_index_in_dim(pieces, share_at, 0, keepdims=False).astype(f32)
        for shift in range(1, sharers):
            perm = [
                (t, (t // sharers) * sharers + (t + shift) % sharers) for t in range(tensor_count)
            ]
            piece = lax.dynamic_index_in_dim(
                pieces, (share_at + shift) % sharers, 0, keepdims=False
            )
            total = total + lax.ppermute(piece, "tensor", perm).astype(f32)
        return total.astype(bf16)

    keys_all = share(keys)
    values_all = share(values)
    unit_ids = jnp.arange(frame_devices * units, dtype=jnp.int32)
    frame_ids = (
        (unit_ids // units) * local_frames + share_at.astype(jnp.int32) * units + unit_ids % units
    )
    values_t = values_all.T
    steps = all_rows // patch_count
    second_list = tensor_parts(after(second_pack, queries))
    cut = steps * 11 // 16
    heads_a, lse_a = attend(
        queries, keys_all, values_t, frame_ids, head_count, patch_count, 0, cut, ()
    )
    heads_a, *second_list = lax.optimization_barrier((heads_a, *second_list))
    second_parts = from_relative(second_list)
    upstream = to_units(after(cotangent, second_parts)).astype(f32)
    heads_b, lse_b = attend(
        queries, keys_all, values_t, frame_ids, head_count, patch_count, cut, steps,
        (second_parts,),
    )
    attended_heads = jnp.concatenate([heads_a, heads_b])
    row_lse = jnp.concatenate([lse_a, lse_b])
    second_all = lax.all_gather(
        second_parts.reshape(-1, model_width), "frame", axis=0, tiled=True
    ).reshape(frame_devices, tensor_count, -1, model_width)
    attended = (
        swap_frame(attended_heads.reshape(frame_devices, own_rows, lanes))
        .transpose(1, 0, 2)
        .reshape(own_rows, model_width)
    )

    grad_two = (gate_two * upstream).astype(bf16).reshape(own_rows, model_width)
    grad_down_bias = jnp.sum(grad_two.astype(f32), axis=0)

    branch_one = dot(attended, out_full).reshape(unit_shape) + out_bias.astype(f32)
    middle = token_values + gate_one * branch_one
    normed_two, inverse_two = layer_norm(middle)
    hidden_two = (normed_two * (1.0 + scale_two) + shift_two).astype(bf16)
    hidden_two = hidden_two.reshape(own_rows, model_width)

    core_id = core.astype(jnp.int32).reshape(1)
    branch_a, back_a, keep_a, send_a, keep_bias_a, send_bias_a = mlp(
        core_id, hidden_two, grad_two, first_bias, first_all, half
    )
    first_half = core_sum(keep_a, send_a)
    branch_b, back_b, keep_b, send_b, keep_bias_b, send_bias_b = mlp(
        core_id, hidden_two, grad_two, second_bias, second_all, half
    )
    second_half = core_sum(keep_b, send_b)
    back_b, first_half = lax.optimization_barrier((back_b, first_half))
    first_sum = scatter(first_half)
    branch_two = (branch_a + branch_b).reshape(unit_shape) + down_bias.astype(f32)
    result = from_units((middle + gate_two * branch_two).astype(bf16))
    grad_gate_two = jnp.sum(upstream * branch_two, axis=1)
    grad_hidden_two = (back_a + back_b).reshape(unit_shape)
    grad_scale_two = jnp.sum(grad_hidden_two * normed_two, axis=1)
    grad_shift_two = jnp.sum(grad_hidden_two, axis=1)
    grad_middle = upstream + norm_back(grad_hidden_two * (1.0 + scale_two), normed_two, inverse_two)
    grad_branch_one = (gate_one * grad_middle).astype(bf16)
    grad_gate_one = jnp.sum(grad_middle * branch_one, axis=1)
    grad_one = grad_branch_one.reshape(own_rows, model_width)
    grad_out_bias = jnp.sum(grad_one.astype(f32), axis=0)
    grad_attended = dot_nt(grad_one, out_full).astype(bf16)
    grad_heads = swap_frame(
        grad_attended.reshape(own_rows, frame_devices, lanes).transpose(1, 0, 2)
    ).reshape(all_rows, lanes)

    grad_out = (
        dot_tn(attended, grad_one)
        .astype(bf16)
        .reshape(shard_groups, shard_heads, head_count, head_parts, out_rows, model_width)
        .transpose(2, 0, 1, 3, 4, 5)
        .reshape(tensor_count, frame_devices, out_rows, model_width)
    )
    grad_out = rolled(grad_out, -shard_base).transpose(1, 0, 2, 3)
    width_part = model_width // frame_devices

    def by_core(keep_part, send_part):
        pair = jnp.stack([keep_part, send_part], axis=1)
        return jnp.where(core == 0, pair, pair[:, ::-1]).reshape(
            (frame_devices,) + keep_part.shape[1:]
        )

    grad_up_bias = jnp.concatenate(
        [
            by_core(keep_bias_a, send_bias_a).reshape(frame_devices, tensor_count, half),
            by_core(keep_bias_b, send_bias_b).reshape(frame_devices, tensor_count, half),
        ],
        axis=2,
    )
    once = jnp.concatenate(
        [
            grad_down_bias.reshape(frame_devices, 1, width_part),
            grad_out_bias.reshape(frame_devices, 1, width_part),
        ],
        axis=2,
    )
    bias_row = jnp.concatenate(
        [jnp.broadcast_to(once, (frame_devices, tensor_count, 2 * width_part)), grad_up_bias],
        axis=2,
    ).astype(bf16)
    bias_row = jnp.pad(
        bias_row[:, :, None, :], ((0, 0), (0, 0), (0, 15), (0, model_width - bias_row.shape[2]))
    )
    out_pairs = jnp.concatenate([grad_out, bias_row], axis=2).reshape(
        chips, 2, tensor_count, out_rows + 16, model_width
    )
    out_half = core_sum(
        lax.dynamic_index_in_dim(out_pairs, core, 1, keepdims=False),
        lax.dynamic_index_in_dim(out_pairs, 1 - core, 1, keepdims=False),
    )
    late_half = jnp.concatenate([second_half, out_half], axis=2)
    late_sum = scatter(late_half)
    first_total = tensor_sum(to_relative(first_sum)).astype(bf16)

    keys_t = keys_all.T
    grad_q_a, *sums = attend_back(
        queries, keys_all, values_all, keys_t, attended_heads, row_lse, grad_heads,
        frame_ids, head_count, patch_count, 0, cut, (), f32, (late_half, result),
    )
    grad_q_b, grad_k_all, grad_v_all = attend_back(
        queries, keys_all, values_all, keys_t, attended_heads, row_lse, grad_heads,
        frame_ids, head_count, patch_count, cut, steps, tuple(sums), bf16, (first_total,),
    )
    grad_q = jnp.concatenate([grad_q_a, grad_q_b])
    grad_k = unshare(grad_k_all)
    grad_v = unshare(grad_v_all)
    grad_projected = jnp.concatenate([grad_q, grad_k, grad_v], axis=1)
    grad_hidden_part = dot(grad_projected, head_weight).astype(bf16)
    grad_hidden_one = lax.psum_scatter(grad_hidden_part, "frame", scatter_dimension=0, tiled=True)
    grad_hidden_one = grad_hidden_one.astype(f32).reshape(unit_shape)

    late_total = tensor_sum(to_relative(late_sum)).astype(bf16)
    grad_head_weight = dot_tn(after(grad_projected, grad_hidden_part), hidden_all).astype(bf16)
    grad_slots = (
        grad_head_weight.reshape(3, head_count, HD, model_width)
        .transpose(1, 0, 2, 3)
        .reshape(head_count, 3 * HD, model_width)
    )
    grad_head_bias = jnp.stack(
        [jnp.sum(grad_q.astype(f32), axis=0), jnp.sum(grad_v.astype(f32), axis=0)]
    ).astype(bf16)
    grad_head_bias = grad_head_bias.reshape(2, head_count, HD).transpose(1, 0, 2)
    grad_head_bias = jnp.pad(
        grad_head_bias.reshape(head_count, 1, 2 * HD),
        ((0, 0), (0, 15), (0, model_width - 2 * HD)),
    )
    grad_slots = jnp.concatenate([grad_slots, grad_head_bias], axis=1)

    slots_total = to_owners([grad_slots[head] for head in range(head_count)])

    grad_scale_one = jnp.sum(grad_hidden_one * normed_one, axis=1)
    grad_shift_one = jnp.sum(grad_hidden_one, axis=1)
    grad_tokens = (
        grad_middle
        + norm_back(grad_hidden_one * (1.0 + scale_one), normed_one, inverse_one)
    ).astype(bf16)
    tail_sums, grad_tokens = lax.optimization_barrier(
        (jnp.concatenate([first_total, late_total]), grad_tokens)
    )
    tail_all = frame_parts(tail_sums)
    slots_sum = frame_parts(slots_total)
    late_tail = tail_all[:, 2 * half :]
    first_tail = tail_all[:, : 2 * half]
    up_first, down_first = first_tail[:, :half], first_tail[:, half:]
    up_second, down_second = late_tail[:, :half], late_tail[:, half : 2 * half]
    tail_out = late_tail[:, 2 * half : 2 * half + out_rows]
    tail_bias = late_tail[:, 2 * half + out_rows :]
    final_up = (
        jnp.concatenate([up_first, up_second], axis=1)
        .reshape(frame_devices * hidden_part, model_width)
        .transpose(1, 0)
    )
    final_down = jnp.concatenate([down_first, down_second], axis=1).reshape(down_weight.shape)
    final_out = tail_out.reshape(out_weight.shape)
    tail_bias = tail_bias[:, 0]
    final_down_bias = tail_bias[:, :width_part].reshape(model_width)
    final_out_bias = tail_bias[:, width_part : 2 * width_part].reshape(model_width)
    final_up_bias = tail_bias[:, 2 * width_part : 2 * width_part + hidden_part].reshape(
        up_bias.shape
    )
    slots_sum, final_up, final_down, final_out = lax.optimization_barrier(
        (slots_sum, final_up, final_down, final_out)
    )
    slots_sum = jnp.sum(
        slots_sum.reshape(shard_groups, shard_heads, -1, model_width), axis=0
    )
    final_qkv = (
        slots_sum[:, : 3 * HD]
        .reshape(shard_heads, 3, HD, model_width)
        .transpose(3, 1, 0, 2)
        .reshape(qkv_weight.shape)
    )
    final_qv_bias = (
        slots_sum[:, 3 * HD, : 2 * HD]
        .reshape(shard_heads, 2, HD)
        .transpose(1, 0, 2)
        .reshape(qv_bias.shape)
    )

    grad_tokens = from_units(grad_tokens).astype(f32)
    grad_modulation = jnp.stack(
        [
            grad_shift_one,
            grad_scale_one,
            grad_gate_one,
            grad_shift_two,
            grad_scale_two,
            grad_gate_two,
        ],
        axis=1,
    )
    unit_steps = lax.dynamic_slice_in_dim(
        noise_steps.reshape(unit_total), tensor_at * units, units
    ).astype(f32)
    grad_mod_parts = exchange(
        to_relative(
            jnp.concatenate(
                [
                    grad_modulation.reshape(units, 6, tensor_count, column_part)
                    .transpose(2, 0, 1, 3)
                    .reshape(tensor_count, units, 6 * column_part),
                    jnp.broadcast_to(unit_steps[None, :, None], (tensor_count, units, 128)),
                ],
                axis=2,
            )
        )
    )
    grad_mod_all = lax.all_gather(
        jnp.stack(grad_mod_parts).reshape(unit_total, -1), "frame", axis=0, tiled=True
    )
    act_all = noise_activation(grad_mod_all[:, -1], model_width)
    grad_mod_all = grad_mod_all[:, :-128].reshape(-1, 6, column_part)
    grad_ada_weight = jnp.einsum(
        "ud,ukj->dkj", act_all.astype(f32), grad_mod_all, precision=lax.Precision.HIGH
    )
    grad_ada_bias = jnp.sum(grad_mod_all, axis=0)
    return (
        result,
        grad_tokens,
        grad_ada_weight,
        grad_ada_bias,
        final_qkv,
        final_qv_bias,
        final_out,
        final_out_bias,
        final_up,
        final_up_bias,
        final_down,
        final_down_bias,
    )


def solution(mesh):
    in_specs = (
        P(None, "frame", "tensor", None),
        P(None, "frame"),
        P(None, None, "tensor"),
        P(None, "tensor"),
        P(None, None, "tensor"),
        P(None, "tensor"),
        P("tensor", None),
        P(),
        P(None, "tensor"),
        P("tensor"),
        P("tensor", None),
        P(),
        P(None, "frame", "tensor", None),
    )
    out_specs = (
        P(None, "frame", "tensor", None),
        P(None, "frame", "tensor", None),
        P(None, None, "tensor"),
        P(None, "tensor"),
        P(None, None, "tensor"),
        P(None, "tensor"),
        P("tensor", None),
        P(),
        P(None, "tensor"),
        P("tensor"),
        P("tensor", None),
        P(),
    )
    return jax.shard_map(
        on_device, mesh=mesh, in_specs=in_specs, out_specs=out_specs, check_vma=False
    )
```

time: 859 us -> 643 us (0.75)
  waiting for transfers between devices: 356 us -> 200 us
  blocking collectives: 100 us -> 9.84 us
  matrix products: 105 us -> 41.3 us
  other arithmetic: 42.5 us -> 74.3 us
  starting transfers between devices: 31.2 us -> 61.2 us
  local copies, waits for them, and re-layouts: 66 us -> 87 us
  Pallas kernels: 135 us -> 146 us
    reduce_scatter x6 -> x3, waiting for transfers between devices: 214 us -> 4.37 us  [the longest x1 4.35 us: on_device(): lax.psum_scatter(grad_hidden_part, 'frame', scatter_dimension=0, tiled=True)]
    ppermute x0 -> x37, waiting for transfers between devices: none -> 162 us  [the longest x30 114 us: shifted(): lax.ppermute(values, 'tensor', [(t, (t + shift) % tensor_count) for t in...]
    all_gather x4 -> x1, blocking collectives: 87.5 us -> 9.84 us  [on_device(): lax.all_gather(jnp.stack(grad_mod_parts).reshape(unit_total, -1), 'frame'...]
    all_to_all x7 -> x2, waiting for transfers between devices: 62.2 us -> 0.01 us  [swap_frame(): lax.all_to_all(values, 'frame', split_axis=0, concat_axis=0, tiled=True)]
    ppermute x0 -> x37, starting transfers between devices: none -> 51.7 us  [the longest x30 45.2 us: shifted(): lax.ppermute(values, 'tensor', [(t, (t + shift) % tensor_count) for t in...]
    all_gather x1, waiting for transfers between devices: 49.6 us -> 0.02 us  [on_device(): lax.all_gather(hidden_one.reshape(own_rows, model_width), 'frame', axis=0...]
    pallas_call x0 -> x2, Pallas kernels: none -> 40.6 us  [mlp(): pl.pallas_call(mlp_kernel, grid_spec=pltpu.PrefetchScalarGridSpec(num_sca...]
    pallas_call x1 -> x2, Pallas kernels: 68.3 us -> 42.6 us  [attend(): pl.pallas_call(partial(attend_kernel, head_count=head_count, patch_count=...]
  transfers between devices with their start and end apart: 22 -> 47, of which waited for: 11 -> 16; matrix products, arithmetic and copies ran while one was open for 17% -> 23% of each run, Pallas kernels for 16% -> 20%
where the time goes in v2:
time: 643 us; the launch traced here: 635 us
  waiting for transfers between devices  200 us (31%)
  Pallas kernels  146 us (23%)
  local copies, waits for them, and re-layouts  87 us (14%)
  other arithmetic  74.3 us (12%)
  starting transfers between devices  61.2 us (10%)
  matrix products  41.3 us (6%)
  between operations  16 us (2%)
  blocking collectives  9.84 us (2%)
    ppermute x30, waiting for transfers between devices, shifted(): lax.ppermute(values, 'tensor', [(t, (t + shift) % tensor_count) for t in...  114 us
    pallas_call x2, Pallas kernels, attend_back(): pl.pallas_call(partial(attend_back_kernel, head_count=head_count, patch_c...  62.4 us
    ppermute x30, starting transfers between devices, shifted(): lax.ppermute(values, 'tensor', [(t, (t + shift) % tensor_count) for t in...  45.2 us
    pallas_call x2, Pallas kernels, attend(): pl.pallas_call(partial(attend_kernel, head_count=head_count, patch_count=...  42.6 us
    pallas_call x2, Pallas kernels, mlp(): pl.pallas_call(mlp_kernel, grid_spec=pltpu.PrefetchScalarGridSpec(num_sca...  40.6 us
    all_gather x2, waiting for transfers between devices, frame_parts(): lax.all_gather(values.astype(bf16), 'frame', axis=0, tiled=True)  33.4 us
    unnamed x183, local copies, waits for them, and re-layouts  30.7 us
    ppermute x2, waiting for transfers between devices, to_owners(): total = total + lax.ppermute(piece, ('frame', 'tensor'), pairs).astype(f32)  19.2 us
  transfers between devices with their start and end apart: 47, of which 16 were waited for; matrix products, arithmetic and copies ran while one was open for 23% of the time, Pallas kernels for 20%

profile of v2, /device:TPU:0, one launch (start us, length us, event | category | flops | bytes accessed | tf_op | source)
XLA Modules:
  0.0 635.2 jit_solution(12298282555047385945)
XLA Ops:
  9.8 5.1 collective-permute-start.3
  21.2 18.4 %collective-permute-done.4 = f32[12,256]{1,0:T(8,128)S(1)} collective-permute-done((f32[12,256]{1,0:T(8,128)S(1)}, f32[12,256]{1,0:T(8,128)S(1)}, u32[]{:S(2)}, u32[]{:S(2)}) %collective-permute-start.4) | collective-permute-done | bytes 12320 | tf_op jit(solution)/shard_map/ppermute | solution.py:464
  52.0 7.5 %collective-permute-done.11 = bf16[176,1024]{1,0:T(8,128)(2,1)S(1)} collective-permute-done((bf16[176,1024]{1,0:T(8,128)(2,1)S(1)}, bf16[176,1024]{1,0:T(8,128)(2,1)S(1)}, u32[]{:S(2)}, u32[]{:S(2)}) %collective-permute-start.11) | collective-permute-done | bytes 360480 | tf_op jit(solution)/shard_map/ppermute | solution.py:464
  59.5 22.2 %collective-permute-done.12 = bf16[176,1024]{1,0:T(8,128)(2,1)S(1)} collective-permute-done((bf16[176,1024]{1,0:T(8,128)(2,1)S(1)}, bf16[176,1024]{1,0:T(8,128)(2,1)S(1)}, u32[]{:S(2)}, u32[]{:S(2)}) %collective-permute-start.12) | collective-permute-done | bytes 360480 | tf_op jit(solution)/shard_map/ppermute | solution.py:464
  89.0 18.9 %collective-permute-done.7 = bf16[208,1024]{1,0:T(8,128)(2,1)S(1)} collective-permute-done((bf16[208,1024]{1,0:T(8,128)(2,1)S(1)}, bf16[208,1024]{1,0:T(8,128)(2,1)S(1)}, u32[]{:S(2)}, u32[]{:S(2)}) %collective-permute-start.7) | collective-permute-done | bytes 426016 | tf_op jit(solution)/shard_map/ppermute | solution.py:508
  109.2 9.9 %add_convert_fusion = bf16[4096,384]{0,1:T(8,128)(2,1)S(1)} fusion(bf16[4096,1024]{1,0:T(8,128)(2,1)} %all-gather.6.cloned.1.call-done, bf16[384,1024]{1,0:T(8,128)(2,1)S(1)} %bitcast.426, f32[384]{0:T(512)S(1)} %pad_maximum_fusion.14), kind=kOutput, calls=%fused_computation.1 | convolution fusion | flops 3224371200 | bytes 12322304 | tf_op jit(solution)/shard_map/dot_general | solution.py:47
  127.7 22.2 %attend.2 = (bf16[2816,128]{1,0:T(8,128)(2,1)S(1)}, f32[11,1,512]{2,1,0:T(1,128)S(1)}) custom-call(s32[16]{0:T(128)S(1)} %fusion.72.frame_ids, bf16[4096,128]{1,0:T(8,128)(2,1)S(1)} %copy.108.q_ref, bf16[4096,128]{1,0:T(8,128)(2,1)S(1)} %copy.109.k_ref, bf16[128,4096]{1,0:T(8,128)(2,1)S(1)} %get-tuple-element.143.vt_ref), custom_call_target="tpu_custom_call" | custom-call | flops 6576668672 | bytes 2883584 | tf_op jit(solution)/shard_map/attend/pallas_call | solution.py:141
  161.2 20.3 %attend.3 = (bf16[1280,128]{1,0:T(8,128)(2,1)S(1)}, f32[5,1,512]{2,1,0:T(1,128)S(1)}) custom-call(s32[16]{0:T(128)S(1)} %fusion.72.frame_ids, bf16[4096,128]{1,0:T(8,128)(2,1)S(1)} %copy.108.q_ref, bf16[4096,128]{1,0:T(8,128)(2,1)S(1)} %copy-done.9, bf16[128,4096]{1,0:T(8,128)(2,1)S(1)} %copy-done.17, bf16[4,128,1024]{2,1,0:T(8,128)(2,1)S(1)} %copy-done.2), custom_call_target="tpu_custom_call" | custom-call | flops 4697620480 | bytes 1310720 | tf_op jit(solution)/shard_map/attend/pallas_call | solution.py:141
  183.0 5.5 all-to-all-start
  197.4 17.9 %collective-permute-done.15 = bf16[2,64,1024]{2,1,0:T(8,128)(2,1)S(1)} collective-permute-done((bf16[2,64,1024]{2,1,0:T(8,128)(2,1)S(1)}, bf16[2,64,1024]{2,1,0:T(8,128)(2,1)S(1)}, u32[]{:S(2)}, u32[]{:S(2)}) %collective-permute-start.15) | collective-permute-done | bytes 262176 | tf_op jit(solution)/shard_map/ppermute | solution.py:464
  224.2 4.6 fusion.78
  230.1 20.2 %mlp.2 = (f32[512,1024]{1,0:T(8,128)}, f32[512,1024]{1,0:T(8,128)}, bf16[4,4,128,1024]{3,2,1,0:T(8,128)(2,1)}, bf16[4,4,128,1024]{3,2,1,0:T(8,128)(2,1)}, f32[4,...) custom-call(s32[1]{0:T(128)} %bitcast.55.core_ref, bf16[512,1024]{1,0:T(8,128)(2,1)S(1)} %bitcast.365, ...), custom_call_target="tpu_custom_call" | custom-call | flops 12884901888 | bytes 16777216 | tf_op jit(solution)/shard_map/mlp/pallas_call | solution.py:378
  252.9 6.5 %collective-permute-done.20 = bf16[4,4,128,1024]{3,2,1,0:T(8,128)(2,1)} collective-permute-done((bf16[4,4,128,1024]{3,2,1,0:T(8,128)(2,1)}, bf16[4,4,128,1024]{3,2,1,0:T(8,128)(2,1)}, u32[]{:S(2)}, u32[]{:S(2)}) %collective-permute-start.20) | collective-permute-done | bytes 4194336 | tf_op jit(solution)/shard_map/ppermute | solution.py:533
  259.4 7.7 %add.408 = bf16[4,4,128,1024]{3,2,1,0:T(8,128)(2,1)} add(bf16[4,4,128,1024]{3,2,1,0:T(8,128)(2,1)} %get-tuple-element.66, bf16[4,4,128,1024]{3,2,1,0:T(8,128)(2,1)} %collective-permute-done.20) | non-fusion elementwise | flops 2097152 | bytes 12582912 | tf_op jit(solution)/shard_map/add | solution.py:534
  267.1 20.4 %mlp.3 = (f32[512,1024]{1,0:T(8,128)}, f32[512,1024]{1,0:T(8,128)}, bf16[4,4,128,1024]{3,2,1,0:T(8,128)(2,1)}, bf16[4,4,128,1024]{3,2,1,0:T(8,128)(2,1)}, f32[4,...) custom-call(s32[1]{0:T(128)} %bitcast.55.core_ref, bf16[512,1024]{1,0:T(8,128)(2,1)S(1)} %bitcast.366, ...), custom_call_target="tpu_custom_call" | custom-call | flops 12884901888 | bytes 16777216 | tf_op jit(solution)/shard_map/mlp/pallas_call | solution.py:378
  342.9 13.6 %collective-permute-done.18 = bf16[2,64,1024]{2,1,0:T(8,128)(2,1)S(1)} collective-permute-done((bf16[2,64,1024]{2,1,0:T(8,128)(2,1)S(1)}, bf16[2,64,1024]{2,1,0:T(8,128)(2,1)S(1)}, u32[]{:S(2)}, u32[]{:S(2)}) %collective-permute-start.18) | collective-permute-done | bytes 262176 | tf_op jit(solution)/shard_map/ppermute | solution.py:464
  370.1 31.8 %attend_back.2 = (bf16[2816,128]{1,0:T(8,128)(2,1)S(1)}, f32[4096,128]{1,0:T(8,128)}, f32[4096,128]{1,0:T(8,128)}) custom-call(s32[16]{0:T(128)S(1)} %fusion.72.frame_ids, bf16[4096,128]{1,0:T(8,128)(2,1)S(1)} %copy-done.6, bf16[4096,128]{1,0:T(8,128)(2,1)S(1)} %bitcast.369, bf16[4096,128]{1,0:T(8,128)(2,1)S(1)} %copy-done.4, ...), custom_call_target="tpu_custom_call" | custom-call | flops 16441671680 | bytes 5767168 | tf_op jit(solution)/shard_map/attend_back/pallas_call | solution.py:254
  403.1 30.6 %attend_back.3 = (bf16[1280,128]{1,0:T(8,128)(2,1)S(1)}, bf16[4096,128]{1,0:T(8,128)(2,1)S(1)}, bf16[4096,128]{1,0:T(8,128)(2,1)S(1)}) custom-call(s32[16]{0:T(128)S(1)} %fusion.72.frame_ids, bf16[4096,128]{1,0:T(8,128)(2,1)S(1)} %copy-done.7, bf16[4096,128]{1,0:T(8,128)(2,1)S(1)} %bitcast.370, bf16[4096,128]{1,0:T(8,128)(2,1)S(1)} %copy-done.4, ...), custom_call_target="tpu_custom_call" | custom-call | flops 11744051200 | bytes 2621440 | tf_op jit(solution)/shard_map/attend_back/pallas_call | solution.py:254
  434.8 8.6 %convolution_convert_fusion = bf16[4096,1024]{1,0:T(8,128)(2,1)} fusion(bf16[384,1024]{1,0:T(8,128)(2,1)S(1)} %bitcast.427, bf16[4096,128]{1,0:T(8,128)(2,1)S(1)} %get-tuple-element.84, bf16[4096,128]{1,0:T(8,128)(2,1)S(1)} %get-tuple-element.83, bf16[1280,128]{1,0:T(8,128)(2,1)S(1)} %get-tuple-element.82, bf16[2816,128]{1,0:T(8,128)(2,1)S(1)} %get-tuple-element.79), kind=kOutput, calls=%fused_computation | convolution fusion | flops 3238002688 | bytes 12320768 | tf_op jit(solution)/shard_map/dot_general | solution.py:43
  444.6 4.5 pad_maximum_fusion.4
  449.1 6.7 %convolution_convert_fusion.3 = bf16[384,1024]{1,0:T(8,128)(2,1)S(1)} fusion(bf16[4096,384]{1,0:T(8,128)(2,1)S(1)} %pad_maximum_fusion.4, bf16[4096,1024]{1,0:T(8,128)(2,1)} %all-gather.6.cloned.1.call-done), kind=kOutput, calls=%fused_computation.64 | convolution fusion | flops 3221618688 | bytes 12320768 | tf_op jit(solution)/shard_map/dot_general | solution.py:51
  458.4 19.1 %collective-permute-done.36 = bf16[208,1024]{1,0:T(8,128)(2,1)S(1)} collective-permute-done((bf16[208,1024]{1,0:T(8,128)(2,1)S(1)}, bf16[208,1024]{1,0:T(8,128)(2,1)S(1)}, u32[]{:S(2)}, u32[]{:S(2)}) %collective-permute-start.36) | collective-permute-done | bytes 426016 | tf_op jit(solution)/shard_map/ppermute | solution.py:517
  484.0 9.2 %collective-permute-done.26 = bf16[176,1024]{1,0:T(8,128)(2,1)S(1)} collective-permute-done((bf16[176,1024]{1,0:T(8,128)(2,1)S(1)}, bf16[176,1024]{1,0:T(8,128)(2,1)S(1)}, u32[]{:S(2)}, u32[]{:S(2)}) %collective-permute-start.26) | collective-permute-done | bytes 360480 | tf_op jit(solution)/shard_map/ppermute | solution.py:464
  493.2 14.5 %collective-permute-done.27 = bf16[176,1024]{1,0:T(8,128)(2,1)S(1)} collective-permute-done((bf16[176,1024]{1,0:T(8,128)(2,1)S(1)}, bf16[176,1024]{1,0:T(8,128)(2,1)S(1)}, u32[]{:S(2)}, u32[]{:S(2)}) %collective-permute-start.27) | collective-permute-done | bytes 360480 | tf_op jit(solution)/shard_map/ppermute | solution.py:464
  520.0 30.1 %all-gather.12.cloned.1.call-done = bf16[1664,1024]{1,0:T(8,128)(2,1)} async-done(((bf16[208,1024]{1,0:T(8,128)(2,1)}), bf16[1664,1024]{1,0:T(8,128)(2,1)}) %all-gather.12.cloned.1.call-update) | async-done | bytes 3407888 | tf_op jit(solution)/shard_map/all_gather | solution.py:547
  550.1 5.5 convert.41
  565.2 9.8 %all_gather.21 = f32[64,1664]{1,0:T(8,128)S(1)} all-gather(f32[8,1664]{1,0:T(8,128)S(1)} %reshape.447), channel_id=1, replica_groups=mesh['frame'=8,'tensor'=4] {'frame'}, dimensions={0}, use_global_device_ids=true | all-gather | bytes 479232 | tf_op jit(solution)/shard_map/all_gather | solution.py:912
  575.8 4.6 fusion.42
  581.0 6.8 %collective-permute-done.30 = bf16[2,64,1024]{2,1,0:T(8,128)(2,1)S(1)} collective-permute-done((bf16[2,64,1024]{2,1,0:T(8,128)(2,1)}, bf16[2,64,1024]{2,1,0:T(8,128)(2,1)S(1)}, u32[]{:S(2)}, u32[]{:S(2)}) %collective-permute-start.30) | collective-permute-done | bytes 262176 | tf_op jit(solution)/shard_map/ppermute | solution.py:464
  592.9 4.4 fusion.79
  601.8 5.3 copy.153
  611.3 5.8 reduce_sum.202
  (445 shorter events, 200.8 us)
Async XLA Ops:
  7.2 101.2 %all-gather.6.cloned.1.call-start = ((), (), s32[]{:S(2)}) async-start(), calls=%async_computation.5 | async-start | bytes 9437184 | tf_op jit(solution)/shard_map/all_gather | solution.py:619
  16.1 23.7 %collective-permute-start = (bf16[2,64,1024]{2,1,0:T(8,128)(2,1)S(1)}, bf16[2,64,1024]{2,1,0:T(8,128)(2,1)S(1)}, u32[]{:S(2)}, u32[]{:S(2)}) collective-permute-start(bf16[2,64,1024]{2,1,0:T(8,128)(2,1)S(1)} %get-tuple-element.167), channel_id=1, source_target_pairs={{0,3},{1,0},{2,1},{3,2},{4,7},{5,4},{6,5},{7,6},{8,11},{9,8},{10,9... | collective-permute-start | bytes 786440 | tf_op jit(solution)/shard_map/ppermute | solution.py:464
  16.6 23.2 %collective-permute-start.1 = (bf16[2,64,1024]{2,1,0:T(8,128)(2,1)S(1)}, bf16[2,64,1024]{2,1,0:T(8,128)(2,1)S(1)}, u32[]{:S(2)}, u32[]{:S(2)}) collective-permute-start(bf16[2,64,1024]{2,1,0:T(8,128)(2,1)S(1)} %get-tuple-element.168), channel_id=1, source_target_pairs={{0,2},{1,3},{2,0},{3,1},{4,6},{5,7},{6,4},{7,5},{8,10},{9,11},{10,... | collective-permute-start | bytes 786440 | tf_op jit(solution)/shard_map/ppermute | solution.py:464
  16.6 23.2 %collective-permute-start.2 = (bf16[2,64,1024]{2,1,0:T(8,128)(2,1)S(1)}, bf16[2,64,1024]{2,1,0:T(8,128)(2,1)S(1)}, u32[]{:S(2)}, u32[]{:S(2)}) collective-permute-start(bf16[2,64,1024]{2,1,0:T(8,128)(2,1)S(1)} %get-tuple-element.170), channel_id=1, source_target_pairs={{0,1},{1,2},{2,3},{3,0},{4,5},{5,6},{6,7},{7,4},{8,9},{9,10},{10,1... | collective-permute-start | bytes 786440 | tf_op jit(solution)/shard_map/ppermute | solution.py:464
  18.2 21.4 %collective-permute-start.4 = (f32[12,256]{1,0:T(8,128)S(1)}, f32[12,256]{1,0:T(8,128)S(1)}, u32[]{:S(2)}, u32[]{:S(2)}) collective-permute-start(f32[12,256]{1,0:T(8,128)S(1)} %get-tuple-element.178), channel_id=1, source_target_pairs={{0,2},{1,3},{2,0},{3,1},{4,6},{5,7},{6,4},{7,5},{8,10},{9,11},{10,... | collective-permute-start | bytes 36872 | tf_op jit(solution)/shard_map/ppermute | solution.py:464
  42.4 176.6 %all-gather.8.cloned.1.call-start = ((), (), s32[]{:S(2)}) async-start(), calls=%async_computation.6 | async-start | bytes 12976128 | tf_op jit(solution)/shard_map/all_gather | solution.py:623
  50.6 31.1 %collective-permute-start.12 = (bf16[176,1024]{1,0:T(8,128)(2,1)S(1)}, bf16[176,1024]{1,0:T(8,128)(2,1)S(1)}, u32[]{:S(2)}, u32[]{:S(2)}) collective-permute-start(bf16[176,1024]{1,0:T(8,128)(2,1)S(1)} %fusion.46), channel_id=1, source_target_pairs={{0,2},{1,3},{2,0},{3,1},{4,6},{5,7},{6,4},{7,5},{8,10},{9,11},{10,... | collective-permute-start | bytes 1081352 | tf_op jit(solution)/shard_map/ppermute | solution.py:464
  50.6 31.1 %collective-permute-start.13 = (bf16[176,1024]{1,0:T(8,128)(2,1)S(1)}, bf16[176,1024]{1,0:T(8,128)(2,1)S(1)}, u32[]{:S(2)}, u32[]{:S(2)}) collective-permute-start(bf16[176,1024]{1,0:T(8,128)(2,1)S(1)} %fusion.46), channel_id=1, source_target_pairs={{0,1},{1,2},{2,3},{3,0},{4,5},{5,6},{6,7},{7,4},{8,9},{9,10},{10,1... | collective-permute-start | bytes 1081352 | tf_op jit(solution)/shard_map/ppermute | solution.py:464
  83.3 183.7 %all-gather.10.cloned.1.call-start = ((), (), s32[]{:S(2)}) async-start(), calls=%async_computation.7 | async-start | bytes 9437184 | tf_op jit(solution)/shard_map/all_gather | solution.py:706
  86.0 21.8 %collective-permute-start.7 = (bf16[208,1024]{1,0:T(8,128)(2,1)S(1)}, bf16[208,1024]{1,0:T(8,128)(2,1)S(1)}, u32[]{:S(2)}, u32[]{:S(2)}) collective-permute-start(bf16[208,1024]{1,0:T(8,128)(2,1)S(1)} %fusion.41), channel_id=1, source_target_pairs={{2,0},{3,1},{0,2},{1,3},{6,4},{7,5},{4,6},{5,7},{10,8},{11,9},{8,1... | collective-permute-start | bytes 1277960 | tf_op jit(solution)/shard_map/ppermute | solution.py:508
  121.7 28.2 %collective-permute-start.10 = (bf16[128,1024]{1,0:T(8,128)(2,1)S(1)}, bf16[128,1024]{1,0:T(8,128)(2,1)}, u32[]{:S(2)}, u32[]{:S(2)}) collective-permute-start(bf16[128,1024]{1,0:T(8,128)(2,1)S(1)} %pad_maximum_fusion.8), channel_id=1, source_target_pairs={{0,1},{1,2},{2,3},{3,0},{4,5},{5,6},{6,7},{7,4},{8,9},{9,10},{10,1... | collective-permute-start | bytes 786440 | tf_op jit(solution)/shard_map/ppermute | solution.py:464
  121.8 28.2 %collective-permute-start.8 = (bf16[128,1024]{1,0:T(8,128)(2,1)S(1)}, bf16[128,1024]{1,0:T(8,128)(2,1)}, u32[]{:S(2)}, u32[]{:S(2)}) collective-permute-start(bf16[128,1024]{1,0:T(8,128)(2,1)S(1)} %pad_maximum_fusion.8), channel_id=1, source_target_pairs={{0,3},{1,0},{2,1},{3,2},{4,7},{5,4},{6,5},{7,6},{8,11},{9,8},{10,9... | collective-permute-start | bytes 786440 | tf_op jit(solution)/shard_map/ppermute | solution.py:464
  126.0 23.9 %collective-permute-start.9 = (bf16[128,1024]{1,0:T(8,128)(2,1)S(1)}, bf16[128,1024]{1,0:T(8,128)(2,1)}, u32[]{:S(2)}, u32[]{:S(2)}) collective-permute-start(bf16[128,1024]{1,0:T(8,128)(2,1)S(1)} %pad_maximum_fusion.8), channel_id=1, source_target_pairs={{0,2},{1,3},{2,0},{3,1},{4,6},{5,7},{6,4},{7,5},{8,10},{9,11},{10,... | collective-permute-start | bytes 786440 | tf_op jit(solution)/shard_map/ppermute | solution.py:464
  183.0 33.4 %all-to-all-start = ((bf16[8,512,128]{1,2,0:T(8,128)(2,1)}), bf16[8,512,128]{1,2,0:T(8,128)(2,1)}, u32[]{:S(2)}, u32[]{:S(2)}) async-start(bf16[8,512,128]{1,2,0:T(8,128)(2,1)} %copy.113), calls=%async_computation | async-start | bytes 2097152 | tf_op jit(solution)/shard_map/all_to_all | solution.py:461
  188.5 170.5 %reduce-scatter.4.cloned.1.call-start = ((), (), s32[]{:S(2)}) async-start(), calls=%async_computation.8 | async-start | bytes 5242880 | tf_op jit(solution)/shard_map/reduce_scatter | solution.py:537
  189.5 25.8 %collective-permute-start.15 = (bf16[2,64,1024]{2,1,0:T(8,128)(2,1)S(1)}, bf16[2,64,1024]{2,1,0:T(8,128)(2,1)S(1)}, u32[]{:S(2)}, u32[]{:S(2)}) collective-permute-start(bf16[2,64,1024]{2,1,0:T(8,128)(2,1)S(1)} %get-tuple-element.166), channel_id=1, source_target_pairs={{0,2},{1,3},{2,0},{3,1},{4,6},{5,7},{6,4},{7,5},{8,10},{9,11},{10,... | collective-permute-start | bytes 786440 | tf_op jit(solution)/shard_map/ppermute | solution.py:464
  191.6 23.7 %collective-permute-start.16 = (bf16[2,64,1024]{2,1,0:T(8,128)(2,1)S(1)}, bf16[2,64,1024]{2,1,0:T(8,128)(2,1)S(1)}, u32[]{:S(2)}, u32[]{:S(2)}) collective-permute-start(bf16[2,64,1024]{2,1,0:T(8,128)(2,1)S(1)} %get-tuple-element.165), channel_id=1, source_target_pairs={{0,1},{1,2},{2,3},{3,0},{4,5},{5,6},{6,7},{7,4},{8,9},{9,10},{10,1... | collective-permute-start | bytes 786440 | tf_op jit(solution)/shard_map/ppermute | solution.py:464
  289.2 189.3 %reduce-scatter.6.cloned.1.call-start = ((), (), s32[]{:S(2)}) async-start(), calls=%async_computation.9 | async-start | bytes 7208960 | tf_op jit(solution)/shard_map/reduce_scatter | solution.py:537
  290.8 29.3 %collective-permute-start.24 = (bf16[4,4,128,1024]{3,2,1,0:T(8,128)(2,1)}, bf16[4,4,128,1024]{3,2,1,0:T(8,128)(2,1)}, u32[]{:S(2)}, u32[]{:S(2)}) collective-permute-start(bf16[4,4,128,1024]{3,2,1,0:T(8,128)(2,1)} %get-tuple-element.70), channel_id=1, source_target_pairs={{0,4},{4,0},{8,12},{12,8},{16,20},{20,16},{24,28},{28,24},{1,5},{5... | collective-permute-start | bytes 12582920 | tf_op jit(solution)/shard_map/ppermute | solution.py:533
  331.2 25.4 %collective-permute-start.18 = (bf16[2,64,1024]{2,1,0:T(8,128)(2,1)S(1)}, bf16[2,64,1024]{2,1,0:T(8,128)(2,1)S(1)}, u32[]{:S(2)}, u32[]{:S(2)}) collective-permute-start(bf16[2,64,1024]{2,1,0:T(8,128)(2,1)S(1)} %get-tuple-element.161), channel_id=1, source_target_pairs={{0,2},{1,3},{2,0},{3,1},{4,6},{5,7},{6,4},{7,5},{8,10},{9,11},{10,... | collective-permute-start | bytes 786440 | tf_op jit(solution)/shard_map/ppermute | solution.py:464
  337.1 28.3 %all-to-all-start.1 = ((bf16[8,512,128]{2,1,0:T(8,128)(2,1)}), bf16[8,512,128]{2,1,0:T(8,128)(2,1)S(1)}, u32[]{:S(2)}, u32[]{:S(2)}) async-start(bf16[8,512,128]{2,1,0:T(8,128)(2,1)} %bitcast.363), calls=%async_computation.3 | async-start | bytes 2097152 | tf_op jit(solution)/shard_map/all_to_all | solution.py:461
  340.7 173.5 %reduce-scatter.8.cloned.1.call-start = ((), (), s32[]{:S(2)}) async-start(), calls=%async_computation.10 | async-start | bytes 9437184 | tf_op jit(solution)/shard_map/reduce_scatter | solution.py:813
  361.0 40.8 %collective-permute-start.21 = (bf16[128,1024]{1,0:T(8,128)(2,1)}, bf16[128,1024]{1,0:T(8,128)(2,1)S(1)}, u32[]{:S(2)}, u32[]{:S(2)}) collective-permute-start(bf16[128,1024]{1,0:T(8,128)(2,1)} %get-tuple-element.157), channel_id=1, source_target_pairs={{0,1},{1,2},{2,3},{3,0},{4,5},{5,6},{6,7},{7,4},{8,9},{9,10},{10,1... | collective-permute-start | bytes 786440 | tf_op jit(solution)/shard_map/ppermute | solution.py:464
  361.0 40.8 %collective-permute-start.22 = (bf16[128,1024]{1,0:T(8,128)(2,1)}, bf16[128,1024]{1,0:T(8,128)(2,1)}, u32[]{:S(2)}, u32[]{:S(2)}) collective-permute-start(bf16[128,1024]{1,0:T(8,128)(2,1)} %get-tuple-element.159), channel_id=1, source_target_pairs={{0,2},{1,3},{2,0},{3,1},{4,6},{5,7},{6,4},{7,5},{8,10},{9,11},{10,... | collective-permute-start | bytes 786440 | tf_op jit(solution)/shard_map/ppermute | solution.py:464
  363.3 38.5 %collective-permute-start.23 = (bf16[128,1024]{1,0:T(8,128)(2,1)}, bf16[128,1024]{1,0:T(8,128)(2,1)}, u32[]{:S(2)}, u32[]{:S(2)}) collective-permute-start(bf16[128,1024]{1,0:T(8,128)(2,1)} %get-tuple-element.158), channel_id=1, source_target_pairs={{0,3},{1,0},{2,1},{3,2},{4,7},{5,4},{6,5},{7,6},{8,11},{9,8},{10,9... | collective-permute-start | bytes 786440 | tf_op jit(solution)/shard_map/ppermute | solution.py:464
  443.4 106.7 %all-gather.12.cloned.1.call-start = ((), (), s32[]{:S(2)}) async-start(), calls=%async_computation.11 | async-start | bytes 3833856 | tf_op jit(solution)/shard_map/all_gather | solution.py:547
  457.2 20.3 %collective-permute-start.36 = (bf16[208,1024]{1,0:T(8,128)(2,1)S(1)}, bf16[208,1024]{1,0:T(8,128)(2,1)S(1)}, u32[]{:S(2)}, u32[]{:S(2)}) collective-permute-start(bf16[208,1024]{1,0:T(8,128)(2,1)S(1)} %get-tuple-element.172), channel_id=1, source_target_pairs={{0,2},{1,3},{2,0},{3,1},{4,6},{5,7},{6,4},{7,5},{8,10},{9,11},{10,... | collective-permute-start | bytes 1277960 | tf_op jit(solution)/shard_map/ppermute | solution.py:517
  478.5 114.4 %all-gather.14.cloned.1.call-start = ((), (), s32[]{:S(2)}) async-start(), calls=%async_computation.12 | async-start | bytes 5603328 | tf_op jit(solution)/shard_map/all_gather | solution.py:547
  480.0 27.7 %collective-permute-start.27 = (bf16[176,1024]{1,0:T(8,128)(2,1)S(1)}, bf16[176,1024]{1,0:T(8,128)(2,1)S(1)}, u32[]{:S(2)}, u32[]{:S(2)}) collective-permute-start(bf16[176,1024]{1,0:T(8,128)(2,1)S(1)} %get-tuple-element.152), channel_id=1, source_target_pairs={{0,2},{1,3},{2,0},{3,1},{4,6},{5,7},{6,4},{7,5},{8,10},{9,11},{10,... | collective-permute-start | bytes 1081352 | tf_op jit(solution)/shard_map/ppermute | solution.py:464
  480.9 26.9 %collective-permute-start.28 = (bf16[176,1024]{1,0:T(8,128)(2,1)S(1)}, bf16[176,1024]{1,0:T(8,128)(2,1)S(1)}, u32[]{:S(2)}, u32[]{:S(2)}) collective-permute-start(bf16[176,1024]{1,0:T(8,128)(2,1)S(1)} %get-tuple-element.151), channel_id=1, source_target_pairs={{0,3},{1,0},{2,1},{3,2},{4,7},{5,4},{6,5},{7,6},{8,11},{9,8},{10,9... | collective-permute-start | bytes 1081352 | tf_op jit(solution)/shard_map/ppermute | solution.py:464
  564.0 23.8 %collective-permute-start.30 = (bf16[2,64,1024]{2,1,0:T(8,128)(2,1)}, bf16[2,64,1024]{2,1,0:T(8,128)(2,1)S(1)}, u32[]{:S(2)}, u32[]{:S(2)}) collective-permute-start(bf16[2,64,1024]{2,1,0:T(8,128)(2,1)} %get-tuple-element.155), channel_id=1, source_target_pairs={{0,2},{1,3},{2,0},{3,1},{4,6},{5,7},{6,4},{7,5},{8,10},{9,11},{10,... | collective-permute-start | bytes 786440 | tf_op jit(solution)/shard_map/ppermute | solution.py:464
  565.1 22.7 %collective-permute-start.31 = (bf16[2,64,1024]{2,1,0:T(8,128)(2,1)S(1)}, bf16[2,64,1024]{2,1,0:T(8,128)(2,1)S(1)}, u32[]{:S(2)}, u32[]{:S(2)}) collective-permute-start(bf16[2,64,1024]{2,1,0:T(8,128)(2,1)S(1)} %get-tuple-element.154), channel_id=1, source_target_pairs={{0,1},{1,2},{2,3},{3,0},{4,5},{5,6},{6,7},{7,4},{8,9},{9,10},{10,1... | collective-permute-start | bytes 786440 | tf_op jit(solution)/shard_map/ppermute | solution.py:464
  (83 other events, 670.6 us)
Sparse Core Ops, SparseCore 0:
  42.5 56.3 all-gather.5
  101.3 67.7 all-gather.7
  171.0 64.5 all-gather.9
  289.3 51.2 reduce-scatter.3
  344.3 68.1 reduce-scatter.5
  443.5 70.6 reduce-scatter.7
  516.7 33.3 all-gather.11
  552.5 40.3 all-gather.13

commit v3 on v2

--- a/solution.py
+++ b/solution.py
@@ -294,6 +294,237 @@
         ),
         name="attend_back",
     )(frame_ids, queries, grad, out, lse, keys, values, keys_t, *start, *waits)
+
+
+def unpack_kernel(tail_ref, *refs, half, out_rows):
+    up_ref, down_ref, out_ref = refs[-3:]
+    ups, downs, outs = [], [], []
+    for part in range(tail_ref.shape[0]):
+        for row in (0, 2 * half):
+            ups.append(tail_ref[part, row : row + half].astype(f32))
+            downs.append(tail_ref[part, row + half : row + 2 * half].astype(f32))
+        outs.append(tail_ref[part, 4 * half : 4 * half + out_rows].astype(f32))
+    up_ref[...] = jnp.swapaxes(jnp.concatenate(ups, axis=0), 0, 1)
+    down_ref[...] = jnp.concatenate(downs, axis=0)
+    out_ref[...] = jnp.concatenate(outs, axis=0)
+
+
+def unpack(tail, half, out_rows, waits):
+    frame_parts, rows, width = tail.shape
+    parts = max(1, 128 // (2 * half))
+    return pl.pallas_call(
+        partial(unpack_kernel, half=half, out_rows=out_rows),
+        grid=(frame_parts // parts,),
+        in_specs=[pl.BlockSpec((parts, rows, width), lambda n: (n, 0, 0))]
+        + [pl.BlockSpec(memory_space=pl.ANY) for _ in waits],
+        out_specs=[
+            pl.BlockSpec((width, parts * 2 * half), lambda n: (0, n)),
+            pl.BlockSpec((parts * 2 * half, width), lambda n: (n, 0)),
+            pl.BlockSpec((parts * out_rows, width), lambda n: (n, 0)),
+        ],
+        out_shape=[
+            jax.ShapeDtypeStruct((width, frame_parts * 2 * half), f32),
+            jax.ShapeDtypeStruct((frame_parts * 2 * half, width), f32),
+            jax.ShapeDtypeStruct((frame_parts * out_rows, width), f32),
+        ],
+        compiler_params=pltpu.CompilerParams(vmem_limit_bytes=32 << 20),
+        cost_estimate=pl.CostEstimate(
+            flops=0, bytes_accessed=frame_parts * rows * width * 6, transcendentals=0
+        ),
+        name="unpack",
+    )(tail, *waits)
+
+
+def unpack_heads_kernel(slots_ref, *refs):
+    out_ref = refs[-1]
+    groups, slots = slots_ref.shape[:2]
+    for kind in range(3):
+        rows = slice(kind * HD, (kind + 1) * HD)
+        pieces = []
+        for slot in range(slots):
+            total = slots_ref[0, slot, rows].astype(f32)
+            for group in range(1, groups):
+                total = total + slots_ref[group, slot, rows].astype(f32)
+            pieces.append(total)
+        out_ref[kind] = jnp.swapaxes(jnp.concatenate(pieces, axis=0), 0, 1)
+
+
+def unpack_heads(slots, waits):
+    groups, count, rows, width = slots.shape
+    pair = 128 // HD
+    return pl.pallas_call(
+        unpack_heads_kernel,
+        grid=(count // pair,),
+        in_specs=[pl.BlockSpec((groups, pair, rows, width), lambda n: (0, n, 0, 0))]
+        + [pl.BlockSpec(memory_space=pl.ANY) for _ in waits],
+        out_specs=pl.BlockSpec((3, width, 128), lambda n: (0, 0, n)),
+        out_shape=jax.ShapeDtypeStruct((3, width, count * HD), f32),
+        compiler_params=pltpu.CompilerParams(vmem_limit_bytes=40 << 20),
+        cost_estimate=pl.CostEstimate(
+            flops=0, bytes_accessed=groups * count * rows * width * 4, transcendentals=0
+        ),
+        name="unpack_heads",
+    )(slots, *waits)
+
+
+ROWS = 128
+
+
+def project_kernel(
+    heads_ref, weight_ref, bias_ref, tokens_ref, mod_ref, attended_ref, branch_ref, hidden_ref
+):
+    attended = jnp.concatenate([heads_ref[n] for n in range(heads_ref.shape[0])], axis=1)
+    attended_ref[...] = attended
+    branch = dot(attended, weight_ref[...]) + bias_ref[...]
+    branch_ref[...] = branch
+    gate_one, shift_two, scale_two = mod_ref[0, 2:3], mod_ref[0, 3:4], mod_ref[0, 4:5]
+    normed = layer_norm(tokens_ref[...].astype(f32) + gate_one * branch)[0]
+    hidden_ref[...] = (normed * (1.0 + scale_two) + shift_two).astype(bf16)
+
+
+def project(heads, weight, bias, tokens, modulation):
+    frame_parts, rows, lanes = heads.shape
+    width = weight.shape[0]
+    unit_steps = rows // modulation.shape[0] // ROWS
+    block = pl.BlockSpec((ROWS, width), lambda n: (n, 0))
+    return pl.pallas_call(
+        project_kernel,
+        grid=(rows // ROWS,),
+        in_specs=[
+            pl.BlockSpec((frame_parts, ROWS, lanes), lambda n: (0, n, 0)),
+            pl.BlockSpec((width, width), lambda n: (0, 0)),
+            pl.BlockSpec((1, width), lambda n: (0, 0)),
+            block,
+            pl.BlockSpec((1, 6, width), lambda n: (n // unit_steps, 0, 0)),
+        ],
+        out_specs=[block, block, block],
+        out_shape=[
+            jax.ShapeDtypeStruct((rows, width), bf16),
+            jax.ShapeDtypeStruct((rows, width), f32),
+            jax.ShapeDtypeStruct((rows, width), bf16),
+        ],
+        compiler_params=pltpu.CompilerParams(vmem_limit_bytes=32 << 20),
+        cost_estimate=pl.CostEstimate(
+            flops=2 * rows * width * width, bytes_accessed=12 * rows * width, transcendentals=0
+        ),
+        name="project",
+    )(heads, weight, bias, tokens, modulation)
+
+
+def middle_kernel(
+    tokens_ref,
+    branch_ref,
+    two_a_ref,
+    two_b_ref,
+    back_a_ref,
+    back_b_ref,
+    grad_ref,
+    mod_ref,
+    bias_ref,
+    weight_ref,
+    result_ref,
+    middle_grad_ref,
+    one_ref,
+    heads_ref,
+    sums_ref,
+    *,
+    unit_steps,
+):
+    gate_one, scale_two, gate_two = mod_ref[0, 2:3], mod_ref[0, 4:5], mod_ref[0, 5:6]
+    branch_one = branch_ref[...]
+    middle = tokens_ref[...].astype(f32) + gate_one * branch_one
+    normed, inverse = layer_norm(middle)
+    branch_two = two_a_ref[...] + two_b_ref[...] + bias_ref[...]
+    grad = grad_ref[...].astype(f32)
+    result_ref[...] = (middle + gate_two * branch_two).astype(bf16)
+    back = back_a_ref[...] + back_b_ref[...]
+    grad_middle = grad + norm_back(back * (1.0 + scale_two), normed, inverse)
+    middle_grad_ref[...] = grad_middle
+    grad_one = (gate_one * grad_middle).astype(bf16)
+    one_ref[...] = grad_one
+    heads = dot_nt(grad_one, weight_ref[...]).astype(bf16)
+    lanes = heads_ref.shape[2]
+    for part in range(heads_ref.shape[0]):
+        heads_ref[part] = heads[:, part * lanes : (part + 1) * lanes]
+
+    @pl.when(pl.program_id(0) % unit_steps == 0)
+    def _():
+        sums_ref[...] = jnp.zeros_like(sums_ref)
+
+    for row, values in enumerate(
+        (grad_middle * branch_one, back, back * normed, grad * branch_two, grad_one.astype(f32))
+    ):
+        sums_ref[0, row : row + 1] += jnp.sum(values, axis=0, keepdims=True)
+
+
+def middle_back(
+    tokens, branch_one, two_a, two_b, back_a, back_b, grad, modulation, bias, weight, frame_parts
+):
+    rows, width = tokens.shape
+    units = modulation.shape[0]
+    unit_steps = rows // units // ROWS
+    lanes = width // frame_parts
+    block = pl.BlockSpec((ROWS, width), lambda n: (n, 0))
+    return pl.pallas_call(
+        partial(middle_kernel, unit_steps=unit_steps),
+        grid=(rows // ROWS,),
+        in_specs=[block] * 7
+        + [
+            pl.BlockSpec((1, 6, width), lambda n: (n // unit_steps, 0, 0)),
+            pl.BlockSpec((1, width), lambda n: (0, 0)),
+            pl.BlockSpec((width, width), lambda n: (0, 0)),
+        ],
+        out_specs=[
+            block,
+            block,
+            block,
+            pl.BlockSpec((frame_parts, ROWS, lanes), lambda n: (0, n, 0)),
+            pl.BlockSpec((1, 8, width), lambda n: (n // unit_steps, 0, 0)),
+        ],
+        out_shape=[
+            jax.ShapeDtypeStruct((rows, width), bf16),
+            jax.ShapeDtypeStruct((rows, width), f32),
+            jax.ShapeDtypeStruct((rows, width), bf16),
+            jax.ShapeDtypeStruct((frame_parts, rows, lanes), bf16),
+            jax.ShapeDtypeStruct((units, 8, width), f32),
+        ],
+        compiler_params=pltpu.CompilerParams(vmem_limit_bytes=40 << 20),
+        cost_estimate=pl.CostEstimate(
+            flops=2 * rows * width * width, bytes_accessed=40 * rows * width, transcendentals=0
+        ),
+        name="middle_back",
+    )(tokens, branch_one, two_a, two_b, back_a, back_b, grad, modulation, bias, weight)
+
+
+def add_pairs_kernel(*refs):
+    out_ref = refs[-1]
+    row = 0
+    for pair in range(len(refs) // 2):
+        left, right = refs[2 * pair], refs[2 * pair + 1]
+        size = left.shape[2]
+        out_ref[:, :, row : row + size, :] = left[...] + right[...]
+        row += size
+
+
+def add_pairs(*pairs):
+    chips, shards, _, width = pairs[0].shape
+    rows = sum(values.shape[2] for values in pairs[::2])
+
+    def spec(size):
+        return pl.BlockSpec((1, shards, size, width), lambda n: (n, 0, 0, 0))
+
+    return pl.pallas_call(
+        add_pairs_kernel,
+        grid=(chips,),
+        in_specs=[spec(values.shape[2]) for values in pairs],
+        out_specs=spec(rows),
+        out_shape=jax.ShapeDtypeStruct((chips, shards, rows, width), bf16),
+        compiler_params=pltpu.CompilerParams(vmem_limit_bytes=32 << 20),
+        cost_estimate=pl.CostEstimate(
+            flops=0, bytes_accessed=6 * chips * shards * rows * width, transcendentals=0
+        ),
+        name="add_pairs",
+    )(*pairs)
 
 
 def mlp_kernel(
@@ -529,9 +760,8 @@
             clip_count, local_frames, local_patches, model_width
         )
 
-    def core_sum(keep, send):
-        got = lax.ppermute(send, "frame", [(i, i ^ 1) for i in range(frame_devices)])
-        return keep + got
+    def core_swap(values):
+        return lax.ppermute(values, "frame", [(i, i ^ 1) for i in range(frame_devices)])
 
     def scatter(values):
         return lax.psum_scatter(
@@ -544,9 +774,8 @@
 
     def frame_parts(values):
         return (
-            lax.all_gather(values.astype(bf16), "frame", axis=0, tiled=True)
+            lax.all_gather(values, "frame", axis=0, tiled=True)
             .reshape(frame_devices, -1, model_width)
-            .astype(f32)
         )
 
     unit_tokens = to_units(tokens)
@@ -696,7 +925,7 @@
     )
     heads_a, *second_list = lax.optimization_barrier((heads_a, *second_list))
     second_parts = from_relative(second_list)
-    upstream = to_units(after(cotangent, second_parts)).astype(f32)
+    upstream = to_units(after(cotangent, second_parts))
     heads_b, lse_b = attend(
         queries, keys_all, values_t, frame_ids, head_count, patch_count, cut, steps,
         (second_parts,),
@@ -706,47 +935,40 @@
     second_all = lax.all_gather(
         second_parts.reshape(-1, model_width), "frame", axis=0, tiled=True
     ).reshape(frame_devices, tensor_count, -1, model_width)
-    attended = (
-        swap_frame(attended_heads.reshape(frame_devices, own_rows, lanes))
-        .transpose(1, 0, 2)
-        .reshape(own_rows, model_width)
-    )
-
-    grad_two = (gate_two * upstream).astype(bf16).reshape(own_rows, model_width)
+    heads_here = swap_frame(attended_heads.reshape(frame_devices, own_rows, lanes))
+
+    grad_two = (gate_two * upstream.astype(f32)).astype(bf16).reshape(own_rows, model_width)
     grad_down_bias = jnp.sum(grad_two.astype(f32), axis=0)
 
-    branch_one = dot(attended, out_full).reshape(unit_shape) + out_bias.astype(f32)
-    middle = token_values + gate_one * branch_one
-    normed_two, inverse_two = layer_norm(middle)
-    hidden_two = (normed_two * (1.0 + scale_two) + shift_two).astype(bf16)
-    hidden_two = hidden_two.reshape(own_rows, model_width)
+    flat_tokens = unit_tokens.reshape(own_rows, model_width)
+    attended, branch_one, hidden_two = project(
+        heads_here, out_full, out_bias.astype(f32)[None, :], flat_tokens, modulation
+    )
 
     core_id = core.astype(jnp.int32).reshape(1)
     branch_a, back_a, keep_a, send_a, keep_bias_a, send_bias_a = mlp(
         core_id, hidden_two, grad_two, first_bias, first_all, half
     )
-    first_half = core_sum(keep_a, send_a)
+    got_a = core_swap(send_a)
     branch_b, back_b, keep_b, send_b, keep_bias_b, send_bias_b = mlp(
         core_id, hidden_two, grad_two, second_bias, second_all, half
     )
-    second_half = core_sum(keep_b, send_b)
-    back_b, first_half = lax.optimization_barrier((back_b, first_half))
+    got_b = core_swap(send_b)
+    got_a, branch_b = lax.optimization_barrier((got_a, branch_b))
+    back_b, first_half = lax.optimization_barrier((back_b, add_pairs(keep_a, got_a)))
     first_sum = scatter(first_half)
-    branch_two = (branch_a + branch_b).reshape(unit_shape) + down_bias.astype(f32)
-    result = from_units((middle + gate_two * branch_two).astype(bf16))
-    grad_gate_two = jnp.sum(upstream * branch_two, axis=1)
-    grad_hidden_two = (back_a + back_b).reshape(unit_shape)
-    grad_scale_two = jnp.sum(grad_hidden_two * normed_two, axis=1)
-    grad_shift_two = jnp.sum(grad_hidden_two, axis=1)
-    grad_middle = upstream + norm_back(grad_hidden_two * (1.0 + scale_two), normed_two, inverse_two)
-    grad_branch_one = (gate_one * grad_middle).astype(bf16)
-    grad_gate_one = jnp.sum(grad_middle * branch_one, axis=1)
-    grad_one = grad_branch_one.reshape(own_rows, model_width)
-    grad_out_bias = jnp.sum(grad_one.astype(f32), axis=0)
-    grad_attended = dot_nt(grad_one, out_full).astype(bf16)
-    grad_heads = swap_frame(
-        grad_attended.reshape(own_rows, frame_devices, lanes).transpose(1, 0, 2)
-    ).reshape(all_rows, lanes)
+    result, grad_middle, grad_one, head_grads, unit_sums = middle_back(
+        flat_tokens, branch_one, branch_a, branch_b, back_a, back_b,
+        upstream.reshape(own_rows, model_width), modulation, down_bias.astype(f32)[None, :],
+        out_full, frame_devices,
+    )
+    grad_heads = swap_frame(head_grads).reshape(all_rows, lanes)
+    result = from_units(result.reshape(unit_shape))
+    grad_middle = grad_middle.reshape(unit_shape)
+    grad_gate_one, grad_shift_two, grad_scale_two, grad_gate_two = (
+        unit_sums[:, n] for n in range(4)
+    )
+    grad_out_bias = jnp.sum(unit_sums[:, 4], axis=0)
 
     grad_out = (
         dot_tn(attended, grad_one)
@@ -788,19 +1010,22 @@
     out_pairs = jnp.concatenate([grad_out, bias_row], axis=2).reshape(
         chips, 2, tensor_count, out_rows + 16, model_width
     )
-    out_half = core_sum(
+    late_half = add_pairs(
+        keep_b,
+        got_b,
         lax.dynamic_index_in_dim(out_pairs, core, 1, keepdims=False),
-        lax.dynamic_index_in_dim(out_pairs, 1 - core, 1, keepdims=False),
-    )
-    late_half = jnp.concatenate([second_half, out_half], axis=2)
+        core_swap(lax.dynamic_index_in_dim(out_pairs, 1 - core, 1, keepdims=False)),
+    )
     late_sum = scatter(late_half)
-    first_total = tensor_sum(to_relative(first_sum)).astype(bf16)
+    first_list = exchange(to_relative(first_sum))
 
     keys_t = keys_all.T
     grad_q_a, *sums = attend_back(
         queries, keys_all, values_all, keys_t, attended_heads, row_lse, grad_heads,
         frame_ids, head_count, patch_count, 0, cut, (), f32, (late_half, result),
     )
+    *sums, first_list = lax.optimization_barrier((*sums, first_list))
+    first_total = sum(part.astype(f32) for part in first_list).astype(bf16)
     grad_q_b, grad_k_all, grad_v_all = attend_back(
         queries, keys_all, values_all, keys_t, attended_heads, row_lse, grad_heads,
         frame_ids, head_count, patch_count, cut, steps, tuple(sums), bf16, (first_total,),
@@ -838,50 +1063,14 @@
         grad_middle
         + norm_back(grad_hidden_one * (1.0 + scale_one), normed_one, inverse_one)
     ).astype(bf16)
-    tail_sums, grad_tokens = lax.optimization_barrier(
-        (jnp.concatenate([first_total, late_total]), grad_tokens)
+    tail_sums, slots_total, grad_tokens = lax.optimization_barrier(
+        (jnp.concatenate([first_total, late_total]), slots_total, grad_tokens)
     )
     tail_all = frame_parts(tail_sums)
-    slots_sum = frame_parts(slots_total)
-    late_tail = tail_all[:, 2 * half :]
-    first_tail = tail_all[:, : 2 * half]
-    up_first, down_first = first_tail[:, :half], first_tail[:, half:]
-    up_second, down_second = late_tail[:, :half], late_tail[:, half : 2 * half]
-    tail_out = late_tail[:, 2 * half : 2 * half + out_rows]
-    tail_bias = late_tail[:, 2 * half + out_rows :]
-    final_up = (
-        jnp.concatenate([up_first, up_second], axis=1)
-        .reshape(frame_devices * hidden_part, model_width)
-        .transpose(1, 0)
-    )
-    final_down = jnp.concatenate([down_first, down_second], axis=1).reshape(down_weight.shape)
-    final_out = tail_out.reshape(out_weight.shape)
-    tail_bias = tail_bias[:, 0]
-    final_down_bias = tail_bias[:, :width_part].reshape(model_width)
-    final_out_bias = tail_bias[:, width_part : 2 * width_part].reshape(model_width)
-    final_up_bias = tail_bias[:, 2 * width_part : 2 * width_part + hidden_part].reshape(
-        up_bias.shape
-    )
-    slots_sum, final_up, final_down, final_out = lax.optimization_barrier(
-        (slots_sum, final_up, final_down, final_out)
-    )
-    slots_sum = jnp.sum(
-        slots_sum.reshape(shard_groups, shard_heads, -1, model_width), axis=0
-    )
-    final_qkv = (
-        slots_sum[:, : 3 * HD]
-        .reshape(shard_heads, 3, HD, model_width)
-        .transpose(3, 1, 0, 2)
-        .reshape(qkv_weight.shape)
-    )
-    final_qv_bias = (
-        slots_sum[:, 3 * HD, : 2 * HD]
-        .reshape(shard_heads, 2, HD)
-        .transpose(1, 0, 2)
-        .reshape(qv_bias.shape)
-    )
-
-    grad_tokens = from_units(grad_tokens).astype(f32)
+    slots_all = frame_parts(slots_total).reshape(
+        shard_groups, shard_heads, -1, model_width
+    )
+    grad_tokens = from_units(grad_tokens)
     grad_modulation = jnp.stack(
         [
             grad_shift_one,
@@ -918,9 +1107,23 @@
         "ud,ukj->dkj", act_all.astype(f32), grad_mod_all, precision=lax.Precision.HIGH
     )
     grad_ada_bias = jnp.sum(grad_mod_all, axis=0)
+    final_up, final_down, final_out = unpack(tail_all, half, out_rows, (grad_tokens,))
+    tail_bias = tail_all[:, 4 * half + out_rows].astype(f32)
+    final_down_bias = tail_bias[:, :width_part].reshape(model_width)
+    final_out_bias = tail_bias[:, width_part : 2 * width_part].reshape(model_width)
+    final_up_bias = tail_bias[:, 2 * width_part : 2 * width_part + hidden_part].reshape(
+        up_bias.shape
+    )
+    final_qkv = unpack_heads(slots_all, (grad_ada_bias, final_up)).transpose(1, 0, 2)
+    final_qv_bias = (
+        jnp.sum(slots_all[:, :, 3 * HD, : 2 * HD].astype(f32), axis=0)
+        .reshape(shard_heads, 2, HD)
+        .transpose(1, 0, 2)
+        .reshape(qv_bias.shape)
+    )
     return (
         result,
-        grad_tokens,
+        grad_tokens.astype(f32),
         grad_ada_weight,
         grad_ada_bias,
         final_qkv,

time: 643 us -> 597 us (0.928)
  other arithmetic: 74.3 us -> 36.8 us
  Pallas kernels: 146 us -> 173 us
  waiting for transfers between devices: 200 us -> 183 us
  matrix products: 41.3 us -> 30 us
  local copies, waits for them, and re-layouts: 87 us -> 78.6 us
    ppermute x30, waiting for transfers between devices: 114 us -> 81.9 us  [shifted(): lax.ppermute(values, 'tensor', [(t, (t + shift) % tensor_count) for t in...]
    pallas_call x0 -> x6, Pallas kernels: none -> 26.7 us  [the longest x1 8.66 us: middle_back(): pl.pallas_call(partial(middle_kernel, unit_steps=unit_steps), grid=(rows...]
    add x3 -> x0, other arithmetic: 13.5 us -> none  [core_sum(): return keep + got]
    all_gather x2, waiting for transfers between devices: 33.4 us -> 46.1 us  [frame_parts(): lax.all_gather(values, 'frame', axis=0, tiled=True)]
    concatenate x3 -> x0, other arithmetic: 9.92 us -> none  [the longest x1 4.19 us: on_device(): jnp.concatenate([down_first, down_second], axis=1)]
    slice x6 -> x2, local copies, waits for them, and re-layouts: 11.5 us -> 1.66 us  [the longest x1 1.66 us: on_device(): first_pack = jnp.concatenate([up_part[:half], down_part[:half], bias_part])]
    reduce_sum x6 -> x4, other arithmetic: 16 us -> 6.43 us  [the longest x1 3.66 us: on_device(): grad_shift_one = jnp.sum(grad_hidden_one, axis=1)]
    unnamed x183 -> x193, local copies, waits for them, and re-layouts: 30.7 us -> 40 us
  transfers between devices with their start and end apart: 47 -> 47, of which waited for: 16 -> 14; matrix products, arithmetic and copies ran while one was open for 23% -> 18% of each run, Pallas kernels for 20% -> 28%
where the time goes in v3:
time: 597 us; the launch traced here: 586 us
  waiting for transfers between devices  183 us (31%)
  Pallas kernels  173 us (29%)
  local copies, waits for them, and re-layouts  78.6 us (13%)
  starting transfers between devices  58.9 us (10%)
  other arithmetic  36.8 us (6%)
  matrix products  30 us (5%)
  between operations  16.3 us (3%)
  blocking collectives  9.85 us (2%)
    ppermute x30, waiting for transfers between devices, shifted(): lax.ppermute(values, 'tensor', [(t, (t + shift) % tensor_count) for t in...  81.9 us
    pallas_call x2, Pallas kernels, attend_back(): pl.pallas_call(partial(attend_back_kernel, head_count=head_count, patch_c...  62.2 us
    all_gather x2, waiting for transfers between devices, frame_parts(): lax.all_gather(values, 'frame', axis=0, tiled=True)  46.1 us
    ppermute x30, starting transfers between devices, shifted(): lax.ppermute(values, 'tensor', [(t, (t + shift) % tensor_count) for t in...  45 us
    pallas_call x2, Pallas kernels, attend(): pl.pallas_call(partial(attend_kernel, head_count=head_count, patch_count=...  42.6 us
    pallas_call x2, Pallas kernels, mlp(): pl.pallas_call(mlp_kernel, grid_spec=pltpu.PrefetchScalarGridSpec(num_sca...  41.1 us
    unnamed x193, local copies, waits for them, and re-layouts  40 us
    ppermute x2, waiting for transfers between devices, to_owners(): total = total + lax.ppermute(piece, ('frame', 'tensor'), pairs).astype(f32)  28.1 us
  transfers between devices with their start and end apart: 47, of which 14 were waited for; matrix products, arithmetic and copies ran while one was open for 18% of the time, Pallas kernels for 28%

profile of v3, /device:TPU:0, one launch (start us, length us, event | category | flops | bytes accessed | tf_op | source)
XLA Modules:
  0.0 585.7 jit_solution(12109652681499367560)
XLA Ops:
  20.6 5.4 collective-permute-done
  26.0 16.3 %collective-permute-done.1 = bf16[2,64,1024]{2,1,0:T(8,128)(2,1)S(1)} collective-permute-done((bf16[2,64,1024]{2,1,0:T(8,128)(2,1)S(1)}, bf16[2,64,1024]{2,1,0:T(8,128)(2,1)S(1)}, u32[]{:S(2)}, u32[]{:S(2)}) %collective-permute-start.1) | collective-permute-done | bytes 262176 | tf_op jit(solution)/shard_map/ppermute | solution.py:695
  52.8 5.4 collective-permute-done.11
  58.2 24.3 %collective-permute-done.12 = bf16[176,1024]{1,0:T(8,128)(2,1)S(1)} collective-permute-done((bf16[176,1024]{1,0:T(8,128)(2,1)S(1)}, bf16[176,1024]{1,0:T(8,128)(2,1)S(1)}, u32[]{:S(2)}, u32[]{:S(2)}) %collective-permute-start.12) | collective-permute-done | bytes 360480 | tf_op jit(solution)/shard_map/ppermute | solution.py:695
  86.9 18.8 %collective-permute-done.7 = bf16[208,1024]{1,0:T(8,128)(2,1)S(1)} collective-permute-done((bf16[208,1024]{1,0:T(8,128)(2,1)S(1)}, bf16[208,1024]{1,0:T(8,128)(2,1)S(1)}, u32[]{:S(2)}, u32[]{:S(2)}) %collective-permute-start.7) | collective-permute-done | bytes 426016 | tf_op jit(solution)/shard_map/ppermute | solution.py:739
  107.1 8.1 %add_convert_fusion = bf16[4096,384]{0,1:T(8,128)(2,1)S(1)} fusion(bf16[4096,1024]{1,0:T(8,128)(2,1)} %all-gather.6.cloned.1.call-done, bf16[384,1024]{1,0:T(8,128)(2,1)} %bitcast.359, f32[384]{0:T(512)S(1)} %pad_maximum_fusion.12), kind=kOutput, calls=%fused_computation.1 | convolution fusion | flops 3224371200 | bytes 12322304 | tf_op jit(solution)/shard_map/dot_general | solution.py:47
  125.6 22.2 %attend.2 = (bf16[2816,128]{1,0:T(8,128)(2,1)S(1)}, f32[11,1,512]{2,1,0:T(1,128)S(1)}) custom-call(s32[16]{0:T(128)S(1)} %fusion.58.frame_ids, bf16[4096,128]{1,0:T(8,128)(2,1)S(1)} %copy.93.q_ref, bf16[4096,128]{1,0:T(8,128)(2,1)S(1)} %copy.94.k_ref, bf16[128,4096]{1,0:T(8,128)(2,1)S(1)} %copy-done.44), custom_call_target="tpu_custom_call" | custom-call | flops 6576668672 | bytes 2883584 | tf_op jit(solution)/shard_map/attend/pallas_call | solution.py:141
  162.7 20.3 %attend.3 = (bf16[1280,128]{1,0:T(8,128)(2,1)S(1)}, f32[5,1,512]{2,1,0:T(1,128)S(1)}) custom-call(s32[16]{0:T(128)S(1)} %fusion.58.frame_ids, bf16[4096,128]{1,0:T(8,128)(2,1)S(1)} %copy-done.35, bf16[4096,128]{1,0:T(8,128)(2,1)S(1)} %copy-done.39, bf16[128,4096]{1,0:T(8,128)(2,1)S(1)} %copy-done.45, bf16[4,128,1024]{2,1,0:T(8,128)(2,1)S(1)} %copy-done.12), custom_call_target="tpu_custom_call" | custom-call | flops 4697620480 | bytes 1310720 | tf_op jit(solution)/shard_map/attend/pallas_call | solution.py:141
  184.1 5.7 all-to-all-start
  201.5 3.8 all-to-all-done.heads_ref
  205.3 4.2 project.1
  211.9 20.8 %mlp.2 = (f32[512,1024]{1,0:T(8,128)}, f32[512,1024]{1,0:T(8,128)}, bf16[4,4,128,1024]{3,2,1,0:T(8,128)(2,1)}, bf16[4,4,128,1024]{3,2,1,0:T(8,128)(2,1)}, f32[4,...) custom-call(s32[1]{0:T(128)} %bitcast.52.core_ref, bf16[512,1024]{1,0:T(8,128)(2,1)S(1)} %get-tuple-element.79.hidden_ref, ...), custom_call_target="tpu_custom_call" | custom-call | flops 12884901888 | bytes 16777216 | tf_op jit(solution)/shard_map/mlp/pallas_call | solution.py:609
  238.7 20.3 %mlp.3 = (f32[512,1024]{1,0:T(8,128)}, f32[512,1024]{1,0:T(8,128)}, bf16[4,4,128,1024]{3,2,1,0:T(8,128)(2,1)}, bf16[4,4,128,1024]{3,2,1,0:T(8,128)(2,1)}, f32[4,...) custom-call(s32[1]{0:T(128)} %bitcast.52.core_ref, bf16[512,1024]{1,0:T(8,128)(2,1)S(1)} %copy-done.31, ...), custom_call_target="tpu_custom_call" | custom-call | flops 12884901888 | bytes 16777216 | tf_op jit(solution)/shard_map/mlp/pallas_call | solution.py:609
  259.1 3.4 add_pairs.2
  275.5 8.7 %middle_back.1 = (bf16[512,1024]{1,0:T(8,128)(2,1)S(1)}, f32[512,1024]{1,0:T(8,128)S(1)}, bf16[512,1024]{1,0:T(8,128)(2,1)S(1)}, bf16[8,512,128]{2,1,0:T(8,128)(2,1)}, f32[2,8,1024]{2,1,0:T(8,128)S(1)}) custom-call(bf16[512,1024]{1,0:T(8,128)(2,1)S(1)} %bitcast.315, f32[512,1024]{1,0:T(8,128)S(1)} %copy-done.25, f32[512,1024]{1,0:T(8,128)S(1)} %copy-done.26, ...), custom_call_target="tpu_custom_call" | custom-call | flops 1073741824 | bytes 20971520 | tf_op jit(solution)/shard_map/middle_back/pallas_call | solution.py:468
  300.1 3.5 collective-permute-start.18
  305.0 4.4 all-to-all-start.1
  311.6 15.2 %collective-permute-done.19 = bf16[2,64,1024]{2,1,0:T(8,128)(2,1)S(1)} collective-permute-done((bf16[2,64,1024]{2,1,0:T(8,128)(2,1)}, bf16[2,64,1024]{2,1,0:T(8,128)(2,1)S(1)}, u32[]{:S(2)}, u32[]{:S(2)}) %collective-permute-start.19) | collective-permute-done | bytes 262176 | tf_op jit(solution)/shard_map/ppermute | solution.py:695
  340.3 31.6 %attend_back.2 = (bf16[2816,128]{1,0:T(8,128)(2,1)S(1)}, f32[4096,128]{1,0:T(8,128)}, f32[4096,128]{1,0:T(8,128)}) custom-call(s32[16]{0:T(128)S(1)} %fusion.58.frame_ids, bf16[4096,128]{1,0:T(8,128)(2,1)S(1)} %copy-done.36, bf16[4096,128]{1,0:T(8,128)(2,1)} %bitcast.75.grad_ref, bf16[4096,128]{1,0:T(8,128)(2,1)S(1)} %copy-done.19, ...), custom_call_target="tpu_custom_call" | custom-call | flops 16441671680 | bytes 5767168 | tf_op jit(solution)/shard_map/attend_back/pallas_call | solution.py:254
  374.3 30.6 %attend_back.3 = (bf16[1280,128]{1,0:T(8,128)(2,1)S(1)}, bf16[4096,128]{1,0:T(8,128)(2,1)S(1)}, bf16[4096,128]{1,0:T(8,128)(2,1)S(1)}) custom-call(s32[16]{0:T(128)S(1)} %fusion.58.frame_ids, bf16[4096,128]{1,0:T(8,128)(2,1)S(1)} %copy-done.37, bf16[4096,128]{1,0:T(8,128)(2,1)} %bitcast.75.grad_ref, bf16[4096,128]{1,0:T(8,128)(2,1)S(1)} %copy-done.19, ...), custom_call_target="tpu_custom_call" | custom-call | flops 11744051200 | bytes 2621440 | tf_op jit(solution)/shard_map/attend_back/pallas_call | solution.py:254
  405.9 8.6 %convolution_convert_fusion = bf16[4096,1024]{1,0:T(8,128)(2,1)} fusion(bf16[384,1024]{1,0:T(8,128)(2,1)S(1)} %bitcast.360, bf16[4096,128]{1,0:T(8,128)(2,1)S(1)} %get-tuple-element.115, bf16[4096,128]{1,0:T(8,128)(2,1)S(1)} %get-tuple-element.114, bf16[1280,128]{1,0:T(8,128)(2,1)S(1)} %get-tuple-element.113, bf16[2816,128]{1,0:T(8,128)(2,1)S(1)} %get-tuple-element.110), kind=kOutput, calls=%fused_computation | convolution fusion | flops 3238002688 | bytes 12320768 | tf_op jit(solution)/shard_map/dot_general | solution.py:43
  417.0 5.1 pad_maximum_fusion.1
  422.1 6.9 %convolution_convert_fusion.2 = bf16[384,1024]{1,0:T(8,128)(2,1)S(1)} fusion(bf16[4096,384]{1,0:T(8,128)(2,1)S(1)} %pad_maximum_fusion.1, bf16[4096,1024]{1,0:T(8,128)(2,1)} %all-gather.6.cloned.1.call-done), kind=kOutput, calls=%fused_computation.40 | convolution fusion | flops 3221618688 | bytes 12320768 | tf_op jit(solution)/shard_map/dot_general | solution.py:51
  432.8 3.3 collective-permute-start.28
  437.3 28.1 %collective-permute-done.30 = bf16[208,1024]{1,0:T(8,128)(2,1)S(1)} collective-permute-done((bf16[208,1024]{1,0:T(8,128)(2,1)S(1)}, bf16[208,1024]{1,0:T(8,128)(2,1)S(1)}, u32[]{:S(2)}, u32[]{:S(2)}) %collective-permute-start.30) | collective-permute-done | bytes 426016 | tf_op jit(solution)/shard_map/ppermute | solution.py:748
  466.4 14.5 %collective-permute-done.27 = bf16[176,1024]{1,0:T(8,128)(2,1)} collective-permute-done((bf16[176,1024]{1,0:T(8,128)(2,1)S(1)}, bf16[176,1024]{1,0:T(8,128)(2,1)}, u32[]{:S(2)}, u32[]{:S(2)}) %collective-permute-start.27) | collective-permute-done | bytes 360480 | tf_op jit(solution)/shard_map/ppermute | solution.py:695
  485.4 3.7 bitcast_reduce_fusion
  499.9 9.8 %all_gather.21 = f32[64,1664]{1,0:T(8,128)S(1)} all-gather(f32[8,1664]{1,0:T(8,128)S(1)} %reshape.363), channel_id=1, replica_groups=mesh['frame'=8,'tensor'=4] {'frame'}, dimensions={0}, use_global_device_ids=true | all-gather | bytes 479232 | tf_op jit(solution)/shard_map/all_gather | solution.py:1101
  510.5 4.6 fusion.28
  517.4 5.1 all-gather.12.cloned.1.call-done
  524.0 41.0 %all-gather.14.cloned.1.call-done = bf16[2432,1024]{1,0:T(8,128)(2,1)} async-done(((bf16[304,1024]{1,0:T(8,128)(2,1)}), bf16[2432,1024]{1,0:T(8,128)(2,1)}) %all-gather.14.cloned.1.call-update) | async-done | bytes 4980752 | tf_op jit(solution)/shard_map/all_gather | solution.py:777
  569.0 4.8 unpack.1
  (432 shorter events, 160.6 us)
Async XLA Ops:
  7.2 99.9 %all-gather.6.cloned.1.call-start = ((), (), s32[]{:S(2)}) async-start(), calls=%async_computation.5 | async-start | bytes 9437184 | tf_op jit(solution)/shard_map/all_gather | solution.py:848
  18.6 23.7 %collective-permute-start.1 = (bf16[2,64,1024]{2,1,0:T(8,128)(2,1)S(1)}, bf16[2,64,1024]{2,1,0:T(8,128)(2,1)S(1)}, u32[]{:S(2)}, u32[]{:S(2)}) collective-permute-start(bf16[2,64,1024]{2,1,0:T(8,128)(2,1)S(1)} %get-tuple-element.164), channel_id=1, source_target_pairs={{0,2},{1,3},{2,0},{3,1},{4,6},{5,7},{6,4},{7,5},{8,10},{9,11},{10,... | collective-permute-start | bytes 786440 | tf_op jit(solution)/shard_map/ppermute | solution.py:695
  20.2 22.0 %collective-permute-start.2 = (bf16[2,64,1024]{2,1,0:T(8,128)(2,1)S(1)}, bf16[2,64,1024]{2,1,0:T(8,128)(2,1)S(1)}, u32[]{:S(2)}, u32[]{:S(2)}) collective-permute-start(bf16[2,64,1024]{2,1,0:T(8,128)(2,1)S(1)} %get-tuple-element.166), channel_id=1, source_target_pairs={{0,1},{1,2},{2,3},{3,0},{4,5},{5,6},{6,7},{7,4},{8,9},{9,10},{10,1... | collective-permute-start | bytes 786440 | tf_op jit(solution)/shard_map/ppermute | solution.py:695
  44.7 148.8 %all-gather.8.cloned.1.call-start = ((), (), s32[]{:S(2)}) async-start(), calls=%async_computation.6 | async-start | bytes 12976128 | tf_op jit(solution)/shard_map/all_gather | solution.py:852
  49.3 33.2 %collective-permute-start.13 = (bf16[176,1024]{1,0:T(8,128)(2,1)S(1)}, bf16[176,1024]{1,0:T(8,128)(2,1)S(1)}, u32[]{:S(2)}, u32[]{:S(2)}) collective-permute-start(bf16[176,1024]{1,0:T(8,128)(2,1)S(1)} %fusion.32), channel_id=1, source_target_pairs={{0,1},{1,2},{2,3},{3,0},{4,5},{5,6},{6,7},{7,4},{8,9},{9,10},{10,1... | collective-permute-start | bytes 1081352 | tf_op jit(solution)/shard_map/ppermute | solution.py:695
  51.3 31.2 %collective-permute-start.12 = (bf16[176,1024]{1,0:T(8,128)(2,1)S(1)}, bf16[176,1024]{1,0:T(8,128)(2,1)S(1)}, u32[]{:S(2)}, u32[]{:S(2)}) collective-permute-start(bf16[176,1024]{1,0:T(8,128)(2,1)S(1)} %fusion.32), channel_id=1, source_target_pairs={{0,2},{1,3},{2,0},{3,1},{4,6},{5,7},{6,4},{7,5},{8,10},{9,11},{10,... | collective-permute-start | bytes 1081352 | tf_op jit(solution)/shard_map/ppermute | solution.py:695
  84.1 152.2 %all-gather.10.cloned.1.call-start = ((), (), s32[]{:S(2)}) async-start(), calls=%async_computation.7 | async-start | bytes 9437184 | tf_op jit(solution)/shard_map/all_gather | solution.py:935
  86.1 19.6 %collective-permute-start.7 = (bf16[208,1024]{1,0:T(8,128)(2,1)S(1)}, bf16[208,1024]{1,0:T(8,128)(2,1)S(1)}, u32[]{:S(2)}, u32[]{:S(2)}) collective-permute-start(bf16[208,1024]{1,0:T(8,128)(2,1)S(1)} %fusion.27), channel_id=1, source_target_pairs={{2,0},{3,1},{0,2},{1,3},{6,4},{7,5},{4,6},{5,7},{10,8},{11,9},{8,1... | collective-permute-start | bytes 1277960 | tf_op jit(solution)/shard_map/ppermute | solution.py:739
  117.5 30.4 %collective-permute-start.10 = (bf16[128,1024]{1,0:T(8,128)(2,1)S(1)}, bf16[128,1024]{1,0:T(8,128)(2,1)}, u32[]{:S(2)}, u32[]{:S(2)}) collective-permute-start(bf16[128,1024]{1,0:T(8,128)(2,1)S(1)} %pad_maximum_fusion.6), channel_id=1, source_target_pairs={{0,1},{1,2},{2,3},{3,0},{4,5},{5,6},{6,7},{7,4},{8,9},{9,10},{10,1... | collective-permute-start | bytes 786440 | tf_op jit(solution)/shard_map/ppermute | solution.py:695
  117.5 30.4 %collective-permute-start.9 = (bf16[128,1024]{1,0:T(8,128)(2,1)S(1)}, bf16[128,1024]{1,0:T(8,128)(2,1)}, u32[]{:S(2)}, u32[]{:S(2)}) collective-permute-start(bf16[128,1024]{1,0:T(8,128)(2,1)S(1)} %pad_maximum_fusion.6), channel_id=1, source_target_pairs={{0,2},{1,3},{2,0},{3,1},{4,6},{5,7},{6,4},{7,5},{8,10},{9,11},{10,... | collective-permute-start | bytes 786440 | tf_op jit(solution)/shard_map/ppermute | solution.py:695
  120.6 27.3 %collective-permute-start.8 = (bf16[128,1024]{1,0:T(8,128)(2,1)S(1)}, bf16[128,1024]{1,0:T(8,128)(2,1)}, u32[]{:S(2)}, u32[]{:S(2)}) collective-permute-start(bf16[128,1024]{1,0:T(8,128)(2,1)S(1)} %pad_maximum_fusion.6), channel_id=1, source_target_pairs={{0,3},{1,0},{2,1},{3,2},{4,7},{5,4},{6,5},{7,6},{8,11},{9,8},{10,9... | collective-permute-start | bytes 786440 | tf_op jit(solution)/shard_map/ppermute | solution.py:695
  157.4 32.7 %collective-permute-start.14 = (bf16[2,64,1024]{2,1,0:T(8,128)(2,1)}, bf16[2,64,1024]{2,1,0:T(8,128)(2,1)}, u32[]{:S(2)}, u32[]{:S(2)}) collective-permute-start(bf16[2,64,1024]{2,1,0:T(8,128)(2,1)} %get-tuple-element.159), channel_id=1, source_target_pairs={{0,3},{1,0},{2,1},{3,2},{4,7},{5,4},{6,5},{7,6},{8,11},{9,8},{10,9... | collective-permute-start | bytes 786440 | tf_op jit(solution)/shard_map/ppermute | solution.py:695
  158.1 32.1 %collective-permute-start.16 = (bf16[2,64,1024]{2,1,0:T(8,128)(2,1)}, bf16[2,64,1024]{2,1,0:T(8,128)(2,1)}, u32[]{:S(2)}, u32[]{:S(2)}) collective-permute-start(bf16[2,64,1024]{2,1,0:T(8,128)(2,1)} %get-tuple-element.161), channel_id=1, source_target_pairs={{0,1},{1,2},{2,3},{3,0},{4,5},{5,6},{6,7},{7,4},{8,9},{9,10},{10,1... | collective-permute-start | bytes 786440 | tf_op jit(solution)/shard_map/ppermute | solution.py:695
  159.5 30.7 %collective-permute-start.15 = (bf16[2,64,1024]{2,1,0:T(8,128)(2,1)}, bf16[2,64,1024]{2,1,0:T(8,128)(2,1)}, u32[]{:S(2)}, u32[]{:S(2)}) collective-permute-start(bf16[2,64,1024]{2,1,0:T(8,128)(2,1)} %get-tuple-element.162), channel_id=1, source_target_pairs={{0,2},{1,3},{2,0},{3,1},{4,6},{5,7},{6,4},{7,5},{8,10},{9,11},{10,... | collective-permute-start | bytes 786440 | tf_op jit(solution)/shard_map/ppermute | solution.py:695
  184.1 21.2 %all-to-all-start = ((bf16[8,512,128]{2,1,0:T(8,128)(2,1)}), bf16[8,512,128]{2,1,0:T(8,128)(2,1)}, u32[]{:S(2)}, u32[]{:S(2)}) async-start(bf16[8,512,128]{2,1,0:T(8,128)(2,1)} %bitcast.326), calls=%async_computation | async-start | bytes 2097152 | tf_op jit(solution)/shard_map/all_to_all | solution.py:692
  189.8 139.2 %reduce-scatter.4.cloned.1.call-start = ((), (), s32[]{:S(2)}) async-start(), calls=%async_computation.8 | async-start | bytes 5242880 | tf_op jit(solution)/shard_map/reduce_scatter | solution.py:767
  234.3 24.8 %collective-permute-start.17 = (bf16[4,4,128,1024]{3,2,1,0:T(8,128)(2,1)}, bf16[4,4,128,1024]{3,2,1,0:T(8,128)(2,1)}, u32[]{:S(2)}, u32[]{:S(2)}) collective-permute-start(bf16[4,4,128,1024]{3,2,1,0:T(8,128)(2,1)} %get-tuple-element.82), channel_id=1, source_target_pairs={{0,4},{4,0},{8,12},{12,8},{16,20},{20,16},{24,28},{28,24},{1,5},{5... | collective-permute-start | bytes 12582920 | tf_op jit(solution)/shard_map/ppermute | solution.py:764
  264.6 165.4 %reduce-scatter.6.cloned.1.call-start = ((), (), s32[]{:S(2)}) async-start(), calls=%async_computation.9 | async-start | bytes 7208960 | tf_op jit(solution)/shard_map/reduce_scatter | solution.py:767
  265.1 27.2 %collective-permute-start.21 = (bf16[4,4,128,1024]{3,2,1,0:T(8,128)(2,1)}, bf16[4,4,128,1024]{3,2,1,0:T(8,128)(2,1)}, u32[]{:S(2)}, u32[]{:S(2)}) collective-permute-start(bf16[4,4,128,1024]{3,2,1,0:T(8,128)(2,1)} %get-tuple-element.95), channel_id=1, source_target_pairs={{0,4},{4,0},{8,12},{12,8},{16,20},{20,16},{24,28},{28,24},{1,5},{5... | collective-permute-start | bytes 12582920 | tf_op jit(solution)/shard_map/ppermute | solution.py:764
  304.9 21.9 %collective-permute-start.19 = (bf16[2,64,1024]{2,1,0:T(8,128)(2,1)}, bf16[2,64,1024]{2,1,0:T(8,128)(2,1)S(1)}, u32[]{:S(2)}, u32[]{:S(2)}) collective-permute-start(bf16[2,64,1024]{2,1,0:T(8,128)(2,1)} %get-tuple-element.157), channel_id=1, source_target_pairs={{0,2},{1,3},{2,0},{3,1},{4,6},{5,7},{6,4},{7,5},{8,10},{9,11},{10,... | collective-permute-start | bytes 786440 | tf_op jit(solution)/shard_map/ppermute | solution.py:695
  305.0 32.6 %all-to-all-start.1 = ((bf16[8,512,128]{2,1,0:T(8,128)(2,1)}), bf16[8,512,128]{2,1,0:T(8,128)(2,1)}, u32[]{:S(2)}, u32[]{:S(2)}) async-start(bf16[8,512,128]{2,1,0:T(8,128)(2,1)} %get-tuple-element.91), calls=%async_computation.1 | async-start | bytes 2097152 | tf_op jit(solution)/shard_map/all_to_all | solution.py:692
  309.4 174.0 %reduce-scatter.8.cloned.1.call-start = ((), (), s32[]{:S(2)}) async-start(), calls=%async_computation.10 | async-start | bytes 9437184 | tf_op jit(solution)/shard_map/reduce_scatter | solution.py:1038
  331.1 40.8 %collective-permute-start.25 = (bf16[128,1024]{1,0:T(8,128)(2,1)}, bf16[128,1024]{1,0:T(8,128)(2,1)}, u32[]{:S(2)}, u32[]{:S(2)}) collective-permute-start(bf16[128,1024]{1,0:T(8,128)(2,1)} %get-tuple-element.153), channel_id=1, source_target_pairs={{0,1},{1,2},{2,3},{3,0},{4,5},{5,6},{6,7},{7,4},{8,9},{9,10},{10,1... | collective-permute-start | bytes 786440 | tf_op jit(solution)/shard_map/ppermute | solution.py:695
  332.6 39.4 %collective-permute-start.24 = (bf16[128,1024]{1,0:T(8,128)(2,1)}, bf16[128,1024]{1,0:T(8,128)(2,1)}, u32[]{:S(2)}, u32[]{:S(2)}) collective-permute-start(bf16[128,1024]{1,0:T(8,128)(2,1)} %get-tuple-element.154), channel_id=1, source_target_pairs={{0,2},{1,3},{2,0},{3,1},{4,6},{5,7},{6,4},{7,5},{8,10},{9,11},{10,... | collective-permute-start | bytes 786440 | tf_op jit(solution)/shard_map/ppermute | solution.py:695
  334.5 37.5 %collective-permute-start.23 = (bf16[128,1024]{1,0:T(8,128)(2,1)}, bf16[128,1024]{1,0:T(8,128)(2,1)}, u32[]{:S(2)}, u32[]{:S(2)}) collective-permute-start(bf16[128,1024]{1,0:T(8,128)(2,1)} %get-tuple-element.155), channel_id=1, source_target_pairs={{0,3},{1,0},{2,1},{3,2},{4,7},{5,4},{6,5},{7,6},{8,11},{9,8},{10,9... | collective-permute-start | bytes 786440 | tf_op jit(solution)/shard_map/ppermute | solution.py:695
  414.5 108.0 %all-gather.12.cloned.1.call-start = ((), (), s32[]{:S(2)}) async-start(), calls=%async_computation.11 | async-start | bytes 3833856 | tf_op jit(solution)/shard_map/all_gather | solution.py:777
  430.0 35.5 %collective-permute-start.30 = (bf16[208,1024]{1,0:T(8,128)(2,1)S(1)}, bf16[208,1024]{1,0:T(8,128)(2,1)S(1)}, u32[]{:S(2)}, u32[]{:S(2)}) collective-permute-start(bf16[208,1024]{1,0:T(8,128)(2,1)S(1)} %get-tuple-element.168), channel_id=1, source_target_pairs={{0,2},{1,3},{2,0},{3,1},{4,6},{5,7},{6,4},{7,5},{8,10},{9,11},{10,... | collective-permute-start | bytes 1277960 | tf_op jit(solution)/shard_map/ppermute | solution.py:748
  432.2 34.1 %collective-permute-start.26 = (bf16[176,1024]{1,0:T(8,128)(2,1)}, bf16[176,1024]{1,0:T(8,128)(2,1)}, u32[]{:S(2)}, u32[]{:S(2)}) collective-permute-start(bf16[176,1024]{1,0:T(8,128)(2,1)} %get-tuple-element.145), channel_id=1, source_target_pairs={{0,1},{1,2},{2,3},{3,0},{4,5},{5,6},{6,7},{7,4},{8,9},{9,10},{10,1... | collective-permute-start | bytes 1081352 | tf_op jit(solution)/shard_map/ppermute | solution.py:695
  432.8 33.6 %collective-permute-start.28 = (bf16[176,1024]{1,0:T(8,128)(2,1)}, bf16[176,1024]{1,0:T(8,128)(2,1)}, u32[]{:S(2)}, u32[]{:S(2)}) collective-permute-start(bf16[176,1024]{1,0:T(8,128)(2,1)} %get-tuple-element.146), channel_id=1, source_target_pairs={{0,3},{1,0},{2,1},{3,2},{4,7},{5,4},{6,5},{7,6},{8,11},{9,8},{10,9... | collective-permute-start | bytes 1081352 | tf_op jit(solution)/shard_map/ppermute | solution.py:695
  436.1 44.8 %collective-permute-start.27 = (bf16[176,1024]{1,0:T(8,128)(2,1)S(1)}, bf16[176,1024]{1,0:T(8,128)(2,1)}, u32[]{:S(2)}, u32[]{:S(2)}) collective-permute-start(bf16[176,1024]{1,0:T(8,128)(2,1)S(1)} %get-tuple-element.147), channel_id=1, source_target_pairs={{0,2},{1,3},{2,0},{3,1},{4,6},{5,7},{6,4},{7,5},{8,10},{9,11},{10,... | collective-permute-start | bytes 1081352 | tf_op jit(solution)/shard_map/ppermute | solution.py:695
  489.1 75.9 %all-gather.14.cloned.1.call-start = ((), (), s32[]{:S(2)}) async-start(), calls=%async_computation.12 | async-start | bytes 5603328 | tf_op jit(solution)/shard_map/all_gather | solution.py:777
  495.0 20.5 %collective-permute-start.33 = (bf16[2,64,1024]{2,1,0:T(8,128)(2,1)S(1)}, bf16[2,64,1024]{2,1,0:T(8,128)(2,1)S(1)}, u32[]{:S(2)}, u32[]{:S(2)}) collective-permute-start(bf16[2,64,1024]{2,1,0:T(8,128)(2,1)S(1)} %get-tuple-element.149), channel_id=1, source_target_pairs={{0,1},{1,2},{2,3},{3,0},{4,5},{5,6},{6,7},{7,4},{8,9},{9,10},{10,1... | collective-permute-start | bytes 786440 | tf_op jit(solution)/shard_map/ppermute | solution.py:695
  (91 other events, 906.5 us)
Sparse Core Ops, SparseCore 0:
  44.9 53.5 all-gather.5
  100.9 67.6 all-gather.7
  171.1 63.3 all-gather.9
  264.7 55.7 reduce-scatter.3
  324.2 73.6 reduce-scatter.5
  414.6 67.9 reduce-scatter.7
  489.2 33.2 all-gather.11
  525.0 40.0 all-gather.13

commit v4 on v3

--- a/solution.py
+++ b/solution.py
@@ -335,36 +335,67 @@
     )(tail, *waits)
 
 
-def unpack_heads_kernel(slots_ref, *refs):
-    out_ref = refs[-1]
-    groups, slots = slots_ref.shape[:2]
+def unpack_heads_kernel(
+    me_ref, left_ref, right_ref, *refs, left_order, right_order, slot_count, group_count
+):
+    out_ref, bias_ref = refs[-2:]
+    pair = out_ref.shape[2] // HD
+
+    def at(member, order):
+        place = 0
+        for stage, bit in enumerate(order):
+            place = place + ((member // bit) % 2) * (1 << stage)
+        return place
+
+    def total(slot, rows):
+        result = 0.0
+        for group in range(group_count):
+            member = (group * slot_count + slot) ^ me_ref[0]
+            left = left_ref[at(member, left_order), rows]
+            right = right_ref[at(member, right_order), rows]
+            result = result + jnp.concatenate([left, right], axis=1).astype(f32)
+        return result
+
+    first = pl.program_id(0) * pair
     for kind in range(3):
         rows = slice(kind * HD, (kind + 1) * HD)
-        pieces = []
-        for slot in range(slots):
-            total = slots_ref[0, slot, rows].astype(f32)
-            for group in range(1, groups):
-                total = total + slots_ref[group, slot, rows].astype(f32)
-            pieces.append(total)
+        pieces = [total(first + n, rows) for n in range(pair)]
         out_ref[kind] = jnp.swapaxes(jnp.concatenate(pieces, axis=0), 0, 1)
-
-
-def unpack_heads(slots, waits):
-    groups, count, rows, width = slots.shape
+    for n in range(pair):
+        bias_ref[n] = total(first + n, slice(3 * HD, 3 * HD + 16))[:8, :128]
+
+
+def unpack_heads(me, left, right, left_order, right_order, slot_count, waits):
+    frame_parts, rows, width = left.shape
     pair = 128 // HD
+    whole = pl.BlockSpec((frame_parts, rows, width), lambda n, m: (0, 0, 0))
     return pl.pallas_call(
-        unpack_heads_kernel,
-        grid=(count // pair,),
-        in_specs=[pl.BlockSpec((groups, pair, rows, width), lambda n: (0, n, 0, 0))]
-        + [pl.BlockSpec(memory_space=pl.ANY) for _ in waits],
-        out_specs=pl.BlockSpec((3, width, 128), lambda n: (0, 0, n)),
-        out_shape=jax.ShapeDtypeStruct((3, width, count * HD), f32),
+        partial(
+            unpack_heads_kernel,
+            left_order=left_order,
+            right_order=right_order,
+            slot_count=slot_count,
+            group_count=frame_parts // slot_count,
+        ),
+        grid_spec=pltpu.PrefetchScalarGridSpec(
+            num_scalar_prefetch=1,
+            grid=(slot_count // pair,),
+            in_specs=[whole, whole] + [pl.BlockSpec(memory_space=pl.ANY) for _ in waits],
+            out_specs=[
+                pl.BlockSpec((3, 2 * width, 128), lambda n, m: (0, 0, n)),
+                pl.BlockSpec((pair, 8, 128), lambda n, m: (n, 0, 0)),
+            ],
+        ),
+        out_shape=[
+            jax.ShapeDtypeStruct((3, 2 * width, slot_count * HD), f32),
+            jax.ShapeDtypeStruct((slot_count, 8, 128), f32),
+        ],
         compiler_params=pltpu.CompilerParams(vmem_limit_bytes=40 << 20),
         cost_estimate=pl.CostEstimate(
-            flops=0, bytes_accessed=groups * count * rows * width * 4, transcendentals=0
+            flops=0, bytes_accessed=frame_parts * rows * width * 8, transcendentals=0
         ),
         name="unpack_heads",
-    )(slots, *waits)
+    )(me, left, right, *waits)
 
 
 ROWS = 128
@@ -642,10 +673,6 @@
     )(core, hidden, grad, bias, bias, weights, weights, weights, weights)
 
 
-def after(value, *others):
-    return lax.optimization_barrier((value,) + others)[0]
-
-
 def on_device(
     tokens,
     noise_steps,
@@ -675,13 +702,12 @@
     unit_total = clip_count * local_frames
     units = unit_total // tensor_count
     sharers = tensor_count // clip_count
-    share_at = tensor_at % sharers
+    share_at = 0 if sharers == 1 else tensor_at % sharers
     own_rows = units * patch_count
     all_rows = frame_devices * own_rows
     slot = frame_at % shard_heads
     group_at = frame_at // shard_heads
     shard_groups = tensor_count // head_count
-    shard_base = (tensor_at // sharers) * sharers
     core = frame_at % 2
     chips = frame_devices // 2
     unit_shape = (units, patch_count, model_width)
@@ -718,12 +744,13 @@
         ]
 
     def rolled(values, start):
+        if isinstance(start, int):
+            start = start % tensor_count
+            return jnp.concatenate([values[start:], values[:start]])
         return lax.dynamic_slice_in_dim(
             jnp.concatenate([values, values]), start % tensor_count, tensor_count, axis=0
         )
 
-    def from_relative(parts, first=0):
-        return rolled(jnp.stack(parts), first - tensor_at - 1)
 
     def head_pairs(head, member):
         pairs = []
@@ -756,7 +783,8 @@
 
     def from_units(values):
         parts = values.reshape(units, tensor_count, local_patches, model_width)
-        return from_relative(exchange([parts[:, n] for n in range(tensor_count)])).reshape(
+        mine = jnp.stack(exchange([parts[:, n] for n in range(tensor_count)]))
+        return rolled(mine, -1 - tensor_at).reshape(
             clip_count, local_frames, local_patches, model_width
         )
 
@@ -772,6 +800,20 @@
             tiled=True,
         ).reshape(values.shape[1:])
 
+    bits = [1 << n for n in range(frame_devices.bit_length() - 1)]
+    bit_orders = (tuple(bits[1:] + bits[:1]), tuple(bits[:0:-1] + bits[:1]))
+
+    def doubled(values):
+        outs = []
+        width = values.shape[1] // 2
+        for n, order in enumerate(bit_orders):
+            part = values[:, n * width : (n + 1) * width]
+            for bit in order:
+                pairs = [(i, i ^ bit) for i in range(frame_devices)]
+                part = jnp.concatenate([part, lax.ppermute(part, "frame", pairs)])
+            outs.append(part.reshape(frame_devices, -1, width))
+        return outs
+
     def frame_parts(values):
         return (
             lax.all_gather(values, "frame", axis=0, tiled=True)
@@ -784,8 +826,11 @@
         "ud,dkj->ukj", act_noise, ada_weight, preferred_element_type=f32
     ) + ada_bias.astype(f32)
     modulation = (
-        from_relative(
-            exchange(to_relative(mod_local.reshape(tensor_count, units * 6, column_part)))
+        rolled(
+            jnp.stack(
+                exchange(to_relative(mod_local.reshape(tensor_count, units * 6, column_part)))
+            ),
+            -1 - tensor_at,
         )
         .reshape(tensor_count, units, 6, column_part)
         .transpose(1, 2, 0, 3)
@@ -820,14 +865,17 @@
     first_pack = jnp.concatenate([up_part[:half], down_part[:half], bias_part])
     second_pack = jnp.concatenate([up_part[half:], down_part[half:]])
     out_pack = own_part(out_weight)
-    slot_pack = after(slot_pack, unit_tokens)
+    slot_pack, unit_tokens = lax.optimization_barrier((slot_pack, unit_tokens))
     head_pack = jnp.stack([from_owners(slot_pack, head) for head in range(head_count)])
-    first_list = tensor_parts(after(jnp.concatenate([first_pack, out_pack]), head_pack))
-    out_at = first_pack.shape[0]
+    first_pack, head_pack = lax.optimization_barrier(
+        (jnp.concatenate([first_pack, out_pack]), head_pack)
+    )
+    first_list = tensor_parts(first_pack)
+    out_at = first_pack.shape[0] - out_rows
     first_parts = jnp.concatenate(
         [
-            from_relative([part[:out_at] for part in first_list]),
-            from_relative([part[out_at:] for part in first_list], shard_base),
+            jnp.stack([part[:out_at] for part in first_list]),
+            rolled(jnp.stack([part[out_at:] for part in first_list]), -1 - share_at),
         ],
         axis=1,
     ).reshape(-1, model_width)
@@ -914,18 +962,20 @@
     values_all = share(values)
     unit_ids = jnp.arange(frame_devices * units, dtype=jnp.int32)
     frame_ids = (
-        (unit_ids // units) * local_frames + share_at.astype(jnp.int32) * units + unit_ids % units
+        (unit_ids // units) * local_frames + share_at * units + unit_ids % units
     )
     values_t = values_all.T
     steps = all_rows // patch_count
-    second_list = tensor_parts(after(second_pack, queries))
+    second_pack, queries = lax.optimization_barrier((second_pack, queries))
+    second_list = tensor_parts(second_pack)
     cut = steps * 11 // 16
     heads_a, lse_a = attend(
         queries, keys_all, values_t, frame_ids, head_count, patch_count, 0, cut, ()
     )
     heads_a, *second_list = lax.optimization_barrier((heads_a, *second_list))
-    second_parts = from_relative(second_list)
-    upstream = to_units(after(cotangent, second_parts))
+    second_parts = jnp.concatenate(second_list)
+    cotangent, second_parts = lax.optimization_barrier((cotangent, second_parts))
+    upstream = to_units(cotangent)
     heads_b, lse_b = attend(
         queries, keys_all, values_t, frame_ids, head_count, patch_count, cut, steps,
         (second_parts,),
@@ -933,7 +983,7 @@
     attended_heads = jnp.concatenate([heads_a, heads_b])
     row_lse = jnp.concatenate([lse_a, lse_b])
     second_all = lax.all_gather(
-        second_parts.reshape(-1, model_width), "frame", axis=0, tiled=True
+        second_parts, "frame", axis=0, tiled=True
     ).reshape(frame_devices, tensor_count, -1, model_width)
     heads_here = swap_frame(attended_heads.reshape(frame_devices, own_rows, lanes))
 
@@ -977,7 +1027,7 @@
         .transpose(2, 0, 1, 3, 4, 5)
         .reshape(tensor_count, frame_devices, out_rows, model_width)
     )
-    grad_out = rolled(grad_out, -shard_base).transpose(1, 0, 2, 3)
+    grad_out = rolled(grad_out, share_at + 1).transpose(1, 0, 2, 3)
     width_part = model_width // frame_devices
 
     def by_core(keep_part, send_part):
@@ -1010,14 +1060,15 @@
     out_pairs = jnp.concatenate([grad_out, bias_row], axis=2).reshape(
         chips, 2, tensor_count, out_rows + 16, model_width
     )
+    got_out = core_swap(lax.dynamic_index_in_dim(out_pairs, 1 - core, 1, keepdims=False))
     late_half = add_pairs(
         keep_b,
         got_b,
         lax.dynamic_index_in_dim(out_pairs, core, 1, keepdims=False),
-        core_swap(lax.dynamic_index_in_dim(out_pairs, 1 - core, 1, keepdims=False)),
+        got_out,
     )
     late_sum = scatter(late_half)
-    first_list = exchange(to_relative(first_sum))
+    first_list = exchange([first_sum[n] for n in range(tensor_count)])
 
     keys_t = keys_all.T
     grad_q_a, *sums = attend_back(
@@ -1034,12 +1085,14 @@
     grad_k = unshare(grad_k_all)
     grad_v = unshare(grad_v_all)
     grad_projected = jnp.concatenate([grad_q, grad_k, grad_v], axis=1)
-    grad_hidden_part = dot(grad_projected, head_weight).astype(bf16)
+    grad_hidden_part, grad_projected = lax.optimization_barrier(
+        (dot(grad_projected, head_weight).astype(bf16), grad_projected)
+    )
     grad_hidden_one = lax.psum_scatter(grad_hidden_part, "frame", scatter_dimension=0, tiled=True)
     grad_hidden_one = grad_hidden_one.astype(f32).reshape(unit_shape)
 
-    late_total = tensor_sum(to_relative(late_sum)).astype(bf16)
-    grad_head_weight = dot_tn(after(grad_projected, grad_hidden_part), hidden_all).astype(bf16)
+    late_total = tensor_sum([late_sum[n] for n in range(tensor_count)]).astype(bf16)
+    grad_head_weight = dot_tn(grad_projected, hidden_all).astype(bf16)
     grad_slots = (
         grad_head_weight.reshape(3, head_count, HD, model_width)
         .transpose(1, 0, 2, 3)
@@ -1057,19 +1110,17 @@
 
     slots_total = to_owners([grad_slots[head] for head in range(head_count)])
 
+    slots_left, slots_right = doubled(slots_total)
+    grad_hidden_one, slots_left, slots_right = lax.optimization_barrier(
+        (grad_hidden_one, slots_left, slots_right)
+    )
     grad_scale_one = jnp.sum(grad_hidden_one * normed_one, axis=1)
     grad_shift_one = jnp.sum(grad_hidden_one, axis=1)
     grad_tokens = (
         grad_middle
         + norm_back(grad_hidden_one * (1.0 + scale_one), normed_one, inverse_one)
     ).astype(bf16)
-    tail_sums, slots_total, grad_tokens = lax.optimization_barrier(
-        (jnp.concatenate([first_total, late_total]), slots_total, grad_tokens)
-    )
-    tail_all = frame_parts(tail_sums)
-    slots_all = frame_parts(slots_total).reshape(
-        shard_groups, shard_heads, -1, model_width
-    )
+    tail_all = frame_parts(jnp.concatenate([first_total, late_total]))
     grad_tokens = from_units(grad_tokens)
     grad_modulation = jnp.stack(
         [
@@ -1114,12 +1165,12 @@
     final_up_bias = tail_bias[:, 2 * width_part : 2 * width_part + hidden_part].reshape(
         up_bias.shape
     )
-    final_qkv = unpack_heads(slots_all, (grad_ada_bias, final_up)).transpose(1, 0, 2)
+    final_qkv, bias_sums = unpack_heads(
+        frame_at.astype(jnp.int32).reshape(1), slots_left, slots_right, *bit_orders, shard_heads, ()
+    )
+    final_qkv = final_qkv.transpose(1, 0, 2)
     final_qv_bias = (
-        jnp.sum(slots_all[:, :, 3 * HD, : 2 * HD].astype(f32), axis=0)
-        .reshape(shard_heads, 2, HD)
-        .transpose(1, 0, 2)
-        .reshape(qv_bias.shape)
+        bias_sums[:, 0].reshape(shard_heads, 2, HD).transpose(1, 0, 2).reshape(qv_bias.shape)
     )
     return (
         result,

time: 597 us -> 586 us (0.982)
  the two profiles are of different devices: /device:TPU:0 before, /device:TPU:9 now
where the time goes in v4:
time: 586 us; the launch traced here: 575 us
  Pallas kernels  173 us (30%)
  waiting for transfers between devices  151 us (26%)
  local copies, waits for them, and re-layouts  75.5 us (13%)
  starting transfers between devices  70.8 us (12%)
  other arithmetic  43.4 us (7%)
  matrix products  32.8 us (6%)
  between operations  16.2 us (3%)
  blocking collectives  12 us (2%)
    ppermute x30, waiting for transfers between devices, shifted(): lax.ppermute(values, 'tensor', [(t, (t + shift) % tensor_count) for t in...  82.2 us
    pallas_call x2, Pallas kernels, attend_back(): pl.pallas_call(partial(attend_back_kernel, head_count=head_count, patch_c...  62.5 us
    ppermute x30, starting transfers between devices, shifted(): lax.ppermute(values, 'tensor', [(t, (t + shift) % tensor_count) for t in...  44.8 us
    pallas_call x2, Pallas kernels, attend(): pl.pallas_call(partial(attend_kernel, head_count=head_count, patch_count=...  42.6 us
    pallas_call x2, Pallas kernels, mlp(): pl.pallas_call(mlp_kernel, grid_spec=pltpu.PrefetchScalarGridSpec(num_sca...  41.7 us
    unnamed x179, local copies, waits for them, and re-layouts  34.9 us
    ppermute x6, waiting for transfers between devices, doubled(): part = jnp.concatenate([part, lax.ppermute(part, 'frame', pairs)])  21.4 us
    ppermute x2, waiting for transfers between devices, to_owners(): total = total + lax.ppermute(piece, ('frame', 'tensor'), pairs).astype(f32)  18.5 us
  transfers between devices with their start and end apart: 52, of which 19 were waited for; matrix products, arithmetic and copies ran while one was open for 20% of the time, Pallas kernels for 29%

profile of v4, /device:TPU:9, one launch (start us, length us, event | category | flops | bytes accessed | tf_op | source)
XLA Modules:
  0.0 574.9 jit_solution(9534708046912326372)
XLA Ops:
  22.3 11.9 %collective-permute-done.1 = bf16[2,64,1024]{2,1,0:T(8,128)(2,1)} collective-permute-done((bf16[2,64,1024]{2,1,0:T(8,128)(2,1)}, bf16[2,64,1024]{2,1,0:T(8,128)(2,1)}, u32[]{:S(2)}, u32[]{:S(2)}) %collective-permute-start.1) | collective-permute-done | bytes 262176 | tf_op jit(solution)/shard_map/ppermute | solution.py:721
  34.2 5.5 collective-permute-done.2
  48.3 15.0 %collective-permute-done.7 = bf16[208,1024]{1,0:T(8,128)(2,1)S(1)} collective-permute-done((bf16[208,1024]{1,0:T(8,128)(2,1)S(1)}, bf16[208,1024]{1,0:T(8,128)(2,1)S(1)}, u32[]{:S(2)}, u32[]{:S(2)}) %collective-permute-start.7) | collective-permute-done | bytes 426016 | tf_op jit(solution)/shard_map/ppermute | solution.py:766
  65.9 4.0 collective-permute-start.12
  70.0 6.1 %collective-permute-done.13 = bf16[176,1024]{1,0:T(8,128)(2,1)S(1)} collective-permute-done((bf16[176,1024]{1,0:T(8,128)(2,1)S(1)}, bf16[176,1024]{1,0:T(8,128)(2,1)S(1)}, u32[]{:S(2)}, u32[]{:S(2)}) %collective-permute-start.13) | collective-permute-done | bytes 360480 | tf_op jit(solution)/shard_map/ppermute | solution.py:721
  76.1 20.1 %collective-permute-done.12 = bf16[176,1024]{1,0:T(8,128)(2,1)S(1)} collective-permute-done((bf16[176,1024]{1,0:T(8,128)(2,1)S(1)}, bf16[176,1024]{1,0:T(8,128)(2,1)S(1)}, u32[]{:S(2)}, u32[]{:S(2)}) %collective-permute-start.12) | collective-permute-done | bytes 360480 | tf_op jit(solution)/shard_map/ppermute | solution.py:721
  96.2 4.1 collective-permute-done.11
  104.1 7.0 %add_convert_fusion = bf16[4096,384]{0,1:T(8,128)(2,1)S(1)} fusion(bf16[4096,1024]{1,0:T(8,128)(2,1)} %all-gather.5.cloned.1.call-done, bf16[384,1024]{1,0:T(8,128)(2,1)} %bitcast.294, f32[384]{0:T(512)S(1)} %pad_maximum_fusion.19), kind=kOutput, calls=%fused_computation.1 | convolution fusion | flops 3224371200 | bytes 12322304 | tf_op jit(solution)/shard_map/dot_general | solution.py:47
  119.1 22.2 %attend.2 = (bf16[2816,128]{1,0:T(8,128)(2,1)S(1)}, f32[11,1,512]{2,1,0:T(1,128)S(1)}) custom-call(s32[16]{0:T(128)S(1)} %fusion.53.frame_ids, bf16[4096,128]{1,0:T(8,128)(2,1)S(1)} %copy.98.q_ref, bf16[4096,128]{1,0:T(8,128)(2,1)S(1)} %copy.99.k_ref, bf16[128,4096]{1,0:T(8,128)(2,1)S(1)} %copy-done.43), custom_call_target="tpu_custom_call" | custom-call | flops 6576668672 | bytes 2883584 | tf_op jit(solution)/shard_map/attend/pallas_call | solution.py:141
  153.5 20.3 %attend.3 = (bf16[1280,128]{1,0:T(8,128)(2,1)S(1)}, f32[5,1,512]{2,1,0:T(1,128)S(1)}) custom-call(s32[16]{0:T(128)S(1)} %fusion.53.frame_ids, bf16[4096,128]{1,0:T(8,128)(2,1)S(1)} %copy-done.35, bf16[4096,128]{1,0:T(8,128)(2,1)S(1)} %copy-done.39, bf16[128,4096]{1,0:T(8,128)(2,1)S(1)} %copy-done.44, bf16[512,1024]{1,0:T(8,128)(2,1)S(1)} %copy-done.13), custom_call_target="tpu_custom_call" | custom-call | flops 4697620480 | bytes 1310720 | tf_op jit(solution)/shard_map/attend/pallas_call | solution.py:141
  174.9 7.6 %all-to-all-start = ((bf16[8,512,128]{2,1,0:T(8,128)(2,1)}), bf16[8,512,128]{2,1,0:T(8,128)(2,1)}, u32[]{:S(2)}, u32[]{:S(2)}) async-start(bf16[8,512,128]{2,1,0:T(8,128)(2,1)} %bitcast.265), calls=%async_computation | async-start | bytes 2097152 | tf_op jit(solution)/shard_map/all_to_all | solution.py:718
  193.5 10.5 %all-to-all-done.heads_ref = bf16[8,512,128]{2,1,0:T(8,128)(2,1)} async-done(((bf16[8,512,128]{2,1,0:T(8,128)(2,1)}), bf16[8,512,128]{2,1,0:T(8,128)(2,1)}, u32[]{:S(2)}, u32[]{:S(2)}) %all-to-all-start) | async-done | bytes 1048608 | tf_op jit(solution)/shard_map/all_to_all | solution.py:718
  204.1 4.2 project.1
  210.6 21.4 %mlp.2 = (f32[512,1024]{1,0:T(8,128)}, f32[512,1024]{1,0:T(8,128)}, bf16[4,4,128,1024]{3,2,1,0:T(8,128)(2,1)}, bf16[4,4,128,1024]{3,2,1,0:T(8,128)(2,1)}, f32[4,...) custom-call(s32[1]{0:T(128)} %bitcast.47.core_ref, bf16[512,1024]{1,0:T(8,128)(2,1)S(1)} %get-tuple-element.90.hidden_ref, ...), custom_call_target="tpu_custom_call" | custom-call | flops 12884901888 | bytes 16777216 | tf_op jit(solution)/shard_map/mlp/pallas_call | solution.py:640
  240.8 20.3 %mlp.3 = (f32[512,1024]{1,0:T(8,128)}, f32[512,1024]{1,0:T(8,128)}, bf16[4,4,128,1024]{3,2,1,0:T(8,128)(2,1)}, bf16[4,4,128,1024]{3,2,1,0:T(8,128)(2,1)}, f32[4,...) custom-call(s32[1]{0:T(128)} %bitcast.47.core_ref, bf16[512,1024]{1,0:T(8,128)(2,1)S(1)} %copy-done.31, ...), custom_call_target="tpu_custom_call" | custom-call | flops 12884901888 | bytes 16777216 | tf_op jit(solution)/shard_map/mlp/pallas_call | solution.py:640
  274.6 8.7 %middle_back.1 = (bf16[512,1024]{1,0:T(8,128)(2,1)S(1)}, f32[512,1024]{1,0:T(8,128)S(1)}, bf16[512,1024]{1,0:T(8,128)(2,1)S(1)}, bf16[8,512,128]{2,1,0:T(8,128)(2,1)}, f32[2,8,1024]{2,1,0:T(8,128)S(1)}) custom-call(bf16[512,1024]{1,0:T(8,128)(2,1)S(1)} %bitcast.253, f32[512,1024]{1,0:T(8,128)S(1)} %copy-done.25, f32[512,1024]{1,0:T(8,128)S(1)} %copy-done.26, ...), custom_call_target="tpu_custom_call" | custom-call | flops 1073741824 | bytes 20971520 | tf_op jit(solution)/shard_map/middle_back/pallas_call | solution.py:499
  311.1 4.9 all-to-all-start.1
  319.1 8.9 %collective-permute-done.19 = bf16[2,64,1024]{2,1,0:T(8,128)(2,1)S(1)} collective-permute-done((bf16[2,64,1024]{2,1,0:T(8,128)(2,1)}, bf16[2,64,1024]{2,1,0:T(8,128)(2,1)S(1)}, u32[]{:S(2)}, u32[]{:S(2)}) %collective-permute-start.19) | collective-permute-done | bytes 262176 | tf_op jit(solution)/shard_map/ppermute | solution.py:721
  328.1 5.5 collective-permute-done.20
  343.9 31.8 %attend_back.2 = (bf16[2816,128]{1,0:T(8,128)(2,1)S(1)}, f32[4096,128]{1,0:T(8,128)}, f32[4096,128]{1,0:T(8,128)}) custom-call(s32[16]{0:T(128)S(1)} %fusion.53.frame_ids, bf16[4096,128]{1,0:T(8,128)(2,1)S(1)} %copy-done.36, bf16[4096,128]{1,0:T(8,128)(2,1)} %bitcast.70.grad_ref, bf16[4096,128]{1,0:T(8,128)(2,1)S(1)} %copy-done.19, ...), custom_call_target="tpu_custom_call" | custom-call | flops 16441671680 | bytes 5767168 | tf_op jit(solution)/shard_map/attend_back/pallas_call | solution.py:254
  378.0 30.7 %attend_back.3 = (bf16[1280,128]{1,0:T(8,128)(2,1)S(1)}, bf16[4096,128]{1,0:T(8,128)(2,1)S(1)}, bf16[4096,128]{1,0:T(8,128)(2,1)S(1)}) custom-call(s32[16]{0:T(128)S(1)} %fusion.53.frame_ids, bf16[4096,128]{1,0:T(8,128)(2,1)S(1)} %copy-done.37, bf16[4096,128]{1,0:T(8,128)(2,1)} %bitcast.70.grad_ref, bf16[4096,128]{1,0:T(8,128)(2,1)S(1)} %copy-done.19, ...), custom_call_target="tpu_custom_call" | custom-call | flops 11744051200 | bytes 2621440 | tf_op jit(solution)/shard_map/attend_back/pallas_call | solution.py:254
  408.7 5.2 pad_maximum_fusion.1
  413.9 8.6 %convolution_convert_fusion = bf16[4096,1024]{1,0:T(8,128)(2,1)} fusion(bf16[384,1024]{1,0:T(8,128)(2,1)S(1)} %bitcast.295, bf16[4096,128]{1,0:T(8,128)(2,1)S(1)} %get-tuple-element.127, bf16[4096,128]{1,0:T(8,128)(2,1)S(1)} %get-tuple-element.126, bf16[1280,128]{1,0:T(8,128)(2,1)S(1)} %get-tuple-element.125, bf16[2816,128]{1,0:T(8,128)(2,1)S(1)} %get-tuple-element.115), kind=kOutput, calls=%fused_computation | convolution fusion | flops 3238002688 | bytes 12320768 | tf_op jit(solution)/shard_map/dot_general | solution.py:43
  430.7 10.8 %convolution_convert_fusion.2 = bf16[384,1024]{1,0:T(8,128)(2,1)} fusion(bf16[4096,384]{1,0:T(8,128)(2,1)} %pad_maximum_fusion.1, bf16[4096,1024]{1,0:T(8,128)(2,1)} %all-gather.5.cloned.1.call-done), kind=kOutput, calls=%fused_computation.41 | convolution fusion | flops 3221618688 | bytes 12320768 | tf_op jit(solution)/shard_map/dot_general | solution.py:51
  443.9 12.2 %collective-permute-done.41 = bf16[176,1024]{1,0:T(8,128)(2,1)} collective-permute-done((bf16[176,1024]{1,0:T(8,128)(2,1)}, bf16[176,1024]{1,0:T(8,128)(2,1)}, u32[]{:S(2)}, u32[]{:S(2)}) %collective-permute-start.41) | collective-permute-done | bytes 360480 | tf_op jit(solution)/shard_map/ppermute | solution.py:721
  462.5 18.5 %collective-permute-done.27 = bf16[208,1024]{1,0:T(8,128)(2,1)S(1)} collective-permute-done((bf16[208,1024]{1,0:T(8,128)(2,1)S(1)}, bf16[208,1024]{1,0:T(8,128)(2,1)S(1)}, u32[]{:S(2)}, u32[]{:S(2)}) %collective-permute-start.27) | collective-permute-done | bytes 426016 | tf_op jit(solution)/shard_map/ppermute | solution.py:775
  482.9 9.5 %collective-permute-done.31 = bf16[208,512]{1,0:T(8,128)(2,1)S(1)} collective-permute-done((bf16[208,512]{1,0:T(8,128)(2,1)S(1)}, bf16[208,512]{1,0:T(8,128)(2,1)S(1)}, u32[]{:S(2)}, u32[]{:S(2)}) %collective-permute-start.31) | collective-permute-done | bytes 213024 | tf_op jit(solution)/shard_map/ppermute | solution.py:813
  494.1 10.2 %collective-permute-done.32 = bf16[416,512]{1,0:T(8,128)(2,1)S(1)} collective-permute-done((bf16[416,512]{1,0:T(8,128)(2,1)S(1)}, bf16[416,512]{1,0:T(8,128)(2,1)S(1)}, u32[]{:S(2)}, u32[]{:S(2)}) %collective-permute-start.32) | collective-permute-done | bytes 426016 | tf_op jit(solution)/shard_map/ppermute | solution.py:813
  532.7 12.0 %all_gather.18 = f32[64,1664]{1,0:T(8,128)S(1)} all-gather(f32[8,1664]{1,0:T(8,128)S(1)} %reshape.332), channel_id=1, replica_groups=mesh['frame'=8,'tensor'=4] {'frame'}, dimensions={0}, use_global_device_ids=true | all-gather | bytes 479232 | tf_op jit(solution)/shard_map/all_gather | solution.py:1152
  545.5 4.6 fusion.31
  550.7 4.6 collective-permute-done.34
  562.8 4.8 unpack.1
  (434 shorter events, 187.1 us)
Async XLA Ops:
  7.2 96.9 %all-gather.5.cloned.1.call-start = ((), (), s32[]{:S(2)}) async-start(), calls=%async_computation.5 | async-start | bytes 9437184 | tf_op jit(solution)/shard_map/all_gather | solution.py:896
  17.7 22.0 %collective-permute-start.2 = (bf16[2,64,1024]{2,1,0:T(8,128)(2,1)S(1)}, bf16[2,64,1024]{2,1,0:T(8,128)(2,1)S(1)}, u32[]{:S(2)}, u32[]{:S(2)}) collective-permute-start(bf16[2,64,1024]{2,1,0:T(8,128)(2,1)S(1)} %get-tuple-element.177), channel_id=1, source_target_pairs={{0,1},{1,2},{2,3},{3,0},{4,5},{5,6},{6,7},{7,4},{8,9},{9,10},{10,1... | collective-permute-start | bytes 786440 | tf_op jit(solution)/shard_map/ppermute | solution.py:721
  43.0 142.5 %all-gather.7.cloned.1.call-start = ((), (), s32[]{:S(2)}) async-start(), calls=%async_computation.6 | async-start | bytes 12976128 | tf_op jit(solution)/shard_map/all_gather | solution.py:900
  45.1 18.1 %collective-permute-start.7 = (bf16[208,1024]{1,0:T(8,128)(2,1)S(1)}, bf16[208,1024]{1,0:T(8,128)(2,1)S(1)}, u32[]{:S(2)}, u32[]{:S(2)}) collective-permute-start(bf16[208,1024]{1,0:T(8,128)(2,1)S(1)} %fusion.30), channel_id=1, source_target_pairs={{2,0},{3,1},{0,2},{1,3},{6,4},{7,5},{4,6},{5,7},{10,8},{11,9},{8,1... | collective-permute-start | bytes 1277960 | tf_op jit(solution)/shard_map/ppermute | solution.py:766
  45.1 18.1 %collective-permute-start.6 = (bf16[208,1024]{1,0:T(8,128)(2,1)S(1)}, bf16[208,1024]{1,0:T(8,128)(2,1)S(1)}, u32[]{:S(2)}, u32[]{:S(2)}) collective-permute-start(bf16[208,1024]{1,0:T(8,128)(2,1)S(1)} %fusion.30), channel_id=1, source_target_pairs={{0,0},{1,1},{2,2},{3,3},{4,4},{5,5},{6,6},{7,7},{8,8},{9,9},{10,10... | collective-permute-start | bytes 1277960 | tf_op jit(solution)/shard_map/ppermute | solution.py:766
  65.9 30.3 %collective-permute-start.12 = (bf16[176,1024]{1,0:T(8,128)(2,1)S(1)}, bf16[176,1024]{1,0:T(8,128)(2,1)S(1)}, u32[]{:S(2)}, u32[]{:S(2)}) collective-permute-start(bf16[176,1024]{1,0:T(8,128)(2,1)S(1)} %fusion.35), channel_id=1, source_target_pairs={{0,2},{1,3},{2,0},{3,1},{4,6},{5,7},{6,4},{7,5},{8,10},{9,11},{10,... | collective-permute-start | bytes 1081352 | tf_op jit(solution)/shard_map/ppermute | solution.py:721
  69.9 30.4 %collective-permute-start.11 = (bf16[176,1024]{1,0:T(8,128)(2,1)S(1)}, bf16[176,1024]{1,0:T(8,128)(2,1)S(1)}, u32[]{:S(2)}, u32[]{:S(2)}) collective-permute-start(bf16[176,1024]{1,0:T(8,128)(2,1)S(1)} %fusion.35), channel_id=1, source_target_pairs={{0,3},{1,0},{2,1},{3,2},{4,7},{5,4},{6,5},{7,6},{8,11},{9,8},{10,9... | collective-permute-start | bytes 1081352 | tf_op jit(solution)/shard_map/ppermute | solution.py:721
  101.7 136.7 %all-gather.9.cloned.1.call-start = ((), (), s32[]{:S(2)}) async-start(), calls=%async_computation.7 | async-start | bytes 9437184 | tf_op jit(solution)/shard_map/all_gather | solution.py:985
  113.3 28.9 %collective-permute-start.10 = (bf16[128,1024]{1,0:T(8,128)(2,1)S(1)}, bf16[128,1024]{1,0:T(8,128)(2,1)}, u32[]{:S(2)}, u32[]{:S(2)}) collective-permute-start(bf16[128,1024]{1,0:T(8,128)(2,1)S(1)} %pad_maximum_fusion.13), channel_id=1, source_target_pairs={{0,1},{1,2},{2,3},{3,0},{4,5},{5,6},{6,7},{7,4},{8,9},{9,10},{10,1... | collective-permute-start | bytes 786440 | tf_op jit(solution)/shard_map/ppermute | solution.py:721
  113.3 28.9 %collective-permute-start.9 = (bf16[128,1024]{1,0:T(8,128)(2,1)S(1)}, bf16[128,1024]{1,0:T(8,128)(2,1)}, u32[]{:S(2)}, u32[]{:S(2)}) collective-permute-start(bf16[128,1024]{1,0:T(8,128)(2,1)S(1)} %pad_maximum_fusion.13), channel_id=1, source_target_pairs={{0,2},{1,3},{2,0},{3,1},{4,6},{5,7},{6,4},{7,5},{8,10},{9,11},{10,... | collective-permute-start | bytes 786440 | tf_op jit(solution)/shard_map/ppermute | solution.py:721
  113.3 28.9 %collective-permute-start.8 = (bf16[128,1024]{1,0:T(8,128)(2,1)S(1)}, bf16[128,1024]{1,0:T(8,128)(2,1)}, u32[]{:S(2)}, u32[]{:S(2)}) collective-permute-start(bf16[128,1024]{1,0:T(8,128)(2,1)S(1)} %pad_maximum_fusion.13), channel_id=1, source_target_pairs={{0,3},{1,0},{2,1},{3,2},{4,7},{5,4},{6,5},{7,6},{8,11},{9,8},{10,9... | collective-permute-start | bytes 786440 | tf_op jit(solution)/shard_map/ppermute | solution.py:721
  146.7 36.1 %collective-permute-start.14 = (bf16[2,64,1024]{2,1,0:T(8,128)(2,1)}, bf16[2,64,1024]{2,1,0:T(8,128)(2,1)}, u32[]{:S(2)}, u32[]{:S(2)}) collective-permute-start(bf16[2,64,1024]{2,1,0:T(8,128)(2,1)} %get-tuple-element.170), channel_id=1, source_target_pairs={{0,3},{1,0},{2,1},{3,2},{4,7},{5,4},{6,5},{7,6},{8,11},{9,8},{10,9... | collective-permute-start | bytes 786440 | tf_op jit(solution)/shard_map/ppermute | solution.py:721
  148.8 34.0 %collective-permute-start.16 = (bf16[2,64,1024]{2,1,0:T(8,128)(2,1)}, bf16[2,64,1024]{2,1,0:T(8,128)(2,1)}, u32[]{:S(2)}, u32[]{:S(2)}) collective-permute-start(bf16[2,64,1024]{2,1,0:T(8,128)(2,1)} %get-tuple-element.172), channel_id=1, source_target_pairs={{0,1},{1,2},{2,3},{3,0},{4,5},{5,6},{6,7},{7,4},{8,9},{9,10},{10,1... | collective-permute-start | bytes 786440 | tf_op jit(solution)/shard_map/ppermute | solution.py:721
  148.8 34.0 %collective-permute-start.15 = (bf16[2,64,1024]{2,1,0:T(8,128)(2,1)}, bf16[2,64,1024]{2,1,0:T(8,128)(2,1)}, u32[]{:S(2)}, u32[]{:S(2)}) collective-permute-start(bf16[2,64,1024]{2,1,0:T(8,128)(2,1)} %get-tuple-element.173), channel_id=1, source_target_pairs={{0,2},{1,3},{2,0},{3,1},{4,6},{5,7},{6,4},{7,5},{8,10},{9,11},{10,... | collective-permute-start | bytes 786440 | tf_op jit(solution)/shard_map/ppermute | solution.py:721
  174.9 29.1 %all-to-all-start = ((bf16[8,512,128]{2,1,0:T(8,128)(2,1)}), bf16[8,512,128]{2,1,0:T(8,128)(2,1)}, u32[]{:S(2)}, u32[]{:S(2)}) async-start(bf16[8,512,128]{2,1,0:T(8,128)(2,1)} %bitcast.265), calls=%async_computation | async-start | bytes 2097152 | tf_op jit(solution)/shard_map/all_to_all | solution.py:718
  182.5 153.3 %reduce-scatter.4.cloned.1.call-start = ((), (), s32[]{:S(2)}) async-start(), calls=%async_computation.8 | async-start | bytes 5242880 | tf_op jit(solution)/shard_map/reduce_scatter | solution.py:795
  233.5 27.6 %collective-permute-start.17 = (bf16[4,4,128,1024]{3,2,1,0:T(8,128)(2,1)}, bf16[4,4,128,1024]{3,2,1,0:T(8,128)(2,1)}, u32[]{:S(2)}, u32[]{:S(2)}) collective-permute-start(bf16[4,4,128,1024]{3,2,1,0:T(8,128)(2,1)} %get-tuple-element.93), channel_id=1, source_target_pairs={{0,4},{4,0},{8,12},{12,8},{16,20},{20,16},{24,28},{28,24},{1,5},{5... | collective-permute-start | bytes 12582920 | tf_op jit(solution)/shard_map/ppermute | solution.py:792
  266.7 157.3 %reduce-scatter.8.cloned.1.call-start = ((), (), s32[]{:S(2)}) async-start(), calls=%async_computation.10 | async-start | bytes 7208960 | tf_op jit(solution)/shard_map/reduce_scatter | solution.py:795
  267.2 27.4 %collective-permute-start.21 = (bf16[4,4,128,1024]{3,2,1,0:T(8,128)(2,1)}, bf16[4,4,128,1024]{3,2,1,0:T(8,128)(2,1)}, u32[]{:S(2)}, u32[]{:S(2)}) collective-permute-start(bf16[4,4,128,1024]{3,2,1,0:T(8,128)(2,1)} %get-tuple-element.107), channel_id=1, source_target_pairs={{0,4},{4,0},{8,12},{12,8},{16,20},{20,16},{24,28},{28,24},{1,5},{5... | collective-permute-start | bytes 12582920 | tf_op jit(solution)/shard_map/ppermute | solution.py:792
  307.6 20.5 %collective-permute-start.19 = (bf16[2,64,1024]{2,1,0:T(8,128)(2,1)}, bf16[2,64,1024]{2,1,0:T(8,128)(2,1)S(1)}, u32[]{:S(2)}, u32[]{:S(2)}) collective-permute-start(bf16[2,64,1024]{2,1,0:T(8,128)(2,1)} %get-tuple-element.168), channel_id=1, source_target_pairs={{0,2},{1,3},{2,0},{3,1},{4,6},{5,7},{6,4},{7,5},{8,10},{9,11},{10,... | collective-permute-start | bytes 786440 | tf_op jit(solution)/shard_map/ppermute | solution.py:721
  311.1 30.3 %all-to-all-start.1 = ((bf16[8,512,128]{2,1,0:T(8,128)(2,1)}), bf16[8,512,128]{2,1,0:T(8,128)(2,1)}, u32[]{:S(2)}, u32[]{:S(2)}) async-start(bf16[8,512,128]{2,1,0:T(8,128)(2,1)} %get-tuple-element.103), calls=%async_computation.1 | async-start | bytes 2097152 | tf_op jit(solution)/shard_map/all_to_all | solution.py:718
  316.0 197.5 %reduce-scatter.6.cloned.1.call-start = ((), (), s32[]{:S(2)}) async-start(), calls=%async_computation.9 | async-start | bytes 9437184 | tf_op jit(solution)/shard_map/reduce_scatter | solution.py:1091
  337.9 37.8 %collective-permute-start.25 = (bf16[128,1024]{1,0:T(8,128)(2,1)}, bf16[128,1024]{1,0:T(8,128)(2,1)}, u32[]{:S(2)}, u32[]{:S(2)}) collective-permute-start(bf16[128,1024]{1,0:T(8,128)(2,1)} %get-tuple-element.164), channel_id=1, source_target_pairs={{0,1},{1,2},{2,3},{3,0},{4,5},{5,6},{6,7},{7,4},{8,9},{9,10},{10,1... | collective-permute-start | bytes 786440 | tf_op jit(solution)/shard_map/ppermute | solution.py:721
  340.1 35.6 %collective-permute-start.24 = (bf16[128,1024]{1,0:T(8,128)(2,1)}, bf16[128,1024]{1,0:T(8,128)(2,1)}, u32[]{:S(2)}, u32[]{:S(2)}) collective-permute-start(bf16[128,1024]{1,0:T(8,128)(2,1)} %get-tuple-element.165), channel_id=1, source_target_pairs={{0,2},{1,3},{2,0},{3,1},{4,6},{5,7},{6,4},{7,5},{8,10},{9,11},{10,... | collective-permute-start | bytes 786440 | tf_op jit(solution)/shard_map/ppermute | solution.py:721
  340.1 35.6 %collective-permute-start.23 = (bf16[128,1024]{1,0:T(8,128)(2,1)}, bf16[128,1024]{1,0:T(8,128)(2,1)}, u32[]{:S(2)}, u32[]{:S(2)}) collective-permute-start(bf16[128,1024]{1,0:T(8,128)(2,1)} %get-tuple-element.166), channel_id=1, source_target_pairs={{0,3},{1,0},{2,1},{3,2},{4,7},{5,4},{6,5},{7,6},{8,11},{9,8},{10,9... | collective-permute-start | bytes 786440 | tf_op jit(solution)/shard_map/ppermute | solution.py:721
  422.5 135.0 %all-gather.11.cloned.1.call-start = ((), (), s32[]{:S(2)}) async-start(), calls=%async_computation.11 | async-start | bytes 5603328 | tf_op jit(solution)/shard_map/all_gather | solution.py:819
  426.2 17.6 %collective-permute-start.40 = (bf16[176,1024]{1,0:T(8,128)(2,1)}, bf16[176,1024]{1,0:T(8,128)(2,1)}, u32[]{:S(2)}, u32[]{:S(2)}) collective-permute-start(bf16[176,1024]{1,0:T(8,128)(2,1)} %get-tuple-element.157), channel_id=1, source_target_pairs={{0,1},{1,2},{2,3},{3,0},{4,5},{5,6},{6,7},{7,4},{8,9},{9,10},{10,1... | collective-permute-start | bytes 1081352 | tf_op jit(solution)/shard_map/ppermute | solution.py:721
  428.7 27.5 %collective-permute-start.41 = (bf16[176,1024]{1,0:T(8,128)(2,1)}, bf16[176,1024]{1,0:T(8,128)(2,1)}, u32[]{:S(2)}, u32[]{:S(2)}) collective-permute-start(bf16[176,1024]{1,0:T(8,128)(2,1)} %get-tuple-element.159), channel_id=1, source_target_pairs={{0,2},{1,3},{2,0},{3,1},{4,6},{5,7},{6,4},{7,5},{8,10},{9,11},{10,... | collective-permute-start | bytes 1081352 | tf_op jit(solution)/shard_map/ppermute | solution.py:721
  459.4 21.5 %collective-permute-start.27 = (bf16[208,1024]{1,0:T(8,128)(2,1)S(1)}, bf16[208,1024]{1,0:T(8,128)(2,1)S(1)}, u32[]{:S(2)}, u32[]{:S(2)}) collective-permute-start(bf16[208,1024]{1,0:T(8,128)(2,1)S(1)} %get-tuple-element.179), channel_id=1, source_target_pairs={{0,2},{1,3},{2,0},{3,1},{4,6},{5,7},{6,4},{7,5},{8,10},{9,11},{10,... | collective-permute-start | bytes 1277960 | tf_op jit(solution)/shard_map/ppermute | solution.py:775
  530.0 25.3 %collective-permute-start.36 = (bf16[2,64,1024]{2,1,0:T(8,128)(2,1)S(1)}, bf16[2,64,1024]{2,1,0:T(8,128)(2,1)S(1)}, u32[]{:S(2)}, u32[]{:S(2)}) collective-permute-start(bf16[2,64,1024]{2,1,0:T(8,128)(2,1)S(1)} %get-tuple-element.160), channel_id=1, source_target_pairs={{0,1},{1,2},{2,3},{3,0},{4,5},{5,6},{6,7},{7,4},{8,9},{9,10},{10,1... | collective-permute-start | bytes 786440 | tf_op jit(solution)/shard_map/ppermute | solution.py:721
  530.2 25.0 %collective-permute-start.35 = (bf16[2,64,1024]{2,1,0:T(8,128)(2,1)}, bf16[2,64,1024]{2,1,0:T(8,128)(2,1)S(1)}, u32[]{:S(2)}, u32[]{:S(2)}) collective-permute-start(bf16[2,64,1024]{2,1,0:T(8,128)(2,1)} %get-tuple-element.161), channel_id=1, source_target_pairs={{0,2},{1,3},{2,0},{3,1},{4,6},{5,7},{6,4},{7,5},{8,10},{9,11},{10,... | collective-permute-start | bytes 786440 | tf_op jit(solution)/shard_map/ppermute | solution.py:721
  531.6 23.7 %collective-permute-start.34 = (bf16[2,64,1024]{2,1,0:T(8,128)(2,1)}, bf16[2,64,1024]{2,1,0:T(8,128)(2,1)S(1)}, u32[]{:S(2)}, u32[]{:S(2)}) collective-permute-start(bf16[2,64,1024]{2,1,0:T(8,128)(2,1)} %get-tuple-element.162), channel_id=1, source_target_pairs={{0,3},{1,0},{2,1},{3,2},{4,7},{5,4},{6,5},{7,6},{8,11},{9,8},{10,9... | collective-permute-start | bytes 786440 | tf_op jit(solution)/shard_map/ppermute | solution.py:721
  (96 other events, 808.2 us)
Sparse Core Ops, SparseCore 0:
  43.2 55.6 all-gather.4
  101.8 68.7 all-gather.6
  173.0 65.3 all-gather.8
  266.8 59.5 reduce-scatter.3
  330.1 74.0 reduce-scatter.7
  422.7 75.6 reduce-scatter.5
  500.8 41.6 all-gather.10

commit v5 on v4

--- a/solution.py
+++ b/solution.py
@@ -51,7 +51,7 @@
     return lax.dot_general(left, right, (((0,), (0,)), ((), ())), preferred_element_type=f32)
 
 
-GROUP = 4
+GROUP = 8
 
 
 def head_blocks(transposed, head_count):

time: 586 us -> 580 us (0.990)
  the two profiles are of different devices: /device:TPU:9 before, /device:TPU:0 now
where the time goes in v5:
time: 580 us; the launch traced here: 569 us
  Pallas kernels  170 us (29%)
  waiting for transfers between devices  153 us (26%)
  local copies, waits for them, and re-layouts  76.7 us (13%)
  starting transfers between devices  66.7 us (12%)
  other arithmetic  43.6 us (8%)
  matrix products  32.6 us (6%)
  between operations  16.2 us (3%)
  blocking collectives  10 us (2%)
    ppermute x30, waiting for transfers between devices, shifted(): lax.ppermute(values, 'tensor', [(t, (t + shift) % tensor_count) for t in...  75.3 us
    pallas_call x2, Pallas kernels, attend_back(): pl.pallas_call(partial(attend_back_kernel, head_count=head_count, patch_c...  61.3 us
    ppermute x30, starting transfers between devices, shifted(): lax.ppermute(values, 'tensor', [(t, (t + shift) % tensor_count) for t in...  49.1 us
    pallas_call x2, Pallas kernels, mlp(): pl.pallas_call(mlp_kernel, grid_spec=pltpu.PrefetchScalarGridSpec(num_sca...  41.6 us
    pallas_call x2, Pallas kernels, attend(): pl.pallas_call(partial(attend_kernel, head_count=head_count, patch_count=...  40.8 us
    unnamed x179, local copies, waits for them, and re-layouts  35.7 us
    ppermute x6, waiting for transfers between devices, doubled(): part = jnp.concatenate([part, lax.ppermute(part, 'frame', pairs)])  20.5 us
    ppermute x2, waiting for transfers between devices, to_owners(): total = total + lax.ppermute(piece, ('frame', 'tensor'), pairs).astype(f32)  18.8 us
  transfers between devices with their start and end apart: 52, of which 17 were waited for; matrix products, arithmetic and copies ran while one was open for 20% of the time, Pallas kernels for 28%

profile of v5, /device:TPU:0, one launch (start us, length us, event | category | flops | bytes accessed | tf_op | source)
XLA Modules:
  0.0 569.5 jit_solution(11369639414260313381)
XLA Ops:
  22.2 4.9 collective-permute-done
  27.1 16.3 %collective-permute-done.1 = bf16[2,64,1024]{2,1,0:T(8,128)(2,1)} collective-permute-done((bf16[2,64,1024]{2,1,0:T(8,128)(2,1)}, bf16[2,64,1024]{2,1,0:T(8,128)(2,1)}, u32[]{:S(2)}, u32[]{:S(2)}) %collective-permute-start.1) | collective-permute-done | bytes 262176 | tf_op jit(solution)/shard_map/ppermute | solution.py:721
  53.1 15.9 %collective-permute-done.7 = bf16[208,1024]{1,0:T(8,128)(2,1)S(1)} collective-permute-done((bf16[208,1024]{1,0:T(8,128)(2,1)S(1)}, bf16[208,1024]{1,0:T(8,128)(2,1)S(1)}, u32[]{:S(2)}, u32[]{:S(2)}) %collective-permute-start.7) | collective-permute-done | bytes 426016 | tf_op jit(solution)/shard_map/ppermute | solution.py:766
  73.0 9.3 %collective-permute-done.13 = bf16[176,1024]{1,0:T(8,128)(2,1)S(1)} collective-permute-done((bf16[176,1024]{1,0:T(8,128)(2,1)S(1)}, bf16[176,1024]{1,0:T(8,128)(2,1)S(1)}, u32[]{:S(2)}, u32[]{:S(2)}) %collective-permute-start.13) | collective-permute-done | bytes 360480 | tf_op jit(solution)/shard_map/ppermute | solution.py:721
  82.3 14.4 %collective-permute-done.12 = bf16[176,1024]{1,0:T(8,128)(2,1)S(1)} collective-permute-done((bf16[176,1024]{1,0:T(8,128)(2,1)S(1)}, bf16[176,1024]{1,0:T(8,128)(2,1)S(1)}, u32[]{:S(2)}, u32[]{:S(2)}) %collective-permute-start.12) | collective-permute-done | bytes 360480 | tf_op jit(solution)/shard_map/ppermute | solution.py:721
  100.4 7.0 %add_convert_fusion = bf16[4096,384]{0,1:T(8,128)(2,1)S(1)} fusion(bf16[4096,1024]{1,0:T(8,128)(2,1)} %all-gather.5.cloned.1.call-done, bf16[384,1024]{1,0:T(8,128)(2,1)} %bitcast.294, f32[384]{0:T(512)S(1)} %pad_maximum_fusion.19), kind=kOutput, calls=%fused_computation.1 | convolution fusion | flops 3224371200 | bytes 12322304 | tf_op jit(solution)/shard_map/dot_general | solution.py:47
  109.7 7.3 %collective-permute-start.10 = (bf16[128,1024]{1,0:T(8,128)(2,1)S(1)}, bf16[128,1024]{1,0:T(8,128)(2,1)}, u32[]{:S(2)}, u32[]{:S(2)}) collective-permute-start(bf16[128,1024]{1,0:T(8,128)(2,1)S(1)} %pad_maximum_fusion.13), channel_id=1, source_target_pairs={{0,1},{1,2},{2,3},{3,0},{4,5},{5,6},{6,7},{7,4},{8,9},{9,10},{10,1... | collective-permute-start | bytes 786440 | tf_op jit(solution)/shard_map/ppermute | solution.py:721
  123.9 21.6 %attend.2 = (bf16[2816,128]{1,0:T(8,128)(2,1)S(1)}, f32[11,1,512]{2,1,0:T(1,128)S(1)}) custom-call(s32[16]{0:T(128)S(1)} %fusion.53.frame_ids, bf16[4096,128]{1,0:T(8,128)(2,1)S(1)} %copy.98.q_ref, bf16[4096,128]{1,0:T(8,128)(2,1)S(1)} %copy.99.k_ref, bf16[128,4096]{1,0:T(8,128)(2,1)S(1)} %copy-done.43), custom_call_target="tpu_custom_call" | custom-call | flops 6576668672 | bytes 2883584 | tf_op jit(solution)/shard_map/attend/pallas_call | solution.py:141
  154.8 19.2 %attend.3 = (bf16[1280,128]{1,0:T(8,128)(2,1)S(1)}, f32[5,1,512]{2,1,0:T(1,128)S(1)}) custom-call(s32[16]{0:T(128)S(1)} %fusion.53.frame_ids, bf16[4096,128]{1,0:T(8,128)(2,1)S(1)} %copy-done.35, bf16[4096,128]{1,0:T(8,128)(2,1)S(1)} %copy-done.39, bf16[128,4096]{1,0:T(8,128)(2,1)S(1)} %copy-done.44, bf16[512,1024]{1,0:T(8,128)(2,1)S(1)} %copy-done.13), custom_call_target="tpu_custom_call" | custom-call | flops 4697620480 | bytes 1310720 | tf_op jit(solution)/shard_map/attend/pallas_call | solution.py:141
  175.0 4.5 all-to-all-start
  182.8 3.5 slice.257
  191.0 13.6 %all-to-all-done.heads_ref = bf16[8,512,128]{2,1,0:T(8,128)(2,1)} async-done(((bf16[8,512,128]{2,1,0:T(8,128)(2,1)}), bf16[8,512,128]{2,1,0:T(8,128)(2,1)}, u32[]{:S(2)}, u32[]{:S(2)}) %all-to-all-start) | async-done | bytes 1048608 | tf_op jit(solution)/shard_map/all_to_all | solution.py:718
  204.7 4.2 project.1
  211.2 21.3 %mlp.2 = (f32[512,1024]{1,0:T(8,128)}, f32[512,1024]{1,0:T(8,128)}, bf16[4,4,128,1024]{3,2,1,0:T(8,128)(2,1)}, bf16[4,4,128,1024]{3,2,1,0:T(8,128)(2,1)}, f32[4,...) custom-call(s32[1]{0:T(128)} %bitcast.47.core_ref, bf16[512,1024]{1,0:T(8,128)(2,1)S(1)} %get-tuple-element.90.hidden_ref, ...), custom_call_target="tpu_custom_call" | custom-call | flops 12884901888 | bytes 16777216 | tf_op jit(solution)/shard_map/mlp/pallas_call | solution.py:640
  236.1 5.9 %all-gather.9.cloned.1.call-done = bf16[4096,1024]{1,0:T(8,128)(2,1)} async-done(((bf16[512,1024]{1,0:T(8,128)(2,1)}), bf16[4096,1024]{1,0:T(8,128)(2,1)}) %all-gather.9.cloned.1.call-update) | async-done | bytes 8388624 | tf_op jit(solution)/shard_map/all_gather | solution.py:985
  244.4 20.3 %mlp.3 = (f32[512,1024]{1,0:T(8,128)}, f32[512,1024]{1,0:T(8,128)}, bf16[4,4,128,1024]{3,2,1,0:T(8,128)(2,1)}, bf16[4,4,128,1024]{3,2,1,0:T(8,128)(2,1)}, f32[4,...) custom-call(s32[1]{0:T(128)} %bitcast.47.core_ref, bf16[512,1024]{1,0:T(8,128)(2,1)S(1)} %copy-done.31, ...), custom_call_target="tpu_custom_call" | custom-call | flops 12884901888 | bytes 16777216 | tf_op jit(solution)/shard_map/mlp/pallas_call | solution.py:640
  278.7 8.7 %middle_back.1 = (bf16[512,1024]{1,0:T(8,128)(2,1)S(1)}, f32[512,1024]{1,0:T(8,128)S(1)}, bf16[512,1024]{1,0:T(8,128)(2,1)S(1)}, bf16[8,512,128]{2,1,0:T(8,128)(2,1)}, f32[2,8,1024]{2,1,0:T(8,128)S(1)}) custom-call(bf16[512,1024]{1,0:T(8,128)(2,1)S(1)} %bitcast.253, f32[512,1024]{1,0:T(8,128)S(1)} %copy-done.25, f32[512,1024]{1,0:T(8,128)S(1)} %copy-done.26, ...), custom_call_target="tpu_custom_call" | custom-call | flops 1073741824 | bytes 20971520 | tf_op jit(solution)/shard_map/middle_back/pallas_call | solution.py:499
  310.7 4.4 all-to-all-start.1
  317.3 15.0 %collective-permute-done.19 = bf16[2,64,1024]{2,1,0:T(8,128)(2,1)S(1)} collective-permute-done((bf16[2,64,1024]{2,1,0:T(8,128)(2,1)}, bf16[2,64,1024]{2,1,0:T(8,128)(2,1)S(1)}, u32[]{:S(2)}, u32[]{:S(2)}) %collective-permute-start.19) | collective-permute-done | bytes 262176 | tf_op jit(solution)/shard_map/ppermute | solution.py:721
  345.7 31.2 %attend_back.2 = (bf16[2816,128]{1,0:T(8,128)(2,1)S(1)}, f32[4096,128]{1,0:T(8,128)}, f32[4096,128]{1,0:T(8,128)}) custom-call(s32[16]{0:T(128)S(1)} %fusion.53.frame_ids, bf16[4096,128]{1,0:T(8,128)(2,1)S(1)} %copy-done.36, bf16[4096,128]{1,0:T(8,128)(2,1)} %bitcast.70.grad_ref, bf16[4096,128]{1,0:T(8,128)(2,1)S(1)} %copy-done.19, ...), custom_call_target="tpu_custom_call" | custom-call | flops 16441671680 | bytes 5767168 | tf_op jit(solution)/shard_map/attend_back/pallas_call | solution.py:254
  379.2 30.1 %attend_back.3 = (bf16[1280,128]{1,0:T(8,128)(2,1)S(1)}, bf16[4096,128]{1,0:T(8,128)(2,1)S(1)}, bf16[4096,128]{1,0:T(8,128)(2,1)S(1)}) custom-call(s32[16]{0:T(128)S(1)} %fusion.53.frame_ids, bf16[4096,128]{1,0:T(8,128)(2,1)S(1)} %copy-done.37, bf16[4096,128]{1,0:T(8,128)(2,1)} %bitcast.70.grad_ref, bf16[4096,128]{1,0:T(8,128)(2,1)S(1)} %copy-done.19, ...), custom_call_target="tpu_custom_call" | custom-call | flops 11744051200 | bytes 2621440 | tf_op jit(solution)/shard_map/attend_back/pallas_call | solution.py:254
  409.4 5.4 pad_maximum_fusion.1
  414.8 8.6 %convolution_convert_fusion = bf16[4096,1024]{1,0:T(8,128)(2,1)} fusion(bf16[384,1024]{1,0:T(8,128)(2,1)S(1)} %bitcast.295, bf16[4096,128]{1,0:T(8,128)(2,1)S(1)} %get-tuple-element.127, bf16[4096,128]{1,0:T(8,128)(2,1)S(1)} %get-tuple-element.126, bf16[1280,128]{1,0:T(8,128)(2,1)S(1)} %get-tuple-element.125, bf16[2816,128]{1,0:T(8,128)(2,1)S(1)} %get-tuple-element.115), kind=kOutput, calls=%fused_computation | convolution fusion | flops 3238002688 | bytes 12320768 | tf_op jit(solution)/shard_map/dot_general | solution.py:43
  427.2 3.8 collective-permute-start.42
  431.0 10.6 %convolution_convert_fusion.2 = bf16[384,1024]{1,0:T(8,128)(2,1)} fusion(bf16[4096,384]{1,0:T(8,128)(2,1)} %pad_maximum_fusion.1, bf16[4096,1024]{1,0:T(8,128)(2,1)} %all-gather.5.cloned.1.call-done), kind=kOutput, calls=%fused_computation.41 | convolution fusion | flops 3221618688 | bytes 12320768 | tf_op jit(solution)/shard_map/dot_general | solution.py:51
  446.4 12.9 %collective-permute-done.41 = bf16[176,1024]{1,0:T(8,128)(2,1)} collective-permute-done((bf16[176,1024]{1,0:T(8,128)(2,1)}, bf16[176,1024]{1,0:T(8,128)(2,1)}, u32[]{:S(2)}, u32[]{:S(2)}) %collective-permute-start.41) | collective-permute-done | bytes 360480 | tf_op jit(solution)/shard_map/ppermute | solution.py:721
  462.8 18.8 %collective-permute-done.27 = bf16[208,1024]{1,0:T(8,128)(2,1)S(1)} collective-permute-done((bf16[208,1024]{1,0:T(8,128)(2,1)S(1)}, bf16[208,1024]{1,0:T(8,128)(2,1)S(1)}, u32[]{:S(2)}, u32[]{:S(2)}) %collective-permute-start.27) | collective-permute-done | bytes 426016 | tf_op jit(solution)/shard_map/ppermute | solution.py:775
  483.8 10.3 %collective-permute-done.31 = bf16[208,512]{1,0:T(8,128)(2,1)S(1)} collective-permute-done((bf16[208,512]{1,0:T(8,128)(2,1)S(1)}, bf16[208,512]{1,0:T(8,128)(2,1)S(1)}, u32[]{:S(2)}, u32[]{:S(2)}) %collective-permute-start.31) | collective-permute-done | bytes 213024 | tf_op jit(solution)/shard_map/ppermute | solution.py:813
  496.2 9.0 %collective-permute-done.32 = bf16[416,512]{1,0:T(8,128)(2,1)S(1)} collective-permute-done((bf16[416,512]{1,0:T(8,128)(2,1)S(1)}, bf16[416,512]{1,0:T(8,128)(2,1)S(1)}, u32[]{:S(2)}, u32[]{:S(2)}) %collective-permute-start.32) | collective-permute-done | bytes 426016 | tf_op jit(solution)/shard_map/ppermute | solution.py:813
  533.8 10.0 %all_gather.18 = f32[64,1664]{1,0:T(8,128)S(1)} all-gather(f32[8,1664]{1,0:T(8,128)S(1)} %reshape.332), channel_id=1, replica_groups=mesh['frame'=8,'tensor'=4] {'frame'}, dimensions={0}, use_global_device_ids=true | all-gather | bytes 479232 | tf_op jit(solution)/shard_map/all_gather | solution.py:1152
  544.6 4.6 fusion.31
  557.4 4.8 unpack.1
  (434 shorter events, 175.9 us)
Async XLA Ops:
  7.2 93.2 %all-gather.5.cloned.1.call-start = ((), (), s32[]{:S(2)}) async-start(), calls=%async_computation.5 | async-start | bytes 9437184 | tf_op jit(solution)/shard_map/all_gather | solution.py:896
  19.3 24.0 %collective-permute-start.1 = (bf16[2,64,1024]{2,1,0:T(8,128)(2,1)}, bf16[2,64,1024]{2,1,0:T(8,128)(2,1)}, u32[]{:S(2)}, u32[]{:S(2)}) collective-permute-start(bf16[2,64,1024]{2,1,0:T(8,128)(2,1)} %get-tuple-element.175), channel_id=1, source_target_pairs={{0,2},{1,3},{2,0},{3,1},{4,6},{5,7},{6,4},{7,5},{8,10},{9,11},{10,... | collective-permute-start | bytes 786440 | tf_op jit(solution)/shard_map/ppermute | solution.py:721
  21.8 21.6 %collective-permute-start.2 = (bf16[2,64,1024]{2,1,0:T(8,128)(2,1)S(1)}, bf16[2,64,1024]{2,1,0:T(8,128)(2,1)S(1)}, u32[]{:S(2)}, u32[]{:S(2)}) collective-permute-start(bf16[2,64,1024]{2,1,0:T(8,128)(2,1)S(1)} %get-tuple-element.177), channel_id=1, source_target_pairs={{0,1},{1,2},{2,3},{3,0},{4,5},{5,6},{6,7},{7,4},{8,9},{9,10},{10,1... | collective-permute-start | bytes 786440 | tf_op jit(solution)/shard_map/ppermute | solution.py:721
  46.7 136.1 %all-gather.7.cloned.1.call-start = ((), (), s32[]{:S(2)}) async-start(), calls=%async_computation.6 | async-start | bytes 12976128 | tf_op jit(solution)/shard_map/all_gather | solution.py:900
  48.7 20.2 %collective-permute-start.7 = (bf16[208,1024]{1,0:T(8,128)(2,1)S(1)}, bf16[208,1024]{1,0:T(8,128)(2,1)S(1)}, u32[]{:S(2)}, u32[]{:S(2)}) collective-permute-start(bf16[208,1024]{1,0:T(8,128)(2,1)S(1)} %fusion.30), channel_id=1, source_target_pairs={{2,0},{3,1},{0,2},{1,3},{6,4},{7,5},{4,6},{5,7},{10,8},{11,9},{8,1... | collective-permute-start | bytes 1277960 | tf_op jit(solution)/shard_map/ppermute | solution.py:766
  49.8 19.1 %collective-permute-start.6 = (bf16[208,1024]{1,0:T(8,128)(2,1)S(1)}, bf16[208,1024]{1,0:T(8,128)(2,1)S(1)}, u32[]{:S(2)}, u32[]{:S(2)}) collective-permute-start(bf16[208,1024]{1,0:T(8,128)(2,1)S(1)} %fusion.30), channel_id=1, source_target_pairs={{0,0},{1,1},{2,2},{3,3},{4,4},{5,5},{6,6},{7,7},{8,8},{9,9},{10,10... | collective-permute-start | bytes 1277960 | tf_op jit(solution)/shard_map/ppermute | solution.py:766
  69.1 27.6 %collective-permute-start.12 = (bf16[176,1024]{1,0:T(8,128)(2,1)S(1)}, bf16[176,1024]{1,0:T(8,128)(2,1)S(1)}, u32[]{:S(2)}, u32[]{:S(2)}) collective-permute-start(bf16[176,1024]{1,0:T(8,128)(2,1)S(1)} %fusion.35), channel_id=1, source_target_pairs={{0,2},{1,3},{2,0},{3,1},{4,6},{5,7},{6,4},{7,5},{8,10},{9,11},{10,... | collective-permute-start | bytes 1081352 | tf_op jit(solution)/shard_map/ppermute | solution.py:721
  70.1 26.6 %collective-permute-start.11 = (bf16[176,1024]{1,0:T(8,128)(2,1)S(1)}, bf16[176,1024]{1,0:T(8,128)(2,1)S(1)}, u32[]{:S(2)}, u32[]{:S(2)}) collective-permute-start(bf16[176,1024]{1,0:T(8,128)(2,1)S(1)} %fusion.35), channel_id=1, source_target_pairs={{0,3},{1,0},{2,1},{3,2},{4,7},{5,4},{6,5},{7,6},{8,11},{9,8},{10,9... | collective-permute-start | bytes 1081352 | tf_op jit(solution)/shard_map/ppermute | solution.py:721
  98.0 143.9 %all-gather.9.cloned.1.call-start = ((), (), s32[]{:S(2)}) async-start(), calls=%async_computation.7 | async-start | bytes 9437184 | tf_op jit(solution)/shard_map/all_gather | solution.py:985
  109.7 36.6 %collective-permute-start.10 = (bf16[128,1024]{1,0:T(8,128)(2,1)S(1)}, bf16[128,1024]{1,0:T(8,128)(2,1)}, u32[]{:S(2)}, u32[]{:S(2)}) collective-permute-start(bf16[128,1024]{1,0:T(8,128)(2,1)S(1)} %pad_maximum_fusion.13), channel_id=1, source_target_pairs={{0,1},{1,2},{2,3},{3,0},{4,5},{5,6},{6,7},{7,4},{8,9},{9,10},{10,1... | collective-permute-start | bytes 786440 | tf_op jit(solution)/shard_map/ppermute | solution.py:721
  117.0 29.3 %collective-permute-start.9 = (bf16[128,1024]{1,0:T(8,128)(2,1)S(1)}, bf16[128,1024]{1,0:T(8,128)(2,1)}, u32[]{:S(2)}, u32[]{:S(2)}) collective-permute-start(bf16[128,1024]{1,0:T(8,128)(2,1)S(1)} %pad_maximum_fusion.13), channel_id=1, source_target_pairs={{0,2},{1,3},{2,0},{3,1},{4,6},{5,7},{6,4},{7,5},{8,10},{9,11},{10,... | collective-permute-start | bytes 786440 | tf_op jit(solution)/shard_map/ppermute | solution.py:721
  117.0 29.3 %collective-permute-start.8 = (bf16[128,1024]{1,0:T(8,128)(2,1)S(1)}, bf16[128,1024]{1,0:T(8,128)(2,1)}, u32[]{:S(2)}, u32[]{:S(2)}) collective-permute-start(bf16[128,1024]{1,0:T(8,128)(2,1)S(1)} %pad_maximum_fusion.13), channel_id=1, source_target_pairs={{0,3},{1,0},{2,1},{3,2},{4,7},{5,4},{6,5},{7,6},{8,11},{9,8},{10,9... | collective-permute-start | bytes 786440 | tf_op jit(solution)/shard_map/ppermute | solution.py:721
  150.8 29.1 %collective-permute-start.14 = (bf16[2,64,1024]{2,1,0:T(8,128)(2,1)}, bf16[2,64,1024]{2,1,0:T(8,128)(2,1)}, u32[]{:S(2)}, u32[]{:S(2)}) collective-permute-start(bf16[2,64,1024]{2,1,0:T(8,128)(2,1)} %get-tuple-element.170), channel_id=1, source_target_pairs={{0,3},{1,0},{2,1},{3,2},{4,7},{5,4},{6,5},{7,6},{8,11},{9,8},{10,9... | collective-permute-start | bytes 786440 | tf_op jit(solution)/shard_map/ppermute | solution.py:721
  152.8 27.1 %collective-permute-start.16 = (bf16[2,64,1024]{2,1,0:T(8,128)(2,1)}, bf16[2,64,1024]{2,1,0:T(8,128)(2,1)}, u32[]{:S(2)}, u32[]{:S(2)}) collective-permute-start(bf16[2,64,1024]{2,1,0:T(8,128)(2,1)} %get-tuple-element.172), channel_id=1, source_target_pairs={{0,1},{1,2},{2,3},{3,0},{4,5},{5,6},{6,7},{7,4},{8,9},{9,10},{10,1... | collective-permute-start | bytes 786440 | tf_op jit(solution)/shard_map/ppermute | solution.py:721
  152.8 27.1 %collective-permute-start.15 = (bf16[2,64,1024]{2,1,0:T(8,128)(2,1)}, bf16[2,64,1024]{2,1,0:T(8,128)(2,1)}, u32[]{:S(2)}, u32[]{:S(2)}) collective-permute-start(bf16[2,64,1024]{2,1,0:T(8,128)(2,1)} %get-tuple-element.173), channel_id=1, source_target_pairs={{0,2},{1,3},{2,0},{3,1},{4,6},{5,7},{6,4},{7,5},{8,10},{9,11},{10,... | collective-permute-start | bytes 786440 | tf_op jit(solution)/shard_map/ppermute | solution.py:721
  175.0 29.6 %all-to-all-start = ((bf16[8,512,128]{2,1,0:T(8,128)(2,1)}), bf16[8,512,128]{2,1,0:T(8,128)(2,1)}, u32[]{:S(2)}, u32[]{:S(2)}) async-start(bf16[8,512,128]{2,1,0:T(8,128)(2,1)} %bitcast.265), calls=%async_computation | async-start | bytes 2097152 | tf_op jit(solution)/shard_map/all_to_all | solution.py:718
  179.5 155.1 %reduce-scatter.4.cloned.1.call-start = ((), (), s32[]{:S(2)}) async-start(), calls=%async_computation.8 | async-start | bytes 5242880 | tf_op jit(solution)/shard_map/reduce_scatter | solution.py:795
  234.1 30.7 %collective-permute-start.17 = (bf16[4,4,128,1024]{3,2,1,0:T(8,128)(2,1)}, bf16[4,4,128,1024]{3,2,1,0:T(8,128)(2,1)}, u32[]{:S(2)}, u32[]{:S(2)}) collective-permute-start(bf16[4,4,128,1024]{3,2,1,0:T(8,128)(2,1)} %get-tuple-element.93), channel_id=1, source_target_pairs={{0,4},{4,0},{8,12},{12,8},{16,20},{20,16},{24,28},{28,24},{1,5},{5... | collective-permute-start | bytes 12582920 | tf_op jit(solution)/shard_map/ppermute | solution.py:792
  270.3 154.7 %reduce-scatter.8.cloned.1.call-start = ((), (), s32[]{:S(2)}) async-start(), calls=%async_computation.10 | async-start | bytes 7208960 | tf_op jit(solution)/shard_map/reduce_scatter | solution.py:795
  270.8 27.9 %collective-permute-start.21 = (bf16[4,4,128,1024]{3,2,1,0:T(8,128)(2,1)}, bf16[4,4,128,1024]{3,2,1,0:T(8,128)(2,1)}, u32[]{:S(2)}, u32[]{:S(2)}) collective-permute-start(bf16[4,4,128,1024]{3,2,1,0:T(8,128)(2,1)} %get-tuple-element.107), channel_id=1, source_target_pairs={{0,4},{4,0},{8,12},{12,8},{16,20},{20,16},{24,28},{28,24},{1,5},{5... | collective-permute-start | bytes 12582920 | tf_op jit(solution)/shard_map/ppermute | solution.py:792
  310.6 21.7 %collective-permute-start.19 = (bf16[2,64,1024]{2,1,0:T(8,128)(2,1)}, bf16[2,64,1024]{2,1,0:T(8,128)(2,1)S(1)}, u32[]{:S(2)}, u32[]{:S(2)}) collective-permute-start(bf16[2,64,1024]{2,1,0:T(8,128)(2,1)} %get-tuple-element.168), channel_id=1, source_target_pairs={{0,2},{1,3},{2,0},{3,1},{4,6},{5,7},{6,4},{7,5},{8,10},{9,11},{10,... | collective-permute-start | bytes 786440 | tf_op jit(solution)/shard_map/ppermute | solution.py:721
  310.7 32.6 %all-to-all-start.1 = ((bf16[8,512,128]{2,1,0:T(8,128)(2,1)}), bf16[8,512,128]{2,1,0:T(8,128)(2,1)}, u32[]{:S(2)}, u32[]{:S(2)}) async-start(bf16[8,512,128]{2,1,0:T(8,128)(2,1)} %get-tuple-element.103), calls=%async_computation.1 | async-start | bytes 2097152 | tf_op jit(solution)/shard_map/all_to_all | solution.py:718
  315.1 197.8 %reduce-scatter.6.cloned.1.call-start = ((), (), s32[]{:S(2)}) async-start(), calls=%async_computation.9 | async-start | bytes 9437184 | tf_op jit(solution)/shard_map/reduce_scatter | solution.py:1091
  336.7 40.2 %collective-permute-start.25 = (bf16[128,1024]{1,0:T(8,128)(2,1)}, bf16[128,1024]{1,0:T(8,128)(2,1)}, u32[]{:S(2)}, u32[]{:S(2)}) collective-permute-start(bf16[128,1024]{1,0:T(8,128)(2,1)} %get-tuple-element.164), channel_id=1, source_target_pairs={{0,1},{1,2},{2,3},{3,0},{4,5},{5,6},{6,7},{7,4},{8,9},{9,10},{10,1... | collective-permute-start | bytes 786440 | tf_op jit(solution)/shard_map/ppermute | solution.py:721
  338.2 38.7 %collective-permute-start.24 = (bf16[128,1024]{1,0:T(8,128)(2,1)}, bf16[128,1024]{1,0:T(8,128)(2,1)}, u32[]{:S(2)}, u32[]{:S(2)}) collective-permute-start(bf16[128,1024]{1,0:T(8,128)(2,1)} %get-tuple-element.165), channel_id=1, source_target_pairs={{0,2},{1,3},{2,0},{3,1},{4,6},{5,7},{6,4},{7,5},{8,10},{9,11},{10,... | collective-permute-start | bytes 786440 | tf_op jit(solution)/shard_map/ppermute | solution.py:721
  340.2 36.7 %collective-permute-start.23 = (bf16[128,1024]{1,0:T(8,128)(2,1)}, bf16[128,1024]{1,0:T(8,128)(2,1)}, u32[]{:S(2)}, u32[]{:S(2)}) collective-permute-start(bf16[128,1024]{1,0:T(8,128)(2,1)} %get-tuple-element.166), channel_id=1, source_target_pairs={{0,3},{1,0},{2,1},{3,2},{4,7},{5,4},{6,5},{7,6},{8,11},{9,8},{10,9... | collective-permute-start | bytes 786440 | tf_op jit(solution)/shard_map/ppermute | solution.py:721
  423.4 128.6 %all-gather.11.cloned.1.call-start = ((), (), s32[]{:S(2)}) async-start(), calls=%async_computation.11 | async-start | bytes 5603328 | tf_op jit(solution)/shard_map/all_gather | solution.py:819
  427.2 19.2 %collective-permute-start.42 = (bf16[176,1024]{1,0:T(8,128)(2,1)}, bf16[176,1024]{1,0:T(8,128)(2,1)}, u32[]{:S(2)}, u32[]{:S(2)}) collective-permute-start(bf16[176,1024]{1,0:T(8,128)(2,1)} %get-tuple-element.158), channel_id=1, source_target_pairs={{0,3},{1,0},{2,1},{3,2},{4,7},{5,4},{6,5},{7,6},{8,11},{9,8},{10,9... | collective-permute-start | bytes 1081352 | tf_op jit(solution)/shard_map/ppermute | solution.py:721
  431.0 28.3 %collective-permute-start.41 = (bf16[176,1024]{1,0:T(8,128)(2,1)}, bf16[176,1024]{1,0:T(8,128)(2,1)}, u32[]{:S(2)}, u32[]{:S(2)}) collective-permute-start(bf16[176,1024]{1,0:T(8,128)(2,1)} %get-tuple-element.159), channel_id=1, source_target_pairs={{0,2},{1,3},{2,0},{3,1},{4,6},{5,7},{6,4},{7,5},{8,10},{9,11},{10,... | collective-permute-start | bytes 1081352 | tf_op jit(solution)/shard_map/ppermute | solution.py:721
  462.5 19.1 %collective-permute-start.27 = (bf16[208,1024]{1,0:T(8,128)(2,1)S(1)}, bf16[208,1024]{1,0:T(8,128)(2,1)S(1)}, u32[]{:S(2)}, u32[]{:S(2)}) collective-permute-start(bf16[208,1024]{1,0:T(8,128)(2,1)S(1)} %get-tuple-element.179), channel_id=1, source_target_pairs={{0,2},{1,3},{2,0},{3,1},{4,6},{5,7},{6,4},{7,5},{8,10},{9,11},{10,... | collective-permute-start | bytes 1277960 | tf_op jit(solution)/shard_map/ppermute | solution.py:775
  528.3 21.5 %collective-permute-start.36 = (bf16[2,64,1024]{2,1,0:T(8,128)(2,1)S(1)}, bf16[2,64,1024]{2,1,0:T(8,128)(2,1)S(1)}, u32[]{:S(2)}, u32[]{:S(2)}) collective-permute-start(bf16[2,64,1024]{2,1,0:T(8,128)(2,1)S(1)} %get-tuple-element.160), channel_id=1, source_target_pairs={{0,1},{1,2},{2,3},{3,0},{4,5},{5,6},{6,7},{7,4},{8,9},{9,10},{10,1... | collective-permute-start | bytes 786440 | tf_op jit(solution)/shard_map/ppermute | solution.py:721
  531.4 18.4 %collective-permute-start.35 = (bf16[2,64,1024]{2,1,0:T(8,128)(2,1)}, bf16[2,64,1024]{2,1,0:T(8,128)(2,1)S(1)}, u32[]{:S(2)}, u32[]{:S(2)}) collective-permute-start(bf16[2,64,1024]{2,1,0:T(8,128)(2,1)} %get-tuple-element.161), channel_id=1, source_target_pairs={{0,2},{1,3},{2,0},{3,1},{4,6},{5,7},{6,4},{7,5},{8,10},{9,11},{10,... | collective-permute-start | bytes 786440 | tf_op jit(solution)/shard_map/ppermute | solution.py:721
  (96 other events, 808.5 us)
Sparse Core Ops, SparseCore 0:
  46.8 53.1 all-gather.4
  102.5 69.1 all-gather.6
  174.2 67.7 all-gather.8
  270.4 54.2 reduce-scatter.3
  328.4 73.4 reduce-scatter.7
  423.6 73.1 reduce-scatter.5
  499.2 41.9 all-gather.10
